TPU v7x, 512 devices: a whole 4x4x16 slice. The times are simulated.
512 devices in a mesh: seq: 32 (over z, y_lo), head: 16 (over y_hi, x, core).
Axes of the slice: x: 4, y: 4 (y_hi: 2, y_lo: 2; y = y_hi * 2 + y_lo), z: 16, core: 2. Of those that a mesh axis runs over, the one named last changes fastest.
Arguments:
- byte_states: bfloat16 [24576, 1280], P('seq', 'head'), may hold values from -19 to 19
- patch_ids: int32 [24576], P('seq'), may hold values from 0 to 3071, never falling along the last dimension, each value on 1 to 16 neighbouring positions
- slot_patch: int32 [3072], replicated, may hold values from 0 to 3071, each once
- pool_gain: float32 [1280], replicated, may hold values from 0.25 to 1.75
- w_in: bfloat16 [1280, 4096], P('seq', 'head'), may hold values from -0.16910264 to 0.16910264
- attn_gain: float32 [4096], replicated, may hold values from 0.25 to 1.75
- w_qkv: bfloat16 [4096, 3, 4096], P('seq', None, 'head'), may hold values from -0.5105401 to 0.5105401
- w_out: bfloat16 [4096, 4096], P('head'), may hold values from -0.09375 to 0.09375
- w_down: bfloat16 [4096, 1280], P('head', 'seq'), may hold values from -0.34375 to 0.34375
Outputs:
- patch_out: bfloat16 [3072, 4096], P('seq', 'head')
- byte_out: bfloat16 [24576, 1280], P('seq', 'head')
Inputs may be any that keep to these rules, and one draw needn't show every extreme that they name: patch_ids never falls along the bytes; each of the 3072 patches holds 1 to 16 consecutive bytes, and some patch exactly 16. `slot_patch`: every patch number appears once; slot r belongs to segment r // 96.
All inputs are finite; a program needn't handle non-finite values.
Results may differ from a plain program's by a relative error of at most 0.015.
Values may be sent and summed in bfloat16 or wider, within the bound.
No kernel may reach another device: no remote copies, remote signals or barrier semaphores. Data moves between devices by JAX's collectives and lax.ppermute only.
A program may use at most 64 MiB of HBM per device.

v0:
```python
import math

import jax
import jax.numpy as jnp
from jax import lax
from jax.sharding import Mesh
from jax.sharding import PartitionSpec as P

HEAD_SIZE = 128
WINDOW = 8
SEQ = ("seq_0", "seq_1")


EPSILON = 1e-05
FLOOR_SCORE = -1e30


def cut_along(x, dim, size):
    lengths = x.shape
    pieces = x.reshape(*lengths[:dim], size, lengths[dim] // size, *lengths[dim + 1 :])
    return jnp.moveaxis(pieces, dim, 0)


def sum_at_owner(x, axis, dim):
    pieces = cut_along(x, dim, lax.axis_size(axis))
    arrived = lax.all_to_all(pieces, axis, split_axis=0, concat_axis=0, tiled=True)
    return arrived.sum(axis=0)


def in_order(pieces, dim):
    pieces = jnp.moveaxis(pieces, 0, dim)
    lengths = pieces.shape
    return pieces.reshape(*lengths[:dim], lengths[dim] * lengths[dim + 1], *lengths[dim + 2 :])


def sent_to_all(x, axis):
    size = lax.axis_size(axis)
    return lax.all_to_all(jnp.broadcast_to(x[None], (size, *x.shape)), axis, 0, 0, tiled=True)


def gathered_copies(x, axis, dim):
    return in_order(sent_to_all(x, axis), dim)


def whole_of(x, axes, dim):
    if not axes:
        return x
    nearer = lax.all_gather(x, axes[-1], axis=dim, tiled=True)
    return whole_of(nearer, axes[:-1], dim)


def side_by_side(arrays, axis, dim, along):
    widths = [a.shape[along] for a in arrays]
    both = jnp.concatenate(arrays, axis=along)
    out = lax.all_gather(both, axis, axis=dim, tiled=True)
    return tuple(jnp.split(out, [sum(widths[:k]) for k in range(1, len(widths))], axis=along))


def rms_scale(values, gain):
    wide = values.astype(jnp.float32)
    return wide * lax.rsqrt(jnp.mean(wide * wide, axis=-1, keepdims=True) + EPSILON) * gain


def over_blocks(carry, keys, labels, update):
    count = labels.shape[0]
    size = math.gcd(count, 512)
    turns = count // size
    key_blocks = jax.tree.map(lambda whole: whole.reshape((turns, size) + whole.shape[1:]), keys)
    label_blocks = labels.reshape(turns, size)

    def advance(state, paired):
        return (update(state, paired[0], paired[1]), None)

    carry, unused = lax.scan(advance, carry, (key_blocks, label_blocks))
    return carry


def softmax_step(carry, scores, allowed, values, equation):
    peak, total, mixed = carry
    scores = jnp.where(allowed, scores, FLOOR_SCORE)
    new_peak = jnp.maximum(peak, jnp.max(scores, axis=-1))
    weights = jnp.where(allowed, jnp.exp(scores - new_peak[..., None]), 0.0)
    rescale = jnp.exp(peak - new_peak)
    total = total * rescale + jnp.sum(weights, axis=-1)
    mixed = mixed * rescale[..., None] + jnp.einsum(
        equation, weights.astype(jnp.bfloat16), values, preferred_element_type=jnp.float32
    )
    return (new_peak, total, mixed)


def body(byte_states, patch_ids, slot_patch, pool_gain, w_in, attn_gain, w_qkv, w_out, w_down):
    rows_each = slot_patch.shape[0] // lax.axis_size(SEQ)
    bytes_here = byte_states.shape[0]
    cross_size = byte_states.shape[1]
    match = (slot_patch[:, None] == patch_ids[None, :]).astype(jnp.bfloat16)
    pooled = sum_at_owner(
        jnp.dot(match, byte_states, preferred_element_type=jnp.float32), SEQ, 0
    ).astype(jnp.bfloat16)
    pooled_full = gathered_copies(pooled, "head", 1)
    normed = rms_scale(pooled_full, pool_gain).astype(jnp.bfloat16)
    columns = normed
    embed = jnp.dot(
        columns, gathered_copies(w_in, SEQ, 0), preferred_element_type=jnp.float32
    ).astype(jnp.bfloat16)
    embed_full = gathered_copies(embed, "head", 1)
    attn_in = rms_scale(embed_full, attn_gain).astype(jnp.bfloat16)
    heads_here = w_qkv.shape[2] // HEAD_SIZE
    piece = whole_of(w_qkv, SEQ, 0)
    columns = attn_in
    projected = jnp.dot(
        columns, piece.reshape(piece.shape[0], -1), preferred_element_type=jnp.float32
    ).astype(jnp.bfloat16)
    projected = projected.reshape(rows_each, 3, heads_here, HEAD_SIZE)
    queries = projected[:, 0].transpose(1, 0, 2)
    keys_here = projected[:, 1]
    values_here = projected[:, 2]
    own_labels = lax.dynamic_slice_in_dim(slot_patch, lax.axis_index(SEQ) * rows_each, rows_each)
    head_scale = 1.0 / math.sqrt(HEAD_SIZE)

    def attend_keys(carry, pieces):

        def update(state, block, block_labels):
            key_block, value_block = block
            scores = (
                jnp.einsum("hqd,khd->hqk", queries, key_block, preferred_element_type=jnp.float32)
                * head_scale
            )
            allowed = block_labels[None, None, :] <= own_labels[None, :, None]
            return softmax_step(state, scores, allowed, value_block, "hqk,khd->hqd")

        return over_blocks(carry, pieces, slot_patch, update)

    attn_init = (
        jnp.full((heads_here, rows_each), FLOOR_SCORE, jnp.float32),
        jnp.zeros((heads_here, rows_each), jnp.float32),
        jnp.zeros((heads_here, rows_each, HEAD_SIZE), jnp.float32),
    )
    peak, total, mixed = attend_keys(attn_init, side_by_side((keys_here, values_here), SEQ, 0, 1))
    attended = (
        (mixed / total[..., None])
        .astype(jnp.bfloat16)
        .transpose(1, 0, 2)
        .reshape(rows_each, heads_here * HEAD_SIZE)
    )
    partial_out = jnp.dot(attended, w_out, preferred_element_type=jnp.float32)
    added = sum_at_owner(partial_out, "head", 1)
    stream = (embed.astype(jnp.float32) + added).astype(jnp.bfloat16)
    down_part = jnp.dot(stream, gathered_copies(w_down, SEQ, 1), preferred_element_type=jnp.float32)
    patch_states = sum_at_owner(down_part, "head", 1).astype(jnp.bfloat16)
    cross_scale = 1.0 / math.sqrt(cross_size)
    lowest = patch_ids[0] - (WINDOW - 1)
    capacity = bytes_here + WINDOW
    wanted = lowest + jnp.arange(capacity, dtype=jnp.int32)

    def pick_rows(carry, piece):

        def update(state, block, block_labels):
            match = (wanted[:, None] == block_labels[None, :]).astype(jnp.bfloat16)
            return state + jnp.dot(match, block, preferred_element_type=jnp.float32)

        return over_blocks(carry, piece, slot_patch, update)

    pick_init = jnp.zeros((capacity, cross_size), jnp.float32)
    picked = pick_rows(pick_init, gathered_copies(patch_states, SEQ, 0)).astype(jnp.bfloat16)
    reach = patch_ids[:, None] - jnp.arange(WINDOW, dtype=jnp.int32)[None, :]
    valid = reach >= 0
    window_keys = picked[reach - lowest]
    scores = (
        jnp.einsum("bc,bwc->bw", byte_states, window_keys, preferred_element_type=jnp.float32)
        * cross_scale
    )
    scores = jnp.where(valid, scores, FLOOR_SCORE)
    cross_peak = jnp.max(scores, axis=-1, keepdims=True)
    weights = jnp.where(valid, jnp.exp(scores - cross_peak), 0.0)
    cross_total = jnp.sum(weights, axis=-1, keepdims=True)
    reached = (
        jnp.einsum(
            "bw,bwc->bc",
            weights.astype(jnp.bfloat16),
            window_keys,
            preferred_element_type=jnp.float32,
        )
        / cross_total
    )
    byte_out = (byte_states.astype(jnp.float32) + reached).astype(jnp.bfloat16)
    return (stream, byte_out)


def solution(mesh):
    torus = Mesh(mesh.devices.reshape(16, 2, mesh.shape["head"]), ("seq_0", "seq_1", "head"))
    return jax.shard_map(
        body,
        mesh=torus,
        in_specs=(
            P(SEQ, "head"),
            P(SEQ),
            P(),
            P(),
            P(SEQ, "head"),
            P(),
            P(SEQ, None, "head"),
            P("head", None),
            P("head", SEQ),
        ),
        out_specs=(P(SEQ, "head"), P(SEQ, "head")),
        check_vma=False,
    )
```

profile of v0, /device:TPU:1, one launch (start us, length us, event | category | flops | bytes accessed | tf_op | source)
XLA Modules:
  0.0 543.9 jit_solution(12014085182086419854)
XLA Ops:
  8.3 6.0 %all_gather.9 = bf16[256,3,256]{0,2,1:T(8,128)(2,1)} all-gather(bf16[128,3,256]{0,2,1:T(8,128)(2,1)S(1)} %copy.63), channel_id=1, replica_groups=mesh['seq_0'=16,'seq_1'=2,'head'=16] {'seq_1'}, dimensions={0}, use_global_device_ids=true | all-gather | bytes 589824 | tf_op jit(solution)/shard_map/all_gather | solution.py:48
  14.3 2.7 fusion.29
  18.3 94.8 %all_to_all.40 = f32[32,96,80]{1,2,0:T(8,128)S(1)} all-to-all(f32[32,96,80]{1,2,0:T(8,128)S(1)} %copy.61), channel_id=1, replica_groups=mesh['seq_0'=16,'seq_1'=2,'head'=16] {'seq_0','seq_1'}, dimensions={0} | all-to-all | bytes 1966080 | tf_op jit(solution)/shard_map/all_to_all | solution.py:26
  113.2 18.0 %all_to_all.41 = bf16[16,96,80]{1,2,0:T(8,128)(2,1)S(1)} all-to-all(bf16[16,96,80]{1,2,0:T(8,128)(2,1)S(1)} %broadcast_in_dim.46), channel_id=1, replica_groups=mesh['seq_0'=16,'seq_1'=2,'head'=16] {'head'}, dimensions={0} | all-to-all | bytes 491520 | tf_op jit(solution)/shard_map/all_to_all | solution.py:38
  132.2 3.9 all-to-all-start.2
  136.6 45.6 %all-to-all-done.2 = bf16[32,40,256]{2,1,0:T(8,128)(2,1)S(1)} async-done(((bf16[32,40,256]{2,1,0:T(8,128)(2,1)}), bf16[32,40,256]{2,1,0:T(8,128)(2,1)S(1)}, u32[]{:S(2)}, u32[]{:S(2)}) %all-to-all-start.2) | async-done | bytes 655392 | tf_op jit(solution)/shard_map/all_to_all | solution.py:38
  183.5 4.2 all-to-all-start.3
  187.8 14.3 %all-to-all-done.3 = bf16[16,96,256]{2,1,0:T(8,128)(2,1)S(1)} async-done(((bf16[16,96,256]{2,1,0:T(8,128)(2,1)}), bf16[16,96,256]{2,1,0:T(8,128)(2,1)S(1)}, u32[]{:S(2)}, u32[]{:S(2)}) %all-to-all-start.3) | async-done | bytes 786464 | tf_op jit(solution)/shard_map/all_to_all | solution.py:38
  202.7 4.9 convolution_convert_fusion
  208.6 3.3 copy.83
  211.9 115.2 %all-gather.5.cloned.1.call-done = bf16[3072,4,128]{2,0,1:T(8,128)(2,1)} async-done(((bf16[96,4,128]{2,0,1:T(8,128)(2,1)}), bf16[3072,4,128]{2,0,1:T(8,128)(2,1)}) %all-gather.5.cloned.1.call-update) | async-done | bytes 3145744 | tf_op jit(solution)/shard_map/all_gather | solution.py:55
  327.1 3.8 fusion.45
  330.8 17.5 %while.26 = (s32[]{:T(128)}, f32[2,96]{1,0:T(2,128)S(1)}, f32[2,96]{1,0:T(2,128)S(1)}, f32[2,96,128]{2,1,0:T(8,128)S(1)}, s32[6,512]{1,0:T(8,128)S(1)}, /*index=...) while((s32[]{:T(128)}, f32[2,96]{1,0:T(2,128)S(1)}, ...), condition=%wide.region_6.7_spmd.clone, body=%wide.region_3.6_spmd.clone.sunk | while | flops 51340224 | bytes 2166269 | solution.py:74
  331.0 1.3 fusion.69
  333.9 1.3 fusion.69
  349.3 50.6 %all_to_all.42 = f32[16,96,256]{2,1,0:T(8,128)S(1)} all-to-all(f32[16,96,256]{2,1,0:T(8,128)S(1)} %convolution_bitcast_fusion), channel_id=1, replica_groups=mesh['seq_0'=16,'seq_1'=2,'head'=16] {'head'}, dimensions={0} | all-to-all | bytes 3145728 | tf_op jit(solution)/shard_map/all_to_all | solution.py:26
  400.8 8.3 %all-to-all-start.5 = ((bf16[32,256,40]{1,2,0:T(8,128)(2,1)}), bf16[32,256,40]{1,2,0:T(8,128)(2,1)S(1)}, u32[]{:S(2)}, u32[]{:S(2)}) async-start(bf16[32,256,40]{1,2,0:T(8,128)(2,1)} %broadcast_in_dim.56), calls=%async_computation.5 | async-start | bytes 1310720 | tf_op jit(solution)/shard_map/all_to_all | solution.py:38
  409.2 36.1 %all-to-all-done.5 = bf16[32,256,40]{1,2,0:T(8,128)(2,1)S(1)} async-done(((bf16[32,256,40]{1,2,0:T(8,128)(2,1)}), bf16[32,256,40]{1,2,0:T(8,128)(2,1)S(1)}, u32[]{:S(2)}, u32[]{:S(2)}) %all-to-all-start.5) | async-done | bytes 655392 | tf_op jit(solution)/shard_map/all_to_all | solution.py:38
  445.7 19.6 %all_to_all.43 = f32[16,96,80]{1,2,0:T(8,128)S(1)} all-to-all(f32[16,96,80]{1,2,0:T(8,128)S(1)} %convolution_bitcast_fusion.1), channel_id=1, replica_groups=mesh['seq_0'=16,'seq_1'=2,'head'=16] {'head'}, dimensions={0} | all-to-all | bytes 983040 | tf_op jit(solution)/shard_map/all_to_all | solution.py:26
  466.3 4.1 all-to-all-start.7
  472.1 36.4 %all-to-all-done.7 = bf16[32,96,80]{1,2,0:T(8,128)(2,1)S(1)} async-done(((bf16[32,96,80]{1,2,0:T(8,128)(2,1)}), bf16[32,96,80]{1,2,0:T(8,128)(2,1)S(1)}, u32[]{:S(2)}, u32[]{:S(2)}) %all-to-all-start.7) | async-done | bytes 491552 | tf_op jit(solution)/shard_map/all_to_all | solution.py:38
  508.8 3.7 while.27
  512.7 18.1 %gather_fusion = bf16[6144,80]{1,0:T(8,128)(2,1)S(1)} fusion(bf16[776,80]{1,0:T(8,128)(2,1)S(1)} %copy.73, s32[6144]{0:T(1024)S(1)} %broadcast_clamp_fusion), kind=kCustom, calls=%fused_computation | custom fusion | bytes 1990656 | tf_op jit(solution)/shard_map/gather | solution.py:167
  532.0 4.2 multiply_reduce_fusion
  (138 shorter events, 31.8 us)
Async XLA Ops:
  7.2 195.5 %all-gather.3.cloned.1.call-start = ((), (), s32[]{:S(2)}) async-start(), calls=%async_computation.8 | async-start | bytes 6684672 | tf_op jit(solution)/shard_map/all_gather | solution.py:48
  113.1 18.2 %copy-start.3 = (bf16[40,256]{1,0:T(8,128)(2,1)S(1)}, bf16[40,256]{1,0:T(8,128)(2,1)}, u32[]{:S(2)}) copy-start(bf16[40,256]{1,0:T(8,128)(2,1)} %param.17) | copy-start | bytes 61444
  113.2 22.9 %copy-start.7 = (f32[1280]{0:T(1024)S(1)}, f32[1280]{0:T(1024)}, u32[]{:S(2)}) copy-start(f32[1280]{0:T(1024)} %param.16) | copy-start | bytes 15364
  132.2 50.0 %all-to-all-start.2 = ((bf16[32,40,256]{2,1,0:T(8,128)(2,1)}), bf16[32,40,256]{2,1,0:T(8,128)(2,1)S(1)}, u32[]{:S(2)}, u32[]{:S(2)}) async-start(bf16[32,40,256]{2,1,0:T(8,128)(2,1)} %broadcast_in_dim.47), calls=%async_computation.2 | async-start | bytes 1310720 | tf_op jit(solution)/shard_map/all_to_all | solution.py:38
  182.2 5.5 %copy-start.5 = (f32[4096]{0:T(1024)S(1)}, f32[4096]{0:T(1024)}, u32[]{:S(2)}) copy-start(f32[4096]{0:T(1024)} %param.18) | copy-start | bytes 49156
  183.5 18.6 %all-to-all-start.3 = ((bf16[16,96,256]{2,1,0:T(8,128)(2,1)}), bf16[16,96,256]{2,1,0:T(8,128)(2,1)S(1)}, u32[]{:S(2)}, u32[]{:S(2)}) async-start(bf16[16,96,256]{2,1,0:T(8,128)(2,1)} %broadcast_in_dim.53), calls=%async_computation.3 | async-start | bytes 1572864 | tf_op jit(solution)/shard_map/all_to_all | solution.py:38
  187.7 139.4 %all-gather.5.cloned.1.call-start = ((), (), s32[]{:S(2)}) async-start(), calls=%async_computation.9 | async-start | bytes 3244032 | tf_op jit(solution)/shard_map/all_gather | solution.py:55
  202.7 5.7 %copy-start.6 = (s32[3072]{0:T(1024)S(1)}, s32[3072]{0:T(1024)}, u32[]{:S(2)}) copy-start(s32[3072]{0:T(1024)} %param.15) | copy-start | bytes 36868
  349.3 50.6 %copy-start.4 = (bf16[256,40]{0,1:T(8,128)(2,1)S(1)}, bf16[256,40]{0,1:T(8,128)(2,1)}, u32[]{:S(2)}) copy-start(bf16[256,40]{0,1:T(8,128)(2,1)} %param.21) | copy-start | bytes 61444
  400.8 44.5 %all-to-all-start.5 = ((bf16[32,256,40]{1,2,0:T(8,128)(2,1)}), bf16[32,256,40]{1,2,0:T(8,128)(2,1)S(1)}, u32[]{:S(2)}, u32[]{:S(2)}) async-start(bf16[32,256,40]{1,2,0:T(8,128)(2,1)} %broadcast_in_dim.56), calls=%async_computation.5 | async-start | bytes 1310720 | tf_op jit(solution)/shard_map/all_to_all | solution.py:38
  409.2 56.1 %copy-start.1 = (bf16[96,256]{1,0:T(8,128)(2,1)}, bf16[96,256]{1,0:T(8,128)(2,1)S(1)}, u32[]{:S(2)}) copy-start(bf16[96,256]{1,0:T(8,128)(2,1)S(1)} %add_convert_fusion.1) | copy-start | bytes 147460
  465.3 5.1 copy-start.2
  465.3 5.6 %copy-start = (bf16[768,80]{0,1:T(8,128)(2,1)S(1)}, bf16[768,80]{0,1:T(8,128)(2,1)}, u32[]{:S(2)}) copy-start(bf16[768,80]{0,1:T(8,128)(2,1)} %param.13) | copy-start | bytes 368644
  466.3 42.1 %all-to-all-start.7 = ((bf16[32,96,80]{1,2,0:T(8,128)(2,1)}), bf16[32,96,80]{1,2,0:T(8,128)(2,1)S(1)}, u32[]{:S(2)}, u32[]{:S(2)}) async-start(bf16[32,96,80]{1,2,0:T(8,128)(2,1)} %broadcast_in_dim.57), calls=%async_computation.7 | async-start | bytes 1310720 | tf_op jit(solution)/shard_map/all_to_all | solution.py:38
Sparse Core Ops, SparseCore 0:
  14.4 187.4 all-gather.2
  208.6 118.4 all-gather.4
where the time goes:
time: 545 us; the launch traced here: 544 us
  waiting for transfers between devices  248 us (46%)
  blocking collectives  189 us (35%)
  local copies, waits for them, and re-layouts  33.7 us (6%)
  matrix products  27.2 us (5%)
  starting transfers between devices  20.6 us (4%)
  between operations  15.1 us (3%)
  other arithmetic  10.1 us (2%)
    all_to_all x3, blocking collectives, sum_at_owner(): lax.all_to_all(pieces, axis, split_axis=0, concat_axis=0, tiled=True)  165 us
    all_to_all x4, waiting for transfers between devices, sent_to_all(): lax.all_to_all(jnp.broadcast_to(x[None], (size, *x.shape)), axis, 0, 0, t...  132 us
    all_gather x1, waiting for transfers between devices, side_by_side(): out = lax.all_gather(both, axis, axis=dim, tiled=True)  115 us
    all_to_all x4, starting transfers between devices, sent_to_all(): lax.all_to_all(jnp.broadcast_to(x[None], (size, *x.shape)), axis, 0, 0, t...  20.5 us
    gather x1, local copies, waits for them, and re-layouts, body(): window_keys = picked[reach - lowest]  18.1 us
    all_to_all x1, blocking collectives, sent_to_all(): lax.all_to_all(jnp.broadcast_to(x[None], (size, *x.shape)), axis, 0, 0, t...  18 us
  transfers between devices with their start and end apart: 6, of which 5 were waited for; matrix products, arithmetic and copies ran while one was open for 2% of the time, Pallas kernels for 0%

commit v1 on v0

v1 whole, which is shorter than its diff:
```python
import functools
import math

import jax
import jax.numpy as jnp
from jax import lax
from jax.experimental import pallas as pl
from jax.experimental.pallas import tpu as pltpu
from jax.sharding import Mesh
from jax.sharding import PartitionSpec as P


HEAD_SIZE = 128
WINDOW = 8
LONGEST = 16
ZL = ("zm", "zp")
Z = ("zh", "zm", "zp")
SEQ = ("zh", "zm", "zp", "yl")
SKIP = ("zh", "zm", "yl")
PLANE = ("yl", "yh", "x")
HEAD = ("yh", "x", "c")
EPSILON = 1e-05
FLOOR_SCORE = -1e30
BF = jnp.bfloat16
F32 = jnp.float32
MAIN = 64
LANES = 128


VMEM = pl.BlockSpec(memory_space=pltpu.VMEM)
SMEM = pl.BlockSpec(memory_space=pltpu.SMEM)


def local_call(kernel, out, inputs, scratch=(), scalars=0, flops=10**8, moved=10**6):
    specs = [SMEM] * scalars + [VMEM] * (len(inputs) - scalars)
    many = isinstance(out, (list, tuple))
    return pl.pallas_call(
        kernel,
        out_shape=out,
        in_specs=specs,
        out_specs=[VMEM] * len(out) if many else VMEM,
        scratch_shapes=list(scratch),
        compiler_params=pltpu.CompilerParams(vmem_limit_bytes=48 << 20),
        cost_estimate=pl.CostEstimate(flops=flops, bytes_accessed=moved, transcendentals=0),
    )(*inputs)


def matmul(a, b):
    return lax.dot_general(a, b, (((1,), (0,)), ((), ())), preferred_element_type=F32)


def matmul_t(a, b):
    return lax.dot_general(a, b, (((1,), (1,)), ((), ())), preferred_element_type=F32)


def pool_kernel(flip, info, slots, ids, rows, out):
    blocks, packed_rows, _ = out.shape
    count = slots.shape[0] // (2 * blocks)
    half = count // 2
    group = packed_rows - half
    blank = jnp.zeros((group, LANES - group * (count // group)), F32)
    side = 1 - info[1] if flip else info[1]

    def step(i, unused):
        at = pl.multiple_of((2 * i + side) * count, count)
        match = jnp.where(slots[pl.ds(at, count), :] == ids[...], 1.0, 0.0).astype(BF)
        part = matmul_t(match, rows[...])
        out[i, 0:half, 0:MAIN] = part[0:half, 0:MAIN].astype(BF)
        out[i, 0:half, MAIN:LANES] = part[half:count, 0:MAIN].astype(BF)
        rest = [part[group * g : group * (g + 1), MAIN:] for g in range(count // group)]
        out[i, half:packed_rows, :] = jnp.concatenate(rest + [blank], axis=1).astype(BF)
        return unused

    lax.fori_loop(0, blocks, step, 0, unroll=4)


def sum_kernel(arrived, out):
    total = jnp.zeros(arrived.shape[1:], F32)
    for i in range(arrived.shape[0]):
        total = total + arrived[i].astype(F32)
    held = total.astype(BF)
    for i in range(out.shape[0]):
        out[i] = held


def embed_kernel(info, own, other, gain, w_in, out, keep):
    planes = own.shape[0] // 2
    count, size = keep.shape[1:]
    each = count // 2
    half = each // 2
    spare = size - MAIN
    group = own.shape[1] - half
    square = jnp.zeros((count, 1), F32)
    for side, source in ((0, own), (1, other)):
        for p in range(planes):
            two = [source[y * planes + p].astype(F32) for y in range(2)]
            main = [v[0:half, at : at + MAIN] for v in two for at in (0, MAIN)]
            main = jnp.concatenate(main, axis=0)
            rest = [
                v[half:, spare * g : spare * (g + 1)] for v in two for g in range(each // group)
            ]
            rest = jnp.concatenate(rest, axis=0)
            keep[side * planes + p, :, 0:MAIN] = main
            keep[side * planes + p, :, MAIN:size] = rest
            square = square + jnp.sum(main * main, axis=1, keepdims=True)
            square = square + jnp.sum(rest * rest, axis=1, keepdims=True)
    scale = lax.rsqrt(square / (2 * planes * size) + EPSILON)
    total = jnp.zeros(out.shape[1:], F32)
    for side in range(2):
        core = info[0] if side == 0 else 1 - info[0]
        for p in range(planes):
            h = 2 * p + core
            normed = keep[side * planes + p] * scale * gain[pl.ds(h, 1), :]
            at = pl.multiple_of(h * size, 16)
            total = total + matmul(normed.astype(BF), w_in[pl.ds(at, size), :])
    held = total.astype(BF)
    for i in range(out.shape[0]):
        out[i] = held


def project_kernel(info, own, other, gain, weights, queries, kv, down):
    planes = own.shape[0] // 2
    count, width = own.shape[1:]
    size = 2 * width
    columns = 3 * HEAD_SIZE
    square = jnp.zeros((count, width), F32)
    for source in (own, other):
        for b in range(2 * planes):
            wide = source[b].astype(F32)
            square = square + wide * wide
    square = jnp.sum(square, axis=1, keepdims=True)
    scale = lax.rsqrt(square / (2 * planes * size) + EPSILON)
    total = jnp.zeros((count, columns), F32)
    for side, source in ((0, own), (1, other)):
        core = info[0] if side == 0 else 1 - info[0]
        for p in range(planes):
            h = 2 * p + core
            both = jnp.concatenate([source[p], source[planes + p]], axis=1).astype(F32)
            attn_in = both * scale * gain[pl.ds(h, 1), :]
            at = pl.multiple_of(h * size, size)
            total = total + matmul(attn_in.astype(BF), weights[pl.ds(at, size), 0:columns])
    queries[...] = total[:, 0:HEAD_SIZE].astype(BF)
    held = total[:, HEAD_SIZE:].astype(BF)
    for i in range(kv.shape[0]):
        kv[i] = held
    down[...] = weights[:, columns:]


def attend_kernel(info, queries, slots, labels, *rest):
    pieces, keep, send, scores, held = rest[:-4], rest[-4], rest[-3], rest[-2], rest[-1]
    query = queries[...]
    own = pl.multiple_of(info[4] * query.shape[0], query.shape[0])
    mine = slots[pl.ds(own, query.shape[0]), :]
    peak = jnp.full((query.shape[0], 1), FLOOR_SCORE, F32)
    turns = ((0, 0), (3, 0), (1, 0), (2, 0), (2, labels.shape[1] // 2))
    start = 0
    for piece, (turn, at) in zip(pieces, turns):
        size = piece.shape[0]
        here = labels[pl.ds((info[3] + turn) % 4, 1), at : at + size]
        part = matmul_t(query, piece[:, 0:HEAD_SIZE]) * (1.0 / math.sqrt(HEAD_SIZE))
        part = jnp.where(here <= mine, part, FLOOR_SCORE)
        scores[:, start : start + size] = part
        peak = jnp.maximum(peak, jnp.max(part, axis=1, keepdims=True))
        start += size
    total = jnp.zeros_like(peak)
    mixed = jnp.zeros(query.shape, F32)
    start = 0
    for piece in pieces:
        size = piece.shape[0]
        weights = jnp.exp(scores[:, start : start + size] - peak)
        total = total + jnp.sum(weights, axis=1, keepdims=True)
        mixed = mixed + matmul(weights.astype(BF), piece[:, HEAD_SIZE:])
        start += size
    held[...] = mixed / total
    count = keep.shape[0]
    at = pl.multiple_of(info[1] * count, count)
    keep[...] = held[pl.ds(at, count), :].astype(BF)
    at = pl.multiple_of((1 - info[1]) * count, count)
    send[...] = held[pl.ds(at, count), :].astype(BF)


def out_kernel(info, kept, came, w_out, out):
    mine = kept[...]
    theirs = came[...]
    width = out.shape[2]
    at = pl.multiple_of(info[1] * HEAD_SIZE, HEAD_SIZE)
    other = pl.multiple_of((1 - info[1]) * HEAD_SIZE, HEAD_SIZE)
    for h in range(out.shape[0]):
        cols = slice(h * width, (h + 1) * width)
        part = matmul(mine, w_out[pl.ds(at, HEAD_SIZE), cols])
        part = part + matmul(theirs, w_out[pl.ds(other, HEAD_SIZE), cols])
        out[h] = part.astype(BF)


def down_kernel(info, arrived, embed, w_down, stream, out):
    count, width = stream.shape
    half = count // 2
    planes = embed.shape[0] // 2
    size = MAIN + LONGEST
    at = pl.multiple_of(info[1] * count, count)
    low = embed[info[2], pl.ds(at, count), :]
    high = embed[planes + info[2], pl.ds(at, count), :]
    total = jnp.concatenate([low, high], axis=1).astype(F32)
    added = jnp.zeros(total.shape, F32)
    for h in range(arrived.shape[0]):
        added = added + arrived[h].astype(F32)
    held = (total + added).astype(BF)
    stream[...] = held
    group = out.shape[1] - half
    blank = jnp.zeros((group, LANES - LONGEST * (count // group)), F32)
    for h in range(out.shape[0]):
        part = matmul(held, w_down[h * width : (h + 1) * width, :])
        out[h, 0:half, 0:MAIN] = part[0:half, 0:MAIN].astype(BF)
        out[h, 0:half, MAIN:LANES] = part[half:, 0:MAIN].astype(BF)
        rest = [part[group * g : group * (g + 1), MAIN:size] for g in range(count // group)]
        out[h, half:, :] = jnp.concatenate(rest + [blank], axis=1).astype(BF)


def pick_rows(base, labels_main, labels_rest, states, main, rest, put):
    groups = labels_rest.shape[0]
    half = groups * LONGEST // 2
    for i in range(states.shape[0]):
        main[i * half : (i + 1) * half, :] = states[i, 0:half, :]
        rest[i * LONGEST : (i + 1) * LONGEST, :] = states[i, half:, :]
    step = LANES

    def hot(at, label):
        wanted = base + at + lax.broadcasted_iota(jnp.int32, (step, label.shape[1]), 0)
        return jnp.where(wanted == label, 1.0, 0.0).astype(BF)

    def pick(i, unused):
        at = pl.multiple_of(i * step, step)
        low = matmul(hot(at, labels_main[0:1, :]), main[...])
        high = matmul(hot(at, labels_main[1:2, :]), main[...])
        tail = jnp.zeros((step, LONGEST), F32)
        for g in range(groups):
            here = matmul(hot(at, labels_rest[g : g + 1, :]), rest[...])
            tail = tail + here[:, g * LONGEST : (g + 1) * LONGEST]
        put(at, low[:, 0:MAIN] + high[:, MAIN:LANES], tail)
        return unused

    return pick


def near_kernel(info, labels_main, labels_rest, states, out, main, rest):
    group = info[5]

    def put(at, low, tail):
        blank = jnp.zeros((LANES, LANES - MAIN - LONGEST), F32)
        out[pl.ds(at, LANES), :] = jnp.concatenate([low, tail, blank], axis=1)

    pick = pick_rows(
        info[6], labels_main.at[group], labels_rest.at[group], states, main, rest, put
    )
    lax.fori_loop(0, out.shape[0] // LANES, pick, 0, unroll=True)


def cross_kernel(
    info, labels_main, labels_rest, ids, rows, states, near, out, picked, main, rest
):
    size = rows.shape[0]
    group = 1 - info[5]
    base = info[6]

    def put(at, low, tail):
        blank = jnp.zeros((LANES, LANES - MAIN - LONGEST), F32)
        here = jnp.concatenate([low, tail, blank], axis=1)
        picked[pl.ds(at, LANES), :] = near[pl.ds(at, LANES), :] + here

    pick = pick_rows(base, labels_main.at[group], labels_rest.at[group], states, main, rest, put)
    lax.fori_loop(0, near.shape[0] // LANES, pick, 0, unroll=True)
    keys = picked[...].astype(BF)[:, 0:size]
    turned = picked[...].T.astype(BF)
    wanted = base + lax.broadcasted_iota(jnp.int32, (near.shape[0], LANES), 0)
    allowed = wanted >= 0

    for i in range(rows.shape[1] // LANES):
        at = slice(i * LANES, (i + 1) * LANES)
        mine = rows[:, at]
        far = ids[:, at] - wanted
        close = (far >= 0) & (far < WINDOW) & allowed
        scores = matmul(keys, mine) * (1.0 / math.sqrt(size))
        scores = jnp.where(close, scores, FLOOR_SCORE)
        weights = jnp.exp(scores - jnp.max(scores, axis=0, keepdims=True))
        total = jnp.sum(weights, axis=0, keepdims=True)
        reached = matmul(turned, weights.astype(BF))[0:size] / total
        out[:, at] = (mine.astype(F32) + reached).astype(BF)


def shift(x, axis, by):
    n = lax.axis_size(axis)
    return lax.ppermute(x, axis, [(i, (i + by) % n) for i in range(n)])


def over_plane(copies):
    near = lax.all_to_all(copies, PLANE, 0, 0, tiled=True)
    return near, shift(near, "c", 1)


def over_z(four):
    half = four.shape[0] // 2
    after = shift(four, Z, 1)
    before = shift(four, Z, -1)
    return [four, after, before, shift(four[:half], Z, 2), shift(four[half:], Z, -2)]


def layer(byte_states, patch_ids, slot_patch, pool_gain, w_in, attn_gain, w_qkv, w_out, w_down):
    n_z = lax.axis_size(Z)
    n_zl = lax.axis_size(ZL)
    n_yl = lax.axis_size("yl")
    n_head = lax.axis_size(HEAD)
    patches = slot_patch.shape[0]
    rows_z = patches // n_z
    rows_each = rows_z // n_yl
    bytes_here, cross_size = byte_states.shape
    info = jnp.stack(
        [
            lax.axis_index("c"),
            lax.axis_index("yl"),
            lax.axis_index(("yh", "x")),
            lax.axis_index(ZL),
            lax.axis_index(Z),
            lax.axis_index("zp"),
            patch_ids[0] - (WINDOW - 1),
        ]
    ).astype(jnp.int32)
    n_plane = lax.axis_size(PLANE)
    slots = slot_patch[:, None]
    rows = byte_states.T
    first = info[1] == 0

    w_in_parts = w_in.reshape(w_in.shape[0], n_yl, -1).transpose(1, 0, 2)
    w_in_parts = jnp.broadcast_to(w_in_parts[None], (n_z, *w_in_parts.shape))
    w_in_parts = w_in_parts.reshape(n_z * n_yl, w_in.shape[0], -1)
    w_in_here = lax.all_to_all(w_in_parts, SEQ, 0, 0, tiled=True)
    w_in_here = w_in_here.reshape(-1, w_in_parts.shape[2])

    halves = [
        jnp.concatenate([w_qkv[:, j, k * HEAD_SIZE : (k + 1) * HEAD_SIZE] for j in range(3)], axis=1)
        for k in range(n_yl)
    ]
    depth = w_qkv.shape[0]
    down_pieces = [w_down[:depth], w_down[depth:]]
    sent = jnp.concatenate([jnp.where(first, halves[1], halves[0]), *down_pieces], axis=1)
    came = shift(sent, "yl", 1)
    kept = jnp.concatenate([jnp.where(first, halves[0], halves[1]), *down_pieces], axis=1)
    low = jnp.where(first, kept, came)
    high = jnp.where(first, came, kept)
    wide = halves[0].shape[1]
    part = w_down.shape[1]
    down_both = [
        jnp.concatenate([v[:, wide : wide + part], v[:, wide + part :]], axis=0) for v in (low, high)
    ]
    blank = jnp.zeros((2 * depth, LANES - 2 * part), BF)
    mine = jnp.concatenate([low[:, :wide], high[:, :wide]], axis=0)
    weights = lax.all_gather(
        jnp.concatenate([mine, *down_both, blank], axis=1), Z, axis=0, tiled=True
    )

    packed = jax.ShapeDtypeStruct((n_z, rows_each // 2 + LONGEST, LANES), BF)
    pool_inputs = [info, slots, patch_ids[None, :], rows]
    sent = local_call(functools.partial(pool_kernel, True), packed, pool_inputs, scalars=1)
    came = shift(sent, "yl", 1)
    kept = local_call(functools.partial(pool_kernel, False), packed, pool_inputs, scalars=1)
    pooled = (kept.astype(F32) + came.astype(F32)).astype(BF)
    pooled = lax.all_to_all(pooled, Z, 0, 0, tiled=True)
    pooled = local_call(
        sum_kernel, jax.ShapeDtypeStruct((n_plane, *pooled.shape[1:]), BF), [pooled]
    )
    embed = local_call(
        embed_kernel,
        jax.ShapeDtypeStruct((n_plane, rows_z, w_in_here.shape[1]), BF),
        [info, *over_plane(pooled), pool_gain.reshape(n_head, cross_size), w_in_here],
        scratch=[pltpu.VMEM((n_head, rows_z, cross_size), F32)],
        scalars=1,
    )
    own_embed, other_embed = over_plane(embed)
    queries, kv, down_here = local_call(
        project_kernel,
        [
            jax.ShapeDtypeStruct((rows_z, HEAD_SIZE), BF),
            jax.ShapeDtypeStruct((n_z // n_zl, rows_z, 2 * HEAD_SIZE), BF),
            jax.ShapeDtypeStruct((weights.shape[0], LANES), BF),
        ],
        [info, own_embed, other_embed, attn_gain.reshape(n_head, -1), weights],
        scalars=1,
    )
    labels = slot_patch.reshape(n_z // n_zl, n_zl, rows_z).transpose(1, 0, 2).reshape(n_zl, -1)
    kv = lax.all_to_all(kv, "zh", 0, 0, tiled=True).reshape(-1, kv.shape[2])
    kept, sent = local_call(
        attend_kernel,
        [jax.ShapeDtypeStruct((rows_each, HEAD_SIZE), BF)] * 2,
        [
            info,
            queries,
            slots,
            labels,
            *over_z(kv),
        ],
        scratch=[pltpu.VMEM((rows_z, patches), F32), pltpu.VMEM((rows_z, HEAD_SIZE), F32)],
        scalars=1,
    )
    out_part = local_call(
        out_kernel,
        jax.ShapeDtypeStruct((n_head, rows_each, w_out.shape[1] // n_head), BF),
        [info, kept, shift(sent, "yl", 1), w_out],
        scalars=1,
    )
    arrived = lax.all_to_all(out_part, HEAD, 0, 0, tiled=True)
    stream, down_part = local_call(
        down_kernel,
        [
            jax.ShapeDtypeStruct((rows_each, w_in.shape[1]), BF),
            jax.ShapeDtypeStruct((n_head, rows_each // 2 + LONGEST, LANES), BF),
        ],
        [info, arrived, own_embed, down_here],
        scalars=1,
    )
    states = lax.all_to_all(down_part, HEAD, 0, 0, tiled=True)
    n_skip = lax.axis_size(SKIP)
    states = local_call(
        sum_kernel, jax.ShapeDtypeStruct((n_skip, *states.shape[1:]), BF), [states]
    )
    states = lax.all_to_all(states, SKIP, 0, 0, tiled=True)
    others = shift(states, "zp", 1)
    by_source = slot_patch.reshape(-1, 2, n_yl, rows_each).transpose(1, 0, 2, 3)
    by_source = by_source.reshape(2, n_skip, rows_each)
    labels_main = by_source.reshape(2, n_skip, 2, -1).transpose(0, 2, 1, 3).reshape(2, 2, -1)
    labels_rest = by_source.reshape(2, n_skip, -1, LONGEST).transpose(0, 2, 1, 3)
    labels_rest = labels_rest.reshape(2, rows_each // LONGEST, -1)
    capacity = bytes_here + LANES
    room = [
        pltpu.VMEM((n_skip * rows_each // 2, LANES), BF),
        pltpu.VMEM((n_skip * LONGEST, LANES), BF),
    ]
    near = local_call(
        near_kernel,
        jax.ShapeDtypeStruct((capacity, LANES), F32),
        [info, labels_main, labels_rest, states],
        scratch=room,
        scalars=1,
    )
    byte_out = local_call(
        cross_kernel,
        jax.ShapeDtypeStruct((cross_size, bytes_here), BF),
        [info, labels_main, labels_rest, patch_ids[None, :], rows, others, near],
        scratch=[pltpu.VMEM((capacity, LANES), F32), *room],
        scalars=1,
    ).T
    return (stream, byte_out)


def solution(mesh):
    torus = Mesh(
        mesh.devices.reshape(4, 2, 2, 2, 2, 4, 2), ("zh", "zm", "zp", "yl", "yh", "x", "c")
    )
    return jax.shard_map(
        layer,
        mesh=torus,
        in_specs=(
            P(SEQ, HEAD),
            P(SEQ),
            P(),
            P(),
            P(SEQ, HEAD),
            P(),
            P(SEQ, None, HEAD),
            P(HEAD, None),
            P(HEAD, SEQ),
        ),
        out_specs=(P(SEQ, HEAD), P(SEQ, HEAD)),
        check_vma=False,
    )
```

time: 545 us -> 283 us (0.52)
  waiting for transfers between devices: 248 us -> 48.5 us
  blocking collectives: 189 us -> 125 us
  starting transfers between devices: 20.6 us -> 55.9 us
  matrix products: 27.2 us -> 0 us
  local copies, waits for them, and re-layouts: 33.7 us -> 7.86 us
  Pallas kernels: 0 us -> 24.6 us
  other arithmetic: 10.1 us -> 1.14 us
    all_gather x2 -> x1, waiting for transfers between devices: 115 us -> 0.01 us  [layer(): lax.all_gather(jnp.concatenate([mine, *down_both, blank], axis=1), Z, axi...]
    all_to_all x4 -> x2, waiting for transfers between devices: 132 us -> 27.3 us  [the longest x1 19.8 us: layer(): w_in_here = lax.all_to_all(w_in_parts, SEQ, 0, 0, tiled=True)]
    all_to_all x4 -> x6, blocking collectives: 183 us -> 125 us  [the longest x1 33.3 us: layer(): pooled = lax.all_to_all(pooled, Z, 0, 0, tiled=True)]
    ppermute x0 -> x10, starting transfers between devices: none -> 39.3 us  [shift(): return lax.ppermute(x, axis, [(i, (i + by) % n) for i in range(n)])]
    dot_general x23 -> x0, matrix products: 27.2 us -> none  [the longest x6 7.61 us: update(): jnp.einsum('hqd,khd->hqk', queries, key_block, preferred_element_type=jnp...]
    pallas_call x0 -> x11, Pallas kernels: none -> 24.6 us  [local_call(): pl.pallas_call(kernel, out_shape=out, in_specs=specs, out_specs=[VMEM] *...]
    ppermute x0 -> x10, waiting for transfers between devices: none -> 21.3 us  [shift(): return lax.ppermute(x, axis, [(i, (i + by) % n) for i in range(n)])]
    gather x1 -> x0, local copies, waits for them, and re-layouts: 18.1 us -> none  [body(): window_keys = picked[reach - lowest]]
  transfers between devices with their start and end apart: 6 -> 13, of which waited for: 5 -> 9; matrix products, arithmetic and copies ran while one was open for 2% -> 2% of each run, Pallas kernels for 0% -> 4%
where the time goes in v1:
time: 283 us; the launch traced here: 279 us
  blocking collectives  125 us (44%)
  starting transfers between devices  55.9 us (20%)
  waiting for transfers between devices  48.5 us (17%)
  Pallas kernels  24.6 us (9%)
  between operations  15.1 us (5%)
  local copies, waits for them, and re-layouts  7.86 us (3%)
    ppermute x10, starting transfers between devices, shift(): return lax.ppermute(x, axis, [(i, (i + by) % n) for i in range(n)])  39.3 us
    all_to_all x1, blocking collectives, layer(): pooled = lax.all_to_all(pooled, Z, 0, 0, tiled=True)  33.3 us
    all_to_all x1, blocking collectives, layer(): kv = lax.all_to_all(kv, 'zh', 0, 0, tiled=True).reshape(-1, kv.shape[2])  24.7 us
    pallas_call x11, Pallas kernels, local_call(): pl.pallas_call(kernel, out_shape=out, in_specs=specs, out_specs=[VMEM] *...  24.6 us
    ppermute x10, waiting for transfers between devices, shift(): return lax.ppermute(x, axis, [(i, (i + by) % n) for i in range(n)])  21.3 us
    all_to_all x1, blocking collectives, layer(): states = lax.all_to_all(states, SKIP, 0, 0, tiled=True)  21.1 us
    all_to_all x1, blocking collectives, layer(): arrived = lax.all_to_all(out_part, HEAD, 0, 0, tiled=True)  19.8 us
    all_to_all x1, waiting for transfers between devices, layer(): w_in_here = lax.all_to_all(w_in_parts, SEQ, 0, 0, tiled=True)  19.8 us
  transfers between devices with their start and end apart: 13, of which 9 were waited for; matrix products, arithmetic and copies ran while one was open for 2% of the time, Pallas kernels for 4%

profile of v1, /device:TPU:1, one launch (start us, length us, event | category | flops | bytes accessed | tf_op | source)
XLA Modules:
  0.0 278.6 jit_solution(15480300250788002191)
XLA Ops:
  9.2 4.0 %collective-permute-start.3 = (bf16[128,464]{1,0:T(8,128)(2,1)S(1)}, bf16[128,464]{1,0:T(8,128)(2,1)S(1)}, u32[]{:S(2)}, u32[]{:S(2)}) collective-permute-start(bf16[128,464]{1,0:T(8,128)(2,1)S(1)} %pad_maximum_fusion), channel_id=1, source_target_pairs={{0,16},{16,0},{1,17},{17,1},{2,18},{18,2},{3,19},{19,3},{4,20},{20... | collective-permute-start | bytes 356360 | tf_op jit(solution)/shard_map/ppermute | solution.py:292
  18.5 2.3 shard_map.105
  20.9 3.4 %collective-permute-start = (bf16[16,64,128]{2,1,0:T(8,128)(2,1)S(1)}, bf16[16,64,128]{2,1,0:T(8,128)(2,1)S(1)}, u32[]{:S(2)}, u32[]{:S(2)}) collective-permute-start(bf16[16,64,128]{2,1,0:T(8,128)(2,1)S(1)} %shard_map.105), channel_id=1, source_target_pairs={{0,16},{16,0},{1,17},{17,1},{2,18},{18,2},{3,19},{19,3},{4,20},{20... | collective-permute-start | bytes 786440 | tf_op jit(solution)/shard_map/ppermute | solution.py:292
  24.2 2.3 shard_map.104
  28.1 33.3 %all_to_all.40.arrived = bf16[16,64,128]{2,1,0:T(8,128)(2,1)S(1)} all-to-all(bf16[16,64,128]{2,1,0:T(8,128)(2,1)S(1)} %add_convert_fusion), channel_id=1, replica_groups=mesh['zh'=4,'zm'=2,'zp'=2,'yl'=2,'yh'=2,'x'=4,'c'=2] {'zh','zm','zp'}, dimensions={0} | all-to-all | bytes 524288 | tf_op jit(solution)/shard_map/all_to_all | solution.py:366
  62.1 7.6 %all-to-all-start.1 = ((bf16[16,64,128]{2,1,0:T(8,128)(2,1)}), bf16[16,64,128]{2,1,0:T(8,128)(2,1)S(1)}, u32[]{:S(2)}, u32[]{:S(2)}) async-start(bf16[16,64,128]{2,1,0:T(8,128)(2,1)} %shard_map.106), calls=%async_computation.1 | async-start | bytes 524288 | tf_op jit(solution)/shard_map/all_to_all | solution.py:296
  69.8 7.5 %all-to-all-done.1.own = bf16[16,64,128]{2,1,0:T(8,128)(2,1)S(1)} async-done(((bf16[16,64,128]{2,1,0:T(8,128)(2,1)}), bf16[16,64,128]{2,1,0:T(8,128)(2,1)S(1)}, u32[]{:S(2)}, u32[]{:S(2)}) %all-to-all-start.1) | async-done | bytes 262176 | tf_op jit(solution)/shard_map/all_to_all | solution.py:296
  78.1 8.9 %all-to-all-start.2 = ((bf16[32,40,128]{2,1,0:T(8,128)(2,1)}), bf16[32,40,128]{2,1,0:T(8,128)(2,1)S(1)}, u32[]{:S(2)}, u32[]{:S(2)}) async-start(bf16[32,40,128]{2,1,0:T(8,128)(2,1)} %bitcast.9), calls=%async_computation.2 | async-start | bytes 655360 | tf_op jit(solution)/shard_map/all_to_all | solution.py:335
  87.0 5.7 %collective-permute-start.1 = (bf16[16,64,128]{2,1,0:T(8,128)(2,1)S(1)}, bf16[16,64,128]{2,1,0:T(8,128)(2,1)S(1)}, u32[]{:S(2)}, u32[]{:S(2)}) collective-permute-start(bf16[16,64,128]{2,1,0:T(8,128)(2,1)S(1)} %all-to-all-done.1.own), channel_id=1, source_target_pairs={{0,1},{1,0},{2,3},{3,2},{4,5},{5,4},{6,7},{7,6},{8,9},{9,8},{10,11... | collective-permute-start | bytes 786440 | tf_op jit(solution)/shard_map/ppermute | solution.py:292
  92.8 19.8 %all-to-all-done.2 = bf16[32,40,128]{2,1,0:T(8,128)(2,1)S(1)} async-done(((bf16[32,40,128]{2,1,0:T(8,128)(2,1)}), bf16[32,40,128]{2,1,0:T(8,128)(2,1)S(1)}, u32[]{:S(2)}, u32[]{:S(2)}) %all-to-all-start.2) | async-done | bytes 327712 | tf_op jit(solution)/shard_map/all_to_all | solution.py:335
  112.6 3.3 %shard_map.107 = bf16[16,192,128]{2,1,0:T(8,128)(2,1)S(1)} custom-call(s32[7]{0:T(128)S(1)} %stack.28.info, bf16[16,64,128]{2,1,0:T(8,128)(2,1)S(1)} %all-to-all-done.1.own, bf16[16,64,128]{2,1,0:T(8,128)(2,1)S(1)} %collective-permute-done.1.other, f32[16,80]{1,0:T(8,128)S(1)} %reshape.43.gain, bf16[1280,128]{1,0:T(8,128)(2,1)S(1)} %bitcast.38), custom_call_target="tpu_custom_call" | custom-call | flops 100000000 | bytes 1000000 | tf_op jit(solution)/shard_map/pallas_call | solution.py:37
  115.9 14.6 %all_to_all.41.own.embed = bf16[16,192,128]{2,1,0:T(8,128)(2,1)S(1)} all-to-all(bf16[16,192,128]{2,1,0:T(8,128)(2,1)S(1)} %shard_map.107), channel_id=1, replica_groups=mesh['zh'=4,'zm'=2,'zp'=2,'yl'=2,'yh'=2,'x'=4,'c'=2] {'yl','yh','x'}, dimensions={0} | all-to-all | bytes 1572864 | tf_op jit(solution)/shard_map/all_to_all | solution.py:296
  130.5 7.4 %collective-permute-start.2 = (bf16[16,192,128]{2,1,0:T(8,128)(2,1)S(1)}, bf16[16,192,128]{2,1,0:T(8,128)(2,1)}, u32[]{:S(2)}, u32[]{:S(2)}) collective-permute-start(bf16[16,192,128]{2,1,0:T(8,128)(2,1)S(1)} %all_to_all.41.own.embed), channel_id=1, source_target_pairs={{0,1},{1,0},{2,3},{3,2},{4,5},{5,4},{6,7},{7,6},{8,9},{9,8},{10,11... | collective-permute-start | bytes 2359304 | tf_op jit(solution)/shard_map/ppermute | solution.py:292
  139.9 3.9 %shard_map.108 = (bf16[192,128]{1,0:T(8,128)(2,1)S(1)}, bf16[4,192,256]{2,1,0:T(8,128)(2,1)S(1)}, bf16[4096,128]{1,0:T(8,128)(2,1)S(1)}) custom-call(s32[7]{0:T(128)S(1)} %stack.28.info, bf16[16,192,128]{2,1,0:T(8,128)(2,1)S(1)} %all_to_all.41.own.embed, bf16[16,192,128]{2,1,0:T(8,128)(2,1)} %collective-permute-done.2.other, f32[16,256]{1,0:T(8,128)S(1)} %reshape.47.gain, ...), custom_call_target="tpu_custom_call" | custom-call | flops 100000000 | bytes 1000000 | tf_op jit(solution)/shard_map/pallas_call | solution.py:37
  144.8 24.7 %all_to_all.42 = bf16[4,192,256]{2,1,0:T(8,128)(2,1)S(1)} all-to-all(bf16[4,192,256]{2,1,0:T(8,128)(2,1)S(1)} %get-tuple-element.10), channel_id=1, replica_groups=mesh['zh'=4,'zm'=2,'zp'=2,'yl'=2,'yh'=2,'x'=4,'c'=2] {'zh'}, dimensions={0} | all-to-all | bytes 786432 | tf_op jit(solution)/shard_map/all_to_all | solution.py:389
  169.6 4.6 %collective-permute-start.4 = (bf16[768,256]{1,0:T(8,128)(2,1)S(1)}, bf16[768,256]{1,0:T(8,128)(2,1)S(1)}, u32[]{:S(2)}, u32[]{:S(2)}) collective-permute-start(bf16[768,256]{1,0:T(8,128)(2,1)S(1)} %bitcast.35), channel_id=1, source_target_pairs={{0,32},{32,64},{64,96},{96,128},{128,160},{160,192},{192,224},{224... | collective-permute-start | bytes 1179656 | tf_op jit(solution)/shard_map/ppermute | solution.py:292
  176.9 6.4 %collective-permute-start.6 = (bf16[384,256]{1,0:T(8,128)(2,1)}, bf16[384,256]{1,0:T(8,128)(2,1)S(1)}, u32[]{:S(2)}, u32[]{:S(2)}) collective-permute-start(bf16[384,256]{1,0:T(8,128)(2,1)} %bitcast.19), channel_id=1, source_target_pairs={{0,64},{32,96},{64,128},{96,160},{128,192},{160,224},{192,256},{22... | collective-permute-start | bytes 589832 | tf_op jit(solution)/shard_map/ppermute | solution.py:292
  188.1 9.3 %collective-permute-done.7.rest_4_ = bf16[384,256]{1,0:T(8,128)(2,1)} collective-permute-done((bf16[384,256]{1,0:T(8,128)(2,1)}, bf16[384,256]{1,0:T(8,128)(2,1)}, u32[]{:S(2)}, u32[]{:S(2)}) %collective-permute-start.7) | collective-permute-done | bytes 196640 | tf_op jit(solution)/shard_map/ppermute | solution.py:292
  197.4 2.3 shard_map.109
  201.7 2.6 collective-permute-done.8.came
  205.5 19.8 %all_to_all.43.arrived = bf16[16,96,256]{2,1,0:T(8,128)(2,1)S(1)} all-to-all(bf16[16,96,256]{2,1,0:T(8,128)(2,1)S(1)} %shard_map.110), channel_id=1, replica_groups=mesh['zh'=4,'zm'=2,'zp'=2,'yl'=2,'yh'=2,'x'=4,'c'=2] {'yh','x','c'}, dimensions={0} | all-to-all | bytes 1572864 | tf_op jit(solution)/shard_map/all_to_all | solution.py:409
  226.9 11.9 %all_to_all.44.arrived = bf16[16,64,128]{2,1,0:T(8,128)(2,1)S(1)} all-to-all(bf16[16,64,128]{2,1,0:T(8,128)(2,1)S(1)} %get-tuple-element.15), channel_id=1, replica_groups=mesh['zh'=4,'zm'=2,'zp'=2,'yl'=2,'yh'=2,'x'=4,'c'=2] {'yh','x','c'}, dimensions={0} | all-to-all | bytes 524288 | tf_op jit(solution)/shard_map/all_to_all | solution.py:419
  238.9 21.1 %all_to_all.45.states = bf16[16,64,128]{2,1,0:T(8,128)(2,1)S(1)} all-to-all(bf16[16,64,128]{2,1,0:T(8,128)(2,1)S(1)} %shard_map.112), channel_id=1, replica_groups=mesh['zh'=4,'zm'=2,'zp'=2,'yl'=2,'yh'=2,'x'=4,'c'=2] {'zh','zm','yl'}, dimensions={0} | all-to-all | bytes 524288 | tf_op jit(solution)/shard_map/all_to_all | solution.py:424
  267.1 4.7 %shard_map.114 = bf16[80,768]{1,0:T(8,128)(2,1)} custom-call(s32[7]{0:T(128)S(1)} %stack.28.info, s32[2,2,768]{2,1,0:T(2,128)S(1)} %reshape.52.labels_main, s32[2,6,256]{2,1,0:T(8,128)S(1)} %reshape.54.labels_rest, s32[1,768]{1,0:T(1,128)S(1)} %broadcast_in_dim.17.ids, bf16[80,768]{1,0:T(8,128)(2,1)S(1)} %bitcast.41, ...), custom_call_target="tpu_custom_call" | custom-call | flops 100000000 | bytes 1000000 | tf_op jit(solution)/shard_map/pallas_call | solution.py:37
  (73 shorter events, 32.1 us)
Async XLA Ops:
  7.2 9.5 %copy-start.8 = (s32[768]{0:T(1024)S(1)}, s32[768]{0:T(1024)}, u32[]{:S(2)}) copy-start(s32[768]{0:T(1024)} %param.10) | copy-start | bytes 9220
  7.2 10.1 %copy-start.4 = (s32[3072]{0:T(1024)S(1)}, s32[3072]{0:T(1024)}, u32[]{:S(2)}) copy-start(s32[3072]{0:T(1024)} %param.11) | copy-start | bytes 36868
  7.2 132.7 %all-gather.2.cloned.1.call-start = ((), (), s32[]{:S(2)}) async-start(), calls=%async_computation.8 | async-start | bytes 4456448 | tf_op jit(solution)/shard_map/all_gather | solution.py:356
  9.1 9.4 %copy-start.1 = (bf16[768,80]{0,1:T(8,128)(2,1)S(1)}, bf16[768,80]{0,1:T(8,128)(2,1)}, u32[]{:S(2)}) copy-start(bf16[768,80]{0,1:T(8,128)(2,1)} %param.9) | copy-start | bytes 368644
  9.2 6.4 %collective-permute-start.3 = (bf16[128,464]{1,0:T(8,128)(2,1)S(1)}, bf16[128,464]{1,0:T(8,128)(2,1)S(1)}, u32[]{:S(2)}, u32[]{:S(2)}) collective-permute-start(bf16[128,464]{1,0:T(8,128)(2,1)S(1)} %pad_maximum_fusion), channel_id=1, source_target_pairs={{0,16},{16,0},{1,17},{17,1},{2,18},{18,2},{3,19},{19,3},{4,20},{20... | collective-permute-start | bytes 356360 | tf_op jit(solution)/shard_map/ppermute | solution.py:292
  20.8 48.9 %copy-start.5 = (bf16[40,256]{1,0:T(8,128)(2,1)S(1)}, bf16[40,256]{1,0:T(8,128)(2,1)}, u32[]{:S(2)}) copy-start(bf16[40,256]{1,0:T(8,128)(2,1)} %param.13) | copy-start | bytes 61444
  20.9 7.1 %collective-permute-start = (bf16[16,64,128]{2,1,0:T(8,128)(2,1)S(1)}, bf16[16,64,128]{2,1,0:T(8,128)(2,1)S(1)}, u32[]{:S(2)}, u32[]{:S(2)}) collective-permute-start(bf16[16,64,128]{2,1,0:T(8,128)(2,1)S(1)} %shard_map.105), channel_id=1, source_target_pairs={{0,16},{16,0},{1,17},{17,1},{2,18},{18,2},{3,19},{19,3},{4,20},{20... | collective-permute-start | bytes 786440 | tf_op jit(solution)/shard_map/ppermute | solution.py:292
  26.5 66.2 %copy-start.7 = (f32[1280]{0:T(1024)S(1)}, f32[1280]{0:T(1024)}, u32[]{:S(2)}) copy-start(f32[1280]{0:T(1024)} %param.12) | copy-start | bytes 15364
  62.1 15.2 %all-to-all-start.1 = ((bf16[16,64,128]{2,1,0:T(8,128)(2,1)}), bf16[16,64,128]{2,1,0:T(8,128)(2,1)S(1)}, u32[]{:S(2)}, u32[]{:S(2)}) async-start(bf16[16,64,128]{2,1,0:T(8,128)(2,1)} %shard_map.106), calls=%async_computation.1 | async-start | bytes 524288 | tf_op jit(solution)/shard_map/all_to_all | solution.py:296
  69.8 68.1 %copy-start.6 = (f32[4096]{0:T(1024)S(1)}, f32[4096]{0:T(1024)}, u32[]{:S(2)}) copy-start(f32[4096]{0:T(1024)} %param.14) | copy-start | bytes 49156
  78.1 34.5 %all-to-all-start.2 = ((bf16[32,40,128]{2,1,0:T(8,128)(2,1)}), bf16[32,40,128]{2,1,0:T(8,128)(2,1)S(1)}, u32[]{:S(2)}, u32[]{:S(2)}) async-start(bf16[32,40,128]{2,1,0:T(8,128)(2,1)} %bitcast.9), calls=%async_computation.2 | async-start | bytes 655360 | tf_op jit(solution)/shard_map/all_to_all | solution.py:335
  87.0 25.6 %collective-permute-start.1 = (bf16[16,64,128]{2,1,0:T(8,128)(2,1)S(1)}, bf16[16,64,128]{2,1,0:T(8,128)(2,1)S(1)}, u32[]{:S(2)}, u32[]{:S(2)}) collective-permute-start(bf16[16,64,128]{2,1,0:T(8,128)(2,1)S(1)} %all-to-all-done.1.own), channel_id=1, source_target_pairs={{0,1},{1,0},{2,3},{3,2},{4,5},{5,4},{6,7},{7,6},{8,9},{9,8},{10,11... | collective-permute-start | bytes 786440 | tf_op jit(solution)/shard_map/ppermute | solution.py:292
  130.5 9.4 %collective-permute-start.2 = (bf16[16,192,128]{2,1,0:T(8,128)(2,1)S(1)}, bf16[16,192,128]{2,1,0:T(8,128)(2,1)}, u32[]{:S(2)}, u32[]{:S(2)}) collective-permute-start(bf16[16,192,128]{2,1,0:T(8,128)(2,1)S(1)} %all_to_all.41.own.embed), channel_id=1, source_target_pairs={{0,1},{1,0},{2,3},{3,2},{4,5},{5,4},{6,7},{7,6},{8,9},{9,8},{10,11... | collective-permute-start | bytes 2359304 | tf_op jit(solution)/shard_map/ppermute | solution.py:292
  143.8 1.0 copy-start.2
  169.6 27.9 %collective-permute-start.4 = (bf16[768,256]{1,0:T(8,128)(2,1)S(1)}, bf16[768,256]{1,0:T(8,128)(2,1)S(1)}, u32[]{:S(2)}, u32[]{:S(2)}) collective-permute-start(bf16[768,256]{1,0:T(8,128)(2,1)S(1)} %bitcast.35), channel_id=1, source_target_pairs={{0,32},{32,64},{64,96},{96,128},{128,160},{160,192},{192,224},{224... | collective-permute-start | bytes 1179656 | tf_op jit(solution)/shard_map/ppermute | solution.py:292
  174.1 23.3 %collective-permute-start.5 = (bf16[768,256]{1,0:T(8,128)(2,1)S(1)}, bf16[768,256]{1,0:T(8,128)(2,1)}, u32[]{:S(2)}, u32[]{:S(2)}) collective-permute-start(bf16[768,256]{1,0:T(8,128)(2,1)S(1)} %bitcast.36), channel_id=1, source_target_pairs={{0,480},{32,0},{64,32},{96,64},{128,96},{160,128},{192,160},{224,1... | collective-permute-start | bytes 1179656 | tf_op jit(solution)/shard_map/ppermute | solution.py:292
  176.9 11.3 %collective-permute-start.6 = (bf16[384,256]{1,0:T(8,128)(2,1)}, bf16[384,256]{1,0:T(8,128)(2,1)S(1)}, u32[]{:S(2)}, u32[]{:S(2)}) collective-permute-start(bf16[384,256]{1,0:T(8,128)(2,1)} %bitcast.19), channel_id=1, source_target_pairs={{0,64},{32,96},{64,128},{96,160},{128,192},{160,224},{192,256},{22... | collective-permute-start | bytes 589832 | tf_op jit(solution)/shard_map/ppermute | solution.py:292
  183.2 14.2 %collective-permute-start.7 = (bf16[384,256]{1,0:T(8,128)(2,1)}, bf16[384,256]{1,0:T(8,128)(2,1)}, u32[]{:S(2)}, u32[]{:S(2)}) collective-permute-start(bf16[384,256]{1,0:T(8,128)(2,1)} %bitcast.20), channel_id=1, source_target_pairs={{0,448},{32,480},{64,0},{96,32},{128,64},{160,96},{192,128},{224,1... | collective-permute-start | bytes 589832 | tf_op jit(solution)/shard_map/ppermute | solution.py:292
  186.7 17.7 %copy-start = (bf16[256,4096]{1,0:T(8,128)(2,1)S(1)}, bf16[256,4096]{1,0:T(8,128)(2,1)}, u32[]{:S(2)}) copy-start(bf16[256,4096]{1,0:T(8,128)(2,1)} %w_out.1) | copy-start | bytes 6291460
  199.8 4.6 %collective-permute-start.8 = (bf16[96,128]{1,0:T(8,128)(2,1)S(1)}, bf16[96,128]{1,0:T(8,128)(2,1)S(1)}, u32[]{:S(2)}, u32[]{:S(2)}) collective-permute-start(bf16[96,128]{1,0:T(8,128)(2,1)S(1)} %get-tuple-element.12), channel_id=1, source_target_pairs={{0,16},{16,0},{1,17},{17,1},{2,18},{18,2},{3,19},{19,3},{4,20},{20... | collective-permute-start | bytes 73736 | tf_op jit(solution)/shard_map/ppermute | solution.py:292
  204.4 20.9 %copy-start.3 = (bf16[4096,128]{1,0:T(8,128)(2,1)S(1)}, bf16[4096,128]{1,0:T(8,128)(2,1)}, u32[]{:S(2)}) copy-start(bf16[4096,128]{1,0:T(8,128)(2,1)} %copy-done.2) | copy-start | bytes 3145732
  260.0 7.1 %collective-permute-start.9 = (bf16[16,64,128]{2,1,0:T(8,128)(2,1)S(1)}, bf16[16,64,128]{2,1,0:T(8,128)(2,1)S(1)}, u32[]{:S(2)}, u32[]{:S(2)}) collective-permute-start(bf16[16,64,128]{2,1,0:T(8,128)(2,1)S(1)} %all_to_all.45.states), channel_id=1, source_target_pairs={{0,32},{32,0},{1,33},{33,1},{2,34},{34,2},{3,35},{35,3},{4,36},{36... | collective-permute-start | bytes 786440 | tf_op jit(solution)/shard_map/ppermute | solution.py:292
Sparse Core Ops, SparseCore 0:
  16.8 98.6 all-gather.1

commit v2 on v1

--- a/solution.py
+++ b/solution.py
@@ -31,8 +31,9 @@
 SMEM = pl.BlockSpec(memory_space=pltpu.SMEM)
 
 
-def local_call(kernel, out, inputs, scratch=(), scalars=0, flops=10**8, moved=10**6):
-    specs = [SMEM] * scalars + [VMEM] * (len(inputs) - scalars)
+def local_call(kernel, out, inputs, scratch=(), scalars=0, left=0, flops=10**8, moved=10**6):
+    specs = [SMEM] * scalars + [VMEM] * (len(inputs) - scalars - left)
+    specs = specs + [pl.BlockSpec(memory_space=pl.ANY)] * left
     many = isinstance(out, (list, tuple))
     return pl.pallas_call(
         kernel,
@@ -83,46 +84,45 @@
         out[i] = held
 
 
-def embed_kernel(info, own, other, gain, w_in, out, keep):
-    planes = own.shape[0] // 2
-    count, size = keep.shape[1:]
+def embed_kernel(pooled, gain, w_in, out, keep):
+    heads, count, size = keep.shape
     each = count // 2
     half = each // 2
     spare = size - MAIN
-    group = own.shape[1] - half
+    group = pooled.shape[1] - half
     square = jnp.zeros((count, 1), F32)
-    for side, source in ((0, own), (1, other)):
-        for p in range(planes):
-            two = [source[y * planes + p].astype(F32) for y in range(2)]
-            main = [v[0:half, at : at + MAIN] for v in two for at in (0, MAIN)]
-            main = jnp.concatenate(main, axis=0)
-            rest = [
-                v[half:, spare * g : spare * (g + 1)] for v in two for g in range(each // group)
-            ]
-            rest = jnp.concatenate(rest, axis=0)
-            keep[side * planes + p, :, 0:MAIN] = main
-            keep[side * planes + p, :, MAIN:size] = rest
-            square = square + jnp.sum(main * main, axis=1, keepdims=True)
-            square = square + jnp.sum(rest * rest, axis=1, keepdims=True)
-    scale = lax.rsqrt(square / (2 * planes * size) + EPSILON)
+    for h in range(heads):
+        two = [pooled[y * heads + h].astype(F32) for y in range(2)]
+        main = [v[0:half, at : at + MAIN] for v in two for at in (0, MAIN)]
+        main = jnp.concatenate(main, axis=0)
+        rest = [v[half:, spare * g : spare * (g + 1)] for v in two for g in range(each // group)]
+        rest = jnp.concatenate(rest, axis=0)
+        keep[h, :, 0:MAIN] = main
+        keep[h, :, MAIN:size] = rest
+        square = square + jnp.sum(main * main, axis=1, keepdims=True)
+        square = square + jnp.sum(rest * rest, axis=1, keepdims=True)
+    scale = lax.rsqrt(square / (heads * size) + EPSILON)
     total = jnp.zeros(out.shape[1:], F32)
-    for side in range(2):
-        core = info[0] if side == 0 else 1 - info[0]
-        for p in range(planes):
-            h = 2 * p + core
-            normed = keep[side * planes + p] * scale * gain[pl.ds(h, 1), :]
-            at = pl.multiple_of(h * size, 16)
-            total = total + matmul(normed.astype(BF), w_in[pl.ds(at, size), :])
+    for h in range(heads):
+        normed = keep[h] * scale * gain[h : h + 1, :]
+        total = total + matmul(normed.astype(BF), w_in[h * size : (h + 1) * size, :])
     held = total.astype(BF)
     for i in range(out.shape[0]):
         out[i] = held
 
 
-def project_kernel(info, own, other, gain, weights, queries, kv, down):
+def project_kernel(info, own, other, gain, weights, queries, kv, down, held, arrived):
     planes = own.shape[0] // 2
     count, width = own.shape[1:]
     size = 2 * width
     columns = 3 * HEAD_SIZE
+
+    def copy(h):
+        at = slice(h * size, (h + 1) * size)
+        return pltpu.make_async_copy(weights.at[at, :], held.at[at, :], arrived.at[h])
+
+    for h in range(2 * planes):
+        copy(h).start()
     square = jnp.zeros((count, width), F32)
     for source in (own, other):
         for b in range(2 * planes):
@@ -131,19 +131,21 @@
     square = jnp.sum(square, axis=1, keepdims=True)
     scale = lax.rsqrt(square / (2 * planes * size) + EPSILON)
     total = jnp.zeros((count, columns), F32)
-    for side, source in ((0, own), (1, other)):
-        core = info[0] if side == 0 else 1 - info[0]
-        for p in range(planes):
+    for p in range(planes):
+        copy(2 * p).wait()
+        copy(2 * p + 1).wait()
+        for side, source in ((0, own), (1, other)):
+            core = info[0] if side == 0 else 1 - info[0]
             h = 2 * p + core
             both = jnp.concatenate([source[p], source[planes + p]], axis=1).astype(F32)
             attn_in = both * scale * gain[pl.ds(h, 1), :]
             at = pl.multiple_of(h * size, size)
-            total = total + matmul(attn_in.astype(BF), weights[pl.ds(at, size), 0:columns])
+            total = total + matmul(attn_in.astype(BF), held[pl.ds(at, size), 0:columns])
     queries[...] = total[:, 0:HEAD_SIZE].astype(BF)
-    held = total[:, HEAD_SIZE:].astype(BF)
+    both = total[:, HEAD_SIZE:].astype(BF)
     for i in range(kv.shape[0]):
-        kv[i] = held
-    down[...] = weights[:, columns:]
+        kv[i] = both
+    down[...] = held[:, columns:]
 
 
 def attend_kernel(info, queries, slots, labels, *rest):
@@ -329,21 +331,32 @@
     rows = byte_states.T
     first = info[1] == 0
 
-    w_in_parts = w_in.reshape(w_in.shape[0], n_yl, -1).transpose(1, 0, 2)
-    w_in_parts = jnp.broadcast_to(w_in_parts[None], (n_z, *w_in_parts.shape))
-    w_in_parts = w_in_parts.reshape(n_z * n_yl, w_in.shape[0], -1)
-    w_in_here = lax.all_to_all(w_in_parts, SEQ, 0, 0, tiled=True)
-    w_in_here = w_in_here.reshape(-1, w_in_parts.shape[2])
-
     halves = [
         jnp.concatenate([w_qkv[:, j, k * HEAD_SIZE : (k + 1) * HEAD_SIZE] for j in range(3)], axis=1)
         for k in range(n_yl)
     ]
     depth = w_qkv.shape[0]
     down_pieces = [w_down[:depth], w_down[depth:]]
-    sent = jnp.concatenate([jnp.where(first, halves[1], halves[0]), *down_pieces], axis=1)
-    came = shift(sent, "yl", 1)
-    kept = jnp.concatenate([jnp.where(first, halves[0], halves[1]), *down_pieces], axis=1)
+    in_width = w_in.shape[1] // n_yl
+    in_halves = [w_in[:, k * in_width : (k + 1) * in_width] for k in range(n_yl)]
+
+    def payload(top, bottom):
+        top = jnp.concatenate([top, *down_pieces], axis=1)
+        fill = jnp.zeros((bottom.shape[0], top.shape[1] - in_width), BF)
+        return jnp.concatenate([top, jnp.concatenate([bottom, fill], axis=1)], axis=0)
+
+    swapped = [jnp.where(first, v[1], v[0]) for v in (halves, in_halves)]
+    stayed = [jnp.where(first, v[0], v[1]) for v in (halves, in_halves)]
+    came = shift(payload(*swapped), "yl", 1)
+    w_in_came = came[depth:, :in_width]
+    w_in_both = [jnp.where(first, stayed[1], w_in_came), jnp.where(first, w_in_came, stayed[1])]
+    w_in_both = jnp.concatenate(w_in_both, axis=0)
+    w_in_here = lax.all_to_all(
+        jnp.broadcast_to(w_in_both[None], (n_z, *w_in_both.shape)), Z, 0, 0, tiled=True
+    )
+    w_in_here = w_in_here.reshape(-1, in_width)
+    kept = jnp.concatenate([stayed[0], *down_pieces], axis=1)
+    came = came[:depth]
     low = jnp.where(first, kept, came)
     high = jnp.where(first, came, kept)
     wide = halves[0].shape[1]
@@ -365,14 +378,14 @@
     pooled = (kept.astype(F32) + came.astype(F32)).astype(BF)
     pooled = lax.all_to_all(pooled, Z, 0, 0, tiled=True)
     pooled = local_call(
-        sum_kernel, jax.ShapeDtypeStruct((n_plane, *pooled.shape[1:]), BF), [pooled]
-    )
+        sum_kernel, jax.ShapeDtypeStruct((2 * n_plane, *pooled.shape[1:]), BF), [pooled]
+    )
+    pooled = lax.all_to_all(pooled, (*PLANE, "c"), 0, 0, tiled=True)
     embed = local_call(
         embed_kernel,
         jax.ShapeDtypeStruct((n_plane, rows_z, w_in_here.shape[1]), BF),
-        [info, *over_plane(pooled), pool_gain.reshape(n_head, cross_size), w_in_here],
+        [pooled, pool_gain.reshape(n_head, cross_size), w_in_here],
         scratch=[pltpu.VMEM((n_head, rows_z, cross_size), F32)],
-        scalars=1,
     )
     own_embed, other_embed = over_plane(embed)
     queries, kv, down_here = local_call(
@@ -383,7 +396,9 @@
             jax.ShapeDtypeStruct((weights.shape[0], LANES), BF),
         ],
         [info, own_embed, other_embed, attn_gain.reshape(n_head, -1), weights],
-        scalars=1,
+        scratch=[pltpu.VMEM(weights.shape, BF), pltpu.SemaphoreType.DMA((n_head,))],
+        scalars=1,
+        left=1,
     )
     labels = slot_patch.reshape(n_z // n_zl, n_zl, rows_z).transpose(1, 0, 2).reshape(n_zl, -1)
     kv = lax.all_to_all(kv, "zh", 0, 0, tiled=True).reshape(-1, kv.shape[2])

time: 283 us -> 291 us (1.028)
  blocking collectives: 125 us -> 97.7 us
  waiting for transfers between devices: 48.5 us -> 68.4 us
  starting transfers between devices: 55.9 us -> 70.1 us
    all_to_all x1 -> x0, blocking collectives: 33.3 us -> none  [layer(): pooled = lax.all_to_all(pooled, Z, 0, 0, tiled=True)]
    all_to_all x2 -> x3, starting transfers between devices: 16.5 us -> 39.4 us  [the longest x1 17.2 us: layer(): pooled = lax.all_to_all(pooled, Z, 0, 0, tiled=True)]
    all_to_all x2 -> x3, waiting for transfers between devices: 27.3 us -> 48.8 us  [the longest x1 18.9 us: layer(): lax.all_to_all(jnp.broadcast_to(w_in_both[None], (n_z, *w_in_both.shape))...]
    ppermute x10 -> x9, starting transfers between devices: 39.3 us -> 30.7 us  [shift(): return lax.ppermute(x, axis, [(i, (i + by) % n) for i in range(n)])]
    ppermute x10 -> x9, waiting for transfers between devices: 21.3 us -> 19.6 us  [shift(): return lax.ppermute(x, axis, [(i, (i + by) % n) for i in range(n)])]
  transfers between devices with their start and end apart: 13 -> 13, of which waited for: 9 -> 10; matrix products, arithmetic and copies ran while one was open for 2% -> 2% of each run, Pallas kernels for 4% -> 4%
where the time goes in v2:
time: 291 us; the launch traced here: 288 us
  blocking collectives  97.7 us (34%)
  starting transfers between devices  70.1 us (24%)
  waiting for transfers between devices  68.4 us (24%)
  Pallas kernels  24.8 us (9%)
  between operations  15.1 us (5%)
  local copies, waits for them, and re-layouts  9.16 us (3%)
    ppermute x9, starting transfers between devices, shift(): return lax.ppermute(x, axis, [(i, (i + by) % n) for i in range(n)])  30.7 us
    all_to_all x1, blocking collectives, layer(): kv = lax.all_to_all(kv, 'zh', 0, 0, tiled=True).reshape(-1, kv.shape[2])  26.3 us
    pallas_call x11, Pallas kernels, local_call(): pl.pallas_call(kernel, out_shape=out, in_specs=specs, out_specs=[VMEM] *...  24.8 us
    all_to_all x1, blocking collectives, layer(): states = lax.all_to_all(states, SKIP, 0, 0, tiled=True)  22.3 us
    all_to_all x1, blocking collectives, layer(): arrived = lax.all_to_all(out_part, HEAD, 0, 0, tiled=True)  19.9 us
    ppermute x9, waiting for transfers between devices, shift(): return lax.ppermute(x, axis, [(i, (i + by) % n) for i in range(n)])  19.6 us
    all_to_all x1, waiting for transfers between devices, layer(): lax.all_to_all(jnp.broadcast_to(w_in_both[None], (n_z, *w_in_both.shape))...  18.9 us
    all_to_all x1, waiting for transfers between devices, layer(): pooled = lax.all_to_all(pooled, Z, 0, 0, tiled=True)  18.2 us
  transfers between devices with their start and end apart: 13, of which 10 were waited for; matrix products, arithmetic and copies ran while one was open for 2% of the time, Pallas kernels for 4%

profile of v2, /device:TPU:1, one launch (start us, length us, event | category | flops | bytes accessed | tf_op | source)
XLA Modules:
  0.0 287.9 jit_solution(7431531805016674493)
XLA Ops:
  10.0 4.0 %collective-permute-start.1 = (bf16[168,464]{1,0:T(8,128)(2,1)S(1)}, bf16[168,464]{1,0:T(8,128)(2,1)S(1)}, u32[]{:S(2)}, u32[]{:S(2)}) collective-permute-start(bf16[168,464]{1,0:T(8,128)(2,1)S(1)} %fusion.1), channel_id=1, source_target_pairs={{0,16},{16,0},{1,17},{17,1},{2,18},{18,2},{3,19},{19,3},{4,20},{20... | collective-permute-start | bytes 467720 | tf_op jit(solution)/shard_map/ppermute | solution.py:294
  14.1 2.7 collective-permute-done.1
  22.1 3.4 %collective-permute-start = (bf16[16,64,128]{2,1,0:T(8,128)(2,1)S(1)}, bf16[16,64,128]{2,1,0:T(8,128)(2,1)S(1)}, u32[]{:S(2)}, u32[]{:S(2)}) collective-permute-start(bf16[16,64,128]{2,1,0:T(8,128)(2,1)S(1)} %shard_map.105), channel_id=1, source_target_pairs={{0,16},{16,0},{1,17},{17,1},{2,18},{18,2},{3,19},{19,3},{4,20},{20... | collective-permute-start | bytes 786440 | tf_op jit(solution)/shard_map/ppermute | solution.py:294
  30.0 17.2 %all-to-all-start = ((bf16[16,64,128]{2,1,0:T(8,128)(2,1)}), bf16[16,64,128]{2,1,0:T(8,128)(2,1)S(1)}, u32[]{:S(2)}, u32[]{:S(2)}) async-start(bf16[16,64,128]{2,1,0:T(8,128)(2,1)} %add_convert_fusion), calls=%async_computation | async-start | bytes 524288 | tf_op jit(solution)/shard_map/all_to_all | solution.py:379
  47.2 18.2 %all-to-all-done.arrived = bf16[16,64,128]{2,1,0:T(8,128)(2,1)S(1)} async-done(((bf16[16,64,128]{2,1,0:T(8,128)(2,1)}), bf16[16,64,128]{2,1,0:T(8,128)(2,1)S(1)}, u32[]{:S(2)}, u32[]{:S(2)}) %all-to-all-start) | async-done | bytes 262176 | tf_op jit(solution)/shard_map/all_to_all | solution.py:379
  66.2 8.1 %all-to-all-start.2 = ((bf16[16,80,128]{2,1,0:T(8,128)(2,1)}), bf16[16,80,128]{2,1,0:T(8,128)(2,1)S(1)}, u32[]{:S(2)}, u32[]{:S(2)}) async-start(bf16[16,80,128]{2,1,0:T(8,128)(2,1)} %broadcast_in_dim.19), calls=%async_computation.2 | async-start | bytes 655360 | tf_op jit(solution)/shard_map/all_to_all | solution.py:354
  75.2 18.9 %all-to-all-done.2 = bf16[16,80,128]{2,1,0:T(8,128)(2,1)S(1)} async-done(((bf16[16,80,128]{2,1,0:T(8,128)(2,1)}), bf16[16,80,128]{2,1,0:T(8,128)(2,1)S(1)}, u32[]{:S(2)}, u32[]{:S(2)}) %all-to-all-start.2) | async-done | bytes 327712 | tf_op jit(solution)/shard_map/all_to_all | solution.py:354
  94.1 14.2 %all-to-all-start.1 = ((bf16[32,64,128]{2,1,0:T(8,128)(2,1)}), bf16[32,64,128]{2,1,0:T(8,128)(2,1)S(1)}, u32[]{:S(2)}, u32[]{:S(2)}) async-start(bf16[32,64,128]{2,1,0:T(8,128)(2,1)} %shard_map.106), calls=%async_computation.1 | async-start | bytes 1048576 | tf_op jit(solution)/shard_map/all_to_all | solution.py:383
  108.3 11.7 %all-to-all-done.1.pooled = bf16[32,64,128]{2,1,0:T(8,128)(2,1)S(1)} async-done(((bf16[32,64,128]{2,1,0:T(8,128)(2,1)}), bf16[32,64,128]{2,1,0:T(8,128)(2,1)S(1)}, u32[]{:S(2)}, u32[]{:S(2)}) %all-to-all-start.1) | async-done | bytes 524320 | tf_op jit(solution)/shard_map/all_to_all | solution.py:383
  120.0 2.7 shard_map.107
  122.7 17.3 %all_to_all.40.own.embed = bf16[16,192,128]{2,1,0:T(8,128)(2,1)S(1)} all-to-all(bf16[16,192,128]{2,1,0:T(8,128)(2,1)S(1)} %shard_map.107), channel_id=1, replica_groups=mesh['zh'=4,'zm'=2,'zp'=2,'yl'=2,'yh'=2,'x'=4,'c'=2] {'yl','yh','x'}, dimensions={0} | all-to-all | bytes 1572864 | tf_op jit(solution)/shard_map/all_to_all | solution.py:298
  140.1 2.9 collective-permute-start.2
  145.0 4.5 %shard_map.108 = (bf16[192,128]{1,0:T(8,128)(2,1)S(1)}, bf16[4,192,256]{2,1,0:T(8,128)(2,1)S(1)}, bf16[4096,128]{1,0:T(8,128)(2,1)S(1)}) custom-call(s32[7]{0:T(128)S(1)} %stack.28.info, bf16[16,192,128]{2,1,0:T(8,128)(2,1)S(1)} %all_to_all.40.own.embed, bf16[16,192,128]{2,1,0:T(8,128)(2,1)} %collective-permute-done.2.other, f32[16,256]{1,0:T(8,128)S(1)} %reshape.39.gain, ...), custom_call_target="tpu_custom_call" | custom-call | flops 100000000 | bytes 1000000 | tf_op jit(solution)/shard_map/pallas_call | solution.py:38
  150.4 26.3 %all_to_all.41 = bf16[4,192,256]{2,1,0:T(8,128)(2,1)S(1)} all-to-all(bf16[4,192,256]{2,1,0:T(8,128)(2,1)S(1)} %get-tuple-element.10), channel_id=1, replica_groups=mesh['zh'=4,'zm'=2,'zp'=2,'yl'=2,'yh'=2,'x'=4,'c'=2] {'zh'}, dimensions={0} | all-to-all | bytes 786432 | tf_op jit(solution)/shard_map/all_to_all | solution.py:404
  176.8 3.1 %collective-permute-start.3 = (bf16[768,256]{1,0:T(8,128)(2,1)S(1)}, bf16[768,256]{1,0:T(8,128)(2,1)S(1)}, u32[]{:S(2)}, u32[]{:S(2)}) collective-permute-start(bf16[768,256]{1,0:T(8,128)(2,1)S(1)} %bitcast.33), channel_id=1, source_target_pairs={{0,32},{32,64},{64,96},{96,128},{128,160},{160,192},{192,224},{224... | collective-permute-start | bytes 1179656 | tf_op jit(solution)/shard_map/ppermute | solution.py:294
  179.9 6.0 %collective-permute-start.4 = (bf16[768,256]{1,0:T(8,128)(2,1)S(1)}, bf16[768,256]{1,0:T(8,128)(2,1)}, u32[]{:S(2)}, u32[]{:S(2)}) collective-permute-start(bf16[768,256]{1,0:T(8,128)(2,1)S(1)} %bitcast.34), channel_id=1, source_target_pairs={{0,480},{32,0},{64,32},{96,64},{128,96},{160,128},{192,160},{224,1... | collective-permute-start | bytes 1179656 | tf_op jit(solution)/shard_map/ppermute | solution.py:294
  186.6 4.7 %collective-permute-start.5 = (bf16[384,256]{1,0:T(8,128)(2,1)}, bf16[384,256]{1,0:T(8,128)(2,1)S(1)}, u32[]{:S(2)}, u32[]{:S(2)}) collective-permute-start(bf16[384,256]{1,0:T(8,128)(2,1)} %bitcast.17), channel_id=1, source_target_pairs={{0,64},{32,96},{64,128},{96,160},{128,192},{160,224},{192,256},{22... | collective-permute-start | bytes 589832 | tf_op jit(solution)/shard_map/ppermute | solution.py:294
  191.3 2.7 collective-permute-start.6
  198.2 7.3 %collective-permute-done.6.rest_4_ = bf16[384,256]{1,0:T(8,128)(2,1)} collective-permute-done((bf16[384,256]{1,0:T(8,128)(2,1)}, bf16[384,256]{1,0:T(8,128)(2,1)}, u32[]{:S(2)}, u32[]{:S(2)}) %collective-permute-start.6) | collective-permute-done | bytes 196640 | tf_op jit(solution)/shard_map/ppermute | solution.py:294
  209.8 2.6 collective-permute-done.7.came
  213.5 19.9 %all_to_all.42.arrived = bf16[16,96,256]{2,1,0:T(8,128)(2,1)S(1)} all-to-all(bf16[16,96,256]{2,1,0:T(8,128)(2,1)S(1)} %shard_map.110), channel_id=1, replica_groups=mesh['zh'=4,'zm'=2,'zp'=2,'yl'=2,'yh'=2,'x'=4,'c'=2] {'yh','x','c'}, dimensions={0} | all-to-all | bytes 1572864 | tf_op jit(solution)/shard_map/all_to_all | solution.py:424
  235.0 11.9 %all_to_all.43.arrived = bf16[16,64,128]{2,1,0:T(8,128)(2,1)S(1)} all-to-all(bf16[16,64,128]{2,1,0:T(8,128)(2,1)S(1)} %get-tuple-element.15), channel_id=1, replica_groups=mesh['zh'=4,'zm'=2,'zp'=2,'yl'=2,'yh'=2,'x'=4,'c'=2] {'yh','x','c'}, dimensions={0} | all-to-all | bytes 524288 | tf_op jit(solution)/shard_map/all_to_all | solution.py:434
  247.0 22.3 %all_to_all.44.states = bf16[16,64,128]{2,1,0:T(8,128)(2,1)S(1)} all-to-all(bf16[16,64,128]{2,1,0:T(8,128)(2,1)S(1)} %shard_map.112), channel_id=1, replica_groups=mesh['zh'=4,'zm'=2,'zp'=2,'yl'=2,'yh'=2,'x'=4,'c'=2] {'zh','zm','yl'}, dimensions={0} | all-to-all | bytes 524288 | tf_op jit(solution)/shard_map/all_to_all | solution.py:439
  276.4 4.7 %shard_map.114 = bf16[80,768]{1,0:T(8,128)(2,1)} custom-call(s32[7]{0:T(128)S(1)} %stack.28.info, s32[2,2,768]{2,1,0:T(2,128)S(1)} %reshape.44.labels_main, s32[2,6,256]{2,1,0:T(8,128)S(1)} %reshape.46.labels_rest, s32[1,768]{1,0:T(1,128)S(1)} %broadcast_in_dim.18.ids, bf16[80,768]{1,0:T(8,128)(2,1)S(1)} %bitcast.39, ...), custom_call_target="tpu_custom_call" | custom-call | flops 100000000 | bytes 1000000 | tf_op jit(solution)/shard_map/pallas_call | solution.py:38
  (73 shorter events, 35.7 us)
Async XLA Ops:
  7.2 10.7 %copy-start.8 = (s32[768]{0:T(1024)S(1)}, s32[768]{0:T(1024)}, u32[]{:S(2)}) copy-start(s32[768]{0:T(1024)} %param.10) | copy-start | bytes 9220
  7.2 11.3 %copy-start.4 = (s32[3072]{0:T(1024)S(1)}, s32[3072]{0:T(1024)}, u32[]{:S(2)}) copy-start(s32[3072]{0:T(1024)} %param.11) | copy-start | bytes 36868
  7.2 137.8 %all-gather.2.cloned.1.call-start = ((), (), s32[]{:S(2)}) async-start(), calls=%async_computation.8 | async-start | bytes 4456448 | tf_op jit(solution)/shard_map/all_gather | solution.py:369
  9.9 9.9 %copy-start.1 = (bf16[768,80]{0,1:T(8,128)(2,1)S(1)}, bf16[768,80]{0,1:T(8,128)(2,1)}, u32[]{:S(2)}) copy-start(bf16[768,80]{0,1:T(8,128)(2,1)} %param.9) | copy-start | bytes 368644
  10.0 6.8 %collective-permute-start.1 = (bf16[168,464]{1,0:T(8,128)(2,1)S(1)}, bf16[168,464]{1,0:T(8,128)(2,1)S(1)}, u32[]{:S(2)}, u32[]{:S(2)}) collective-permute-start(bf16[168,464]{1,0:T(8,128)(2,1)S(1)} %fusion.1), channel_id=1, source_target_pairs={{0,16},{16,0},{1,17},{17,1},{2,18},{18,2},{3,19},{19,3},{4,20},{20... | collective-permute-start | bytes 467720 | tf_op jit(solution)/shard_map/ppermute | solution.py:294
  22.1 25.1 %copy-start.5 = (bf16[40,256]{1,0:T(8,128)(2,1)S(1)}, bf16[40,256]{1,0:T(8,128)(2,1)}, u32[]{:S(2)}) copy-start(bf16[40,256]{1,0:T(8,128)(2,1)} %param.13) | copy-start | bytes 61444
  22.1 7.1 %collective-permute-start = (bf16[16,64,128]{2,1,0:T(8,128)(2,1)S(1)}, bf16[16,64,128]{2,1,0:T(8,128)(2,1)S(1)}, u32[]{:S(2)}, u32[]{:S(2)}) collective-permute-start(bf16[16,64,128]{2,1,0:T(8,128)(2,1)S(1)} %shard_map.105), channel_id=1, source_target_pairs={{0,16},{16,0},{1,17},{17,1},{2,18},{18,2},{3,19},{19,3},{4,20},{20... | collective-permute-start | bytes 786440 | tf_op jit(solution)/shard_map/ppermute | solution.py:294
  27.7 80.5 %copy-start.7 = (f32[1280]{0:T(1024)S(1)}, f32[1280]{0:T(1024)}, u32[]{:S(2)}) copy-start(f32[1280]{0:T(1024)} %param.12) | copy-start | bytes 15364
  30.0 35.4 %all-to-all-start = ((bf16[16,64,128]{2,1,0:T(8,128)(2,1)}), bf16[16,64,128]{2,1,0:T(8,128)(2,1)S(1)}, u32[]{:S(2)}, u32[]{:S(2)}) async-start(bf16[16,64,128]{2,1,0:T(8,128)(2,1)} %add_convert_fusion), calls=%async_computation | async-start | bytes 524288 | tf_op jit(solution)/shard_map/all_to_all | solution.py:379
  66.2 27.9 %all-to-all-start.2 = ((bf16[16,80,128]{2,1,0:T(8,128)(2,1)}), bf16[16,80,128]{2,1,0:T(8,128)(2,1)S(1)}, u32[]{:S(2)}, u32[]{:S(2)}) async-start(bf16[16,80,128]{2,1,0:T(8,128)(2,1)} %broadcast_in_dim.19), calls=%async_computation.2 | async-start | bytes 655360 | tf_op jit(solution)/shard_map/all_to_all | solution.py:354
  75.2 67.8 %copy-start.6 = (f32[4096]{0:T(1024)S(1)}, f32[4096]{0:T(1024)}, u32[]{:S(2)}) copy-start(f32[4096]{0:T(1024)} %param.14) | copy-start | bytes 49156
  94.1 25.9 %all-to-all-start.1 = ((bf16[32,64,128]{2,1,0:T(8,128)(2,1)}), bf16[32,64,128]{2,1,0:T(8,128)(2,1)S(1)}, u32[]{:S(2)}, u32[]{:S(2)}) async-start(bf16[32,64,128]{2,1,0:T(8,128)(2,1)} %shard_map.106), calls=%async_computation.1 | async-start | bytes 1048576 | tf_op jit(solution)/shard_map/all_to_all | solution.py:383
  140.1 4.9 %collective-permute-start.2 = (bf16[16,192,128]{2,1,0:T(8,128)(2,1)S(1)}, bf16[16,192,128]{2,1,0:T(8,128)(2,1)}, u32[]{:S(2)}, u32[]{:S(2)}) collective-permute-start(bf16[16,192,128]{2,1,0:T(8,128)(2,1)S(1)} %all_to_all.40.own.embed), channel_id=1, source_target_pairs={{0,1},{1,0},{2,3},{3,2},{4,5},{5,4},{6,7},{7,6},{8,9},{9,8},{10,11... | collective-permute-start | bytes 2359304 | tf_op jit(solution)/shard_map/ppermute | solution.py:294
  149.4 1.0 copy-start.2
  176.8 28.7 %collective-permute-start.3 = (bf16[768,256]{1,0:T(8,128)(2,1)S(1)}, bf16[768,256]{1,0:T(8,128)(2,1)S(1)}, u32[]{:S(2)}, u32[]{:S(2)}) collective-permute-start(bf16[768,256]{1,0:T(8,128)(2,1)S(1)} %bitcast.33), channel_id=1, source_target_pairs={{0,32},{32,64},{64,96},{96,128},{128,160},{160,192},{192,224},{224... | collective-permute-start | bytes 1179656 | tf_op jit(solution)/shard_map/ppermute | solution.py:294
  179.9 25.6 %collective-permute-start.4 = (bf16[768,256]{1,0:T(8,128)(2,1)S(1)}, bf16[768,256]{1,0:T(8,128)(2,1)}, u32[]{:S(2)}, u32[]{:S(2)}) collective-permute-start(bf16[768,256]{1,0:T(8,128)(2,1)S(1)} %bitcast.34), channel_id=1, source_target_pairs={{0,480},{32,0},{64,32},{96,64},{128,96},{160,128},{192,160},{224,1... | collective-permute-start | bytes 1179656 | tf_op jit(solution)/shard_map/ppermute | solution.py:294
  186.6 11.6 %collective-permute-start.5 = (bf16[384,256]{1,0:T(8,128)(2,1)}, bf16[384,256]{1,0:T(8,128)(2,1)S(1)}, u32[]{:S(2)}, u32[]{:S(2)}) collective-permute-start(bf16[384,256]{1,0:T(8,128)(2,1)} %bitcast.17), channel_id=1, source_target_pairs={{0,64},{32,96},{64,128},{96,160},{128,192},{160,224},{192,256},{22... | collective-permute-start | bytes 589832 | tf_op jit(solution)/shard_map/ppermute | solution.py:294
  191.3 14.2 %collective-permute-start.6 = (bf16[384,256]{1,0:T(8,128)(2,1)}, bf16[384,256]{1,0:T(8,128)(2,1)}, u32[]{:S(2)}, u32[]{:S(2)}) collective-permute-start(bf16[384,256]{1,0:T(8,128)(2,1)} %bitcast.18), channel_id=1, source_target_pairs={{0,448},{32,480},{64,0},{96,32},{128,64},{160,96},{192,128},{224,1... | collective-permute-start | bytes 589832 | tf_op jit(solution)/shard_map/ppermute | solution.py:294
  196.8 15.6 %copy-start = (bf16[256,4096]{1,0:T(8,128)(2,1)S(1)}, bf16[256,4096]{1,0:T(8,128)(2,1)}, u32[]{:S(2)}) copy-start(bf16[256,4096]{1,0:T(8,128)(2,1)} %w_out.1) | copy-start | bytes 6291460
  207.8 4.6 %collective-permute-start.7 = (bf16[96,128]{1,0:T(8,128)(2,1)S(1)}, bf16[96,128]{1,0:T(8,128)(2,1)S(1)}, u32[]{:S(2)}, u32[]{:S(2)}) collective-permute-start(bf16[96,128]{1,0:T(8,128)(2,1)S(1)} %get-tuple-element.12), channel_id=1, source_target_pairs={{0,16},{16,0},{1,17},{17,1},{2,18},{18,2},{3,19},{19,3},{4,20},{20... | collective-permute-start | bytes 73736 | tf_op jit(solution)/shard_map/ppermute | solution.py:294
  212.4 21.0 %copy-start.3 = (bf16[4096,128]{1,0:T(8,128)(2,1)S(1)}, bf16[4096,128]{1,0:T(8,128)(2,1)}, u32[]{:S(2)}) copy-start(bf16[4096,128]{1,0:T(8,128)(2,1)} %copy-done.2) | copy-start | bytes 3145732
  269.3 7.1 %collective-permute-start.8 = (bf16[16,64,128]{2,1,0:T(8,128)(2,1)S(1)}, bf16[16,64,128]{2,1,0:T(8,128)(2,1)S(1)}, u32[]{:S(2)}, u32[]{:S(2)}) collective-permute-start(bf16[16,64,128]{2,1,0:T(8,128)(2,1)S(1)} %all_to_all.44.states), channel_id=1, source_target_pairs={{0,32},{32,0},{1,33},{33,1},{2,34},{34,2},{3,35},{35,3},{4,36},{36... | collective-permute-start | bytes 786440 | tf_op jit(solution)/shard_map/ppermute | solution.py:294
Sparse Core Ops, SparseCore 0:
  17.9 99.7 all-gather.1

commit v3 on v2

--- a/solution.py
+++ b/solution.py
@@ -31,13 +31,13 @@
 SMEM = pl.BlockSpec(memory_space=pltpu.SMEM)
 
 
-def local_call(kernel, out, inputs, scratch=(), scalars=0, left=0, flops=10**8, moved=10**6):
-    specs = [SMEM] * scalars + [VMEM] * (len(inputs) - scalars - left)
-    specs = specs + [pl.BlockSpec(memory_space=pl.ANY)] * left
+def local_call(kernel, out, inputs, scratch=(), scalars=0, last=(), flops=10**8, moved=10**6):
+    specs = [SMEM] * scalars + [VMEM] * (len(inputs) - scalars - len(last)) + list(last)
     many = isinstance(out, (list, tuple))
     return pl.pallas_call(
         kernel,
         out_shape=out,
+        grid=(1,) if last else (),
         in_specs=specs,
         out_specs=[VMEM] * len(out) if many else VMEM,
         scratch_shapes=list(scratch),
@@ -52,6 +52,16 @@
 
 def matmul_t(a, b):
     return lax.dot_general(a, b, (((1,), (1,)), ((), ())), preferred_element_type=F32)
+
+
+def split_kernel(w_in, out):
+    width = out.shape[2]
+    for i in range(out.shape[0]):
+        out[i] = w_in[:, (i % 2) * width : (i % 2 + 1) * width]
+
+
+def take_kernel(weights, out):
+    out[...] = weights[...]
 
 
 def pool_kernel(flip, info, slots, ids, rows, out):
@@ -111,18 +121,11 @@
         out[i] = held
 
 
-def project_kernel(info, own, other, gain, weights, queries, kv, down, held, arrived):
+def project_kernel(info, own, other, gain, weights, queries, kv):
     planes = own.shape[0] // 2
     count, width = own.shape[1:]
     size = 2 * width
     columns = 3 * HEAD_SIZE
-
-    def copy(h):
-        at = slice(h * size, (h + 1) * size)
-        return pltpu.make_async_copy(weights.at[at, :], held.at[at, :], arrived.at[h])
-
-    for h in range(2 * planes):
-        copy(h).start()
     square = jnp.zeros((count, width), F32)
     for source in (own, other):
         for b in range(2 * planes):
@@ -131,25 +134,22 @@
     square = jnp.sum(square, axis=1, keepdims=True)
     scale = lax.rsqrt(square / (2 * planes * size) + EPSILON)
     total = jnp.zeros((count, columns), F32)
-    for p in range(planes):
-        copy(2 * p).wait()
-        copy(2 * p + 1).wait()
-        for side, source in ((0, own), (1, other)):
-            core = info[0] if side == 0 else 1 - info[0]
+    for side, source in ((0, own), (1, other)):
+        core = info[0] if side == 0 else 1 - info[0]
+        for p in range(planes):
             h = 2 * p + core
             both = jnp.concatenate([source[p], source[planes + p]], axis=1).astype(F32)
             attn_in = both * scale * gain[pl.ds(h, 1), :]
             at = pl.multiple_of(h * size, size)
-            total = total + matmul(attn_in.astype(BF), held[pl.ds(at, size), 0:columns])
+            total = total + matmul(attn_in.astype(BF), weights[pl.ds(at, size), :])
     queries[...] = total[:, 0:HEAD_SIZE].astype(BF)
-    both = total[:, HEAD_SIZE:].astype(BF)
+    held = total[:, HEAD_SIZE:].astype(BF)
     for i in range(kv.shape[0]):
-        kv[i] = both
-    down[...] = held[:, columns:]
+        kv[i] = held
 
 
 def attend_kernel(info, queries, slots, labels, *rest):
-    pieces, keep, send, scores, held = rest[:-4], rest[-4], rest[-3], rest[-2], rest[-1]
+    pieces, out, scores = rest[:-2], rest[-2], rest[-1]
     query = queries[...]
     own = pl.multiple_of(info[4] * query.shape[0], query.shape[0])
     mine = slots[pl.ds(own, query.shape[0]), :]
@@ -173,25 +173,20 @@
         total = total + jnp.sum(weights, axis=1, keepdims=True)
         mixed = mixed + matmul(weights.astype(BF), piece[:, HEAD_SIZE:])
         start += size
-    held[...] = mixed / total
-    count = keep.shape[0]
-    at = pl.multiple_of(info[1] * count, count)
-    keep[...] = held[pl.ds(at, count), :].astype(BF)
-    at = pl.multiple_of((1 - info[1]) * count, count)
-    send[...] = held[pl.ds(at, count), :].astype(BF)
-
-
-def out_kernel(info, kept, came, w_out, out):
-    mine = kept[...]
-    theirs = came[...]
-    width = out.shape[2]
+    out[...] = (mixed / total).astype(BF)
+
+
+def out_kernel(flip, info, attended, w_out, out):
+    count, width = out.shape[1:]
+    planes = out.shape[0] // 2
+    mine = attended[...]
     at = pl.multiple_of(info[1] * HEAD_SIZE, HEAD_SIZE)
-    other = pl.multiple_of((1 - info[1]) * HEAD_SIZE, HEAD_SIZE)
-    for h in range(out.shape[0]):
-        cols = slice(h * width, (h + 1) * width)
-        part = matmul(mine, w_out[pl.ds(at, HEAD_SIZE), cols])
-        part = part + matmul(theirs, w_out[pl.ds(other, HEAD_SIZE), cols])
-        out[h] = part.astype(BF)
+    core = 1 - info[0] if flip else info[0]
+    for p in range(planes):
+        cols = pl.multiple_of((2 * p + core) * width, width)
+        part = matmul(mine, w_out[pl.ds(at, HEAD_SIZE), pl.ds(cols, width)]).astype(BF)
+        out[p] = part[0:count]
+        out[planes + p] = part[count:]
 
 
 def down_kernel(info, arrived, embed, w_down, stream, out):
@@ -331,32 +326,23 @@
     rows = byte_states.T
     first = info[1] == 0
 
+    w_in_parts = local_call(
+        split_kernel,
+        jax.ShapeDtypeStruct((n_z * n_yl, w_in.shape[0], w_in.shape[1] // n_yl), BF),
+        [w_in],
+    )
+    w_in_here = lax.all_to_all(w_in_parts, SEQ, 0, 0, tiled=True)
+    w_in_here = w_in_here.reshape(-1, w_in_parts.shape[2])
+
     halves = [
         jnp.concatenate([w_qkv[:, j, k * HEAD_SIZE : (k + 1) * HEAD_SIZE] for j in range(3)], axis=1)
         for k in range(n_yl)
     ]
     depth = w_qkv.shape[0]
     down_pieces = [w_down[:depth], w_down[depth:]]
-    in_width = w_in.shape[1] // n_yl
-    in_halves = [w_in[:, k * in_width : (k + 1) * in_width] for k in range(n_yl)]
-
-    def payload(top, bottom):
-        top = jnp.concatenate([top, *down_pieces], axis=1)
-        fill = jnp.zeros((bottom.shape[0], top.shape[1] - in_width), BF)
-        return jnp.concatenate([top, jnp.concatenate([bottom, fill], axis=1)], axis=0)
-
-    swapped = [jnp.where(first, v[1], v[0]) for v in (halves, in_halves)]
-    stayed = [jnp.where(first, v[0], v[1]) for v in (halves, in_halves)]
-    came = shift(payload(*swapped), "yl", 1)
-    w_in_came = came[depth:, :in_width]
-    w_in_both = [jnp.where(first, stayed[1], w_in_came), jnp.where(first, w_in_came, stayed[1])]
-    w_in_both = jnp.concatenate(w_in_both, axis=0)
-    w_in_here = lax.all_to_all(
-        jnp.broadcast_to(w_in_both[None], (n_z, *w_in_both.shape)), Z, 0, 0, tiled=True
-    )
-    w_in_here = w_in_here.reshape(-1, in_width)
-    kept = jnp.concatenate([stayed[0], *down_pieces], axis=1)
-    came = came[:depth]
+    sent = jnp.concatenate([jnp.where(first, halves[1], halves[0]), *down_pieces], axis=1)
+    came = shift(sent, "yl", 1)
+    kept = jnp.concatenate([jnp.where(first, halves[0], halves[1]), *down_pieces], axis=1)
     low = jnp.where(first, kept, came)
     high = jnp.where(first, came, kept)
     wide = halves[0].shape[1]
@@ -388,40 +374,39 @@
         scratch=[pltpu.VMEM((n_head, rows_z, cross_size), F32)],
     )
     own_embed, other_embed = over_plane(embed)
-    queries, kv, down_here = local_call(
+    queries, kv = local_call(
         project_kernel,
         [
             jax.ShapeDtypeStruct((rows_z, HEAD_SIZE), BF),
             jax.ShapeDtypeStruct((n_z // n_zl, rows_z, 2 * HEAD_SIZE), BF),
-            jax.ShapeDtypeStruct((weights.shape[0], LANES), BF),
         ],
         [info, own_embed, other_embed, attn_gain.reshape(n_head, -1), weights],
-        scratch=[pltpu.VMEM(weights.shape, BF), pltpu.SemaphoreType.DMA((n_head,))],
         scalars=1,
-        left=1,
+        last=[pl.BlockSpec((weights.shape[0], wide), lambda i: (0, 0))],
+    )
+    down_here = local_call(
+        take_kernel,
+        jax.ShapeDtypeStruct((weights.shape[0], LANES), BF),
+        [weights],
+        last=[pl.BlockSpec((weights.shape[0], LANES), lambda i: (0, wide // LANES))],
     )
     labels = slot_patch.reshape(n_z // n_zl, n_zl, rows_z).transpose(1, 0, 2).reshape(n_zl, -1)
     kv = lax.all_to_all(kv, "zh", 0, 0, tiled=True).reshape(-1, kv.shape[2])
-    kept, sent = local_call(
+    attended = local_call(
         attend_kernel,
-        [jax.ShapeDtypeStruct((rows_each, HEAD_SIZE), BF)] * 2,
-        [
-            info,
-            queries,
-            slots,
-            labels,
-            *over_z(kv),
-        ],
-        scratch=[pltpu.VMEM((rows_z, patches), F32), pltpu.VMEM((rows_z, HEAD_SIZE), F32)],
+        jax.ShapeDtypeStruct((rows_z, HEAD_SIZE), BF),
+        [info, queries, slots, labels, *over_z(kv)],
+        scratch=[pltpu.VMEM((rows_z, patches), F32)],
         scalars=1,
     )
-    out_part = local_call(
-        out_kernel,
-        jax.ShapeDtypeStruct((n_head, rows_each, w_out.shape[1] // n_head), BF),
-        [info, kept, shift(sent, "yl", 1), w_out],
-        scalars=1,
-    )
-    arrived = lax.all_to_all(out_part, HEAD, 0, 0, tiled=True)
+    out_shape = jax.ShapeDtypeStruct((n_plane, rows_each, w_out.shape[1] // n_head), BF)
+    out_inputs = [info, attended, w_out]
+    sent = local_call(functools.partial(out_kernel, True), out_shape, out_inputs, scalars=1)
+    came = shift(sent, "c", 1)
+    kept = local_call(functools.partial(out_kernel, False), out_shape, out_inputs, scalars=1)
+    arrived = lax.all_to_all(
+        (kept.astype(F32) + came.astype(F32)).astype(BF), PLANE, 0, 0, tiled=True
+    )
     stream, down_part = local_call(
         down_kernel,
         [

time: 291 us -> 289 us (level)
  blocking collectives: 97.7 us -> 75.5 us
  waiting for transfers between devices: 68.4 us -> 86.4 us
    all_to_all x1 -> x0, blocking collectives: 19.9 us -> none  [layer(): arrived = lax.all_to_all(out_part, HEAD, 0, 0, tiled=True)]
    all_to_all x1 -> x2, waiting for transfers between devices: 18.9 us -> 37.5 us  [the longest x1 26.2 us: layer(): w_in_here = lax.all_to_all(w_in_parts, SEQ, 0, 0, tiled=True)]
    all_to_all x1 -> x2, starting transfers between devices: 8.07 us -> 12.6 us  [the longest x1 8.98 us: layer(): w_in_here = lax.all_to_all(w_in_parts, SEQ, 0, 0, tiled=True)]
    all_to_all x1, starting transfers between devices: 14.2 us -> 9.8 us  [layer(): pooled = lax.all_to_all(pooled, (*PLANE, 'c'), 0, 0, tiled=True)]
    pallas_call x11 -> x14, Pallas kernels: 24.8 us -> 25.5 us  [local_call(): pl.pallas_call(kernel, out_shape=out, grid=(1,) if last else (), in_specs...]
  transfers between devices with their start and end apart: 13 -> 14, of which waited for: 10 -> 11; matrix products, arithmetic and copies ran while one was open for 2% -> 2% of each run, Pallas kernels for 4% -> 4%
where the time goes in v3:
time: 289 us; the launch traced here: 284 us
  waiting for transfers between devices  86.4 us (30%)
  blocking collectives  75.5 us (26%)
  starting transfers between devices  70 us (24%)
  Pallas kernels  25.5 us (9%)
  between operations  15.1 us (5%)
  local copies, waits for them, and re-layouts  8.27 us (3%)
  other arithmetic  2.95 us (1%)
    ppermute x9, starting transfers between devices, shift(): return lax.ppermute(x, axis, [(i, (i + by) % n) for i in range(n)])  30.7 us
    all_to_all x1, waiting for transfers between devices, layer(): w_in_here = lax.all_to_all(w_in_parts, SEQ, 0, 0, tiled=True)  26.2 us
    pallas_call x14, Pallas kernels, local_call(): pl.pallas_call(kernel, out_shape=out, grid=(1,) if last else (), in_specs...  25.5 us
    all_to_all x1, blocking collectives, layer(): kv = lax.all_to_all(kv, 'zh', 0, 0, tiled=True).reshape(-1, kv.shape[2])  24.8 us
    all_to_all x1, blocking collectives, layer(): states = lax.all_to_all(states, SKIP, 0, 0, tiled=True)  20.8 us
    ppermute x9, waiting for transfers between devices, shift(): return lax.ppermute(x, axis, [(i, (i + by) % n) for i in range(n)])  19.5 us
    all_to_all x1, waiting for transfers between devices, layer(): pooled = lax.all_to_all(pooled, Z, 0, 0, tiled=True)  17.8 us
    all_to_all x1, blocking collectives, over_plane(): near = lax.all_to_all(copies, PLANE, 0, 0, tiled=True)  17.3 us
  transfers between devices with their start and end apart: 14, of which 11 were waited for; matrix products, arithmetic and copies ran while one was open for 2% of the time, Pallas kernels for 4%

profile of v3, /device:TPU:1, one launch (start us, length us, event | category | flops | bytes accessed | tf_op | source)
XLA Modules:
  0.0 283.8 jit_solution(12503874652942090124)
XLA Ops:
  9.2 4.0 %collective-permute-start.2 = (bf16[128,464]{1,0:T(8,128)(2,1)S(1)}, bf16[128,464]{1,0:T(8,128)(2,1)S(1)}, u32[]{:S(2)}, u32[]{:S(2)}) collective-permute-start(bf16[128,464]{1,0:T(8,128)(2,1)S(1)} %pad_maximum_fusion), channel_id=1, source_target_pairs={{0,16},{16,0},{1,17},{17,1},{2,18},{18,2},{3,19},{19,3},{4,20},{20... | collective-permute-start | bytes 356360 | tf_op jit(solution)/shard_map/ppermute | solution.py:289
  20.9 3.4 %collective-permute-start = (bf16[16,64,128]{2,1,0:T(8,128)(2,1)S(1)}, bf16[16,64,128]{2,1,0:T(8,128)(2,1)S(1)}, u32[]{:S(2)}, u32[]{:S(2)}) collective-permute-start(bf16[16,64,128]{2,1,0:T(8,128)(2,1)S(1)} %shard_map.105), channel_id=1, source_target_pairs={{0,16},{16,0},{1,17},{17,1},{2,18},{18,2},{3,19},{19,3},{4,20},{20... | collective-permute-start | bytes 786440 | tf_op jit(solution)/shard_map/ppermute | solution.py:289
  24.2 2.3 shard_map.104
  28.8 16.9 %all-to-all-start = ((bf16[16,64,128]{2,1,0:T(8,128)(2,1)}), bf16[16,64,128]{2,1,0:T(8,128)(2,1)S(1)}, u32[]{:S(2)}, u32[]{:S(2)}) async-start(bf16[16,64,128]{2,1,0:T(8,128)(2,1)} %add_convert_fusion.1), calls=%async_computation | async-start | bytes 524288 | tf_op jit(solution)/shard_map/all_to_all | solution.py:365
  46.4 17.8 %all-to-all-done.arrived = bf16[16,64,128]{2,1,0:T(8,128)(2,1)S(1)} async-done(((bf16[16,64,128]{2,1,0:T(8,128)(2,1)}), bf16[16,64,128]{2,1,0:T(8,128)(2,1)S(1)}, u32[]{:S(2)}, u32[]{:S(2)}) %all-to-all-start) | async-done | bytes 262176 | tf_op jit(solution)/shard_map/all_to_all | solution.py:365
  64.2 9.0 %all-to-all-start.2 = ((bf16[32,40,128]{2,1,0:T(8,128)(2,1)}), bf16[32,40,128]{2,1,0:T(8,128)(2,1)S(1)}, u32[]{:S(2)}, u32[]{:S(2)}) async-start(bf16[32,40,128]{2,1,0:T(8,128)(2,1)} %shard_map.107), calls=%async_computation.2 | async-start | bytes 655360 | tf_op jit(solution)/shard_map/all_to_all | solution.py:334
  74.1 26.2 %all-to-all-done.2 = bf16[32,40,128]{2,1,0:T(8,128)(2,1)S(1)} async-done(((bf16[32,40,128]{2,1,0:T(8,128)(2,1)}), bf16[32,40,128]{2,1,0:T(8,128)(2,1)S(1)}, u32[]{:S(2)}, u32[]{:S(2)}) %all-to-all-start.2) | async-done | bytes 327712 | tf_op jit(solution)/shard_map/all_to_all | solution.py:334
  100.3 9.8 %all-to-all-start.1 = ((bf16[32,64,128]{2,1,0:T(8,128)(2,1)}), bf16[32,64,128]{2,1,0:T(8,128)(2,1)S(1)}, u32[]{:S(2)}, u32[]{:S(2)}) async-start(bf16[32,64,128]{2,1,0:T(8,128)(2,1)} %shard_map.106), calls=%async_computation.1 | async-start | bytes 1048576 | tf_op jit(solution)/shard_map/all_to_all | solution.py:369
  110.2 11.7 %all-to-all-done.1.pooled = bf16[32,64,128]{2,1,0:T(8,128)(2,1)S(1)} async-done(((bf16[32,64,128]{2,1,0:T(8,128)(2,1)}), bf16[32,64,128]{2,1,0:T(8,128)(2,1)S(1)}, u32[]{:S(2)}, u32[]{:S(2)}) %all-to-all-start.1) | async-done | bytes 524320 | tf_op jit(solution)/shard_map/all_to_all | solution.py:369
  121.8 2.8 shard_map.108
  124.6 17.3 %all_to_all.40.own.embed = bf16[16,192,128]{2,1,0:T(8,128)(2,1)S(1)} all-to-all(bf16[16,192,128]{2,1,0:T(8,128)(2,1)S(1)} %shard_map.108), channel_id=1, replica_groups=mesh['zh'=4,'zm'=2,'zp'=2,'yl'=2,'yh'=2,'x'=4,'c'=2] {'yl','yh','x'}, dimensions={0} | all-to-all | bytes 1572864 | tf_op jit(solution)/shard_map/all_to_all | solution.py:293
  141.9 2.9 %collective-permute-start.1 = (bf16[16,192,128]{2,1,0:T(8,128)(2,1)S(1)}, bf16[16,192,128]{2,1,0:T(8,128)(2,1)S(1)}, u32[]{:S(2)}, u32[]{:S(2)}) collective-permute-start(bf16[16,192,128]{2,1,0:T(8,128)(2,1)S(1)} %all_to_all.40.own.embed), channel_id=1, source_target_pairs={{0,1},{1,0},{2,3},{3,2},{4,5},{5,4},{6,7},{7,6},{8,9},{9,8},{10,11... | collective-permute-start | bytes 2359304 | tf_op jit(solution)/shard_map/ppermute | solution.py:289
  146.6 3.3 %shard_map.109 = (bf16[192,128]{1,0:T(8,128)(2,1)S(1)}, bf16[4,192,256]{2,1,0:T(8,128)(2,1)S(1)}) custom-call(s32[7]{0:T(128)S(1)} %stack.28.info, bf16[16,192,128]{2,1,0:T(8,128)(2,1)S(1)} %all_to_all.40.own.embed, bf16[16,192,128]{2,1,0:T(8,128)(2,1)S(1)} %collective-permute-done.1.other, f32[16,256]{1,0:T(8,128)S(1)} %reshape.38.gain, ...), custom_call_target="tpu_custom_call" | custom-call | flops 100000000 | bytes 1000000 | tf_op jit(solution)/shard_map/pallas_call | solution.py:37
  149.9 24.8 %all_to_all.41 = bf16[4,192,256]{2,1,0:T(8,128)(2,1)S(1)} all-to-all(bf16[4,192,256]{2,1,0:T(8,128)(2,1)S(1)} %get-tuple-element.7), channel_id=1, replica_groups=mesh['zh'=4,'zm'=2,'zp'=2,'yl'=2,'yh'=2,'x'=4,'c'=2] {'zh'}, dimensions={0} | all-to-all | bytes 786432 | tf_op jit(solution)/shard_map/all_to_all | solution.py:394
  174.7 4.5 %collective-permute-start.3 = (bf16[768,256]{1,0:T(8,128)(2,1)S(1)}, bf16[768,256]{1,0:T(8,128)(2,1)S(1)}, u32[]{:S(2)}, u32[]{:S(2)}) collective-permute-start(bf16[768,256]{1,0:T(8,128)(2,1)S(1)} %bitcast.33), channel_id=1, source_target_pairs={{0,32},{32,64},{64,96},{96,128},{128,160},{160,192},{192,224},{224... | collective-permute-start | bytes 1179656 | tf_op jit(solution)/shard_map/ppermute | solution.py:289
  182.0 6.3 %collective-permute-start.5 = (bf16[384,256]{1,0:T(8,128)(2,1)}, bf16[384,256]{1,0:T(8,128)(2,1)S(1)}, u32[]{:S(2)}, u32[]{:S(2)}) collective-permute-start(bf16[384,256]{1,0:T(8,128)(2,1)} %bitcast.17), channel_id=1, source_target_pairs={{0,64},{32,96},{64,128},{96,160},{128,192},{160,224},{192,256},{22... | collective-permute-start | bytes 589832 | tf_op jit(solution)/shard_map/ppermute | solution.py:289
  193.2 9.3 %collective-permute-done.6.rest_4_ = bf16[384,256]{1,0:T(8,128)(2,1)} collective-permute-done((bf16[384,256]{1,0:T(8,128)(2,1)}, bf16[384,256]{1,0:T(8,128)(2,1)}, u32[]{:S(2)}, u32[]{:S(2)}) %collective-permute-start.6) | collective-permute-done | bytes 196640 | tf_op jit(solution)/shard_map/ppermute | solution.py:289
  202.5 2.5 shard_map.110.attended
  205.9 3.6 %collective-permute-start.7 = (bf16[16,96,256]{2,1,0:T(8,128)(2,1)S(1)}, bf16[16,96,256]{2,1,0:T(8,128)(2,1)S(1)}, u32[]{:S(2)}, u32[]{:S(2)}) collective-permute-start(bf16[16,96,256]{2,1,0:T(8,128)(2,1)S(1)} %shard_map.112), channel_id=1, source_target_pairs={{0,1},{1,0},{2,3},{3,2},{4,5},{5,4},{6,7},{7,6},{8,9},{9,8},{10,11... | collective-permute-start | bytes 2359304 | tf_op jit(solution)/shard_map/ppermute | solution.py:289
  212.6 3.6 %all-to-all-start.5 = ((bf16[16,96,256]{2,1,0:T(8,128)(2,1)}), bf16[16,96,256]{2,1,0:T(8,128)(2,1)S(1)}, u32[]{:S(2)}, u32[]{:S(2)}) async-start(bf16[16,96,256]{2,1,0:T(8,128)(2,1)} %add_convert_fusion), calls=%async_computation.5 | async-start | bytes 1572864 | tf_op jit(solution)/shard_map/all_to_all | solution.py:407
  218.6 11.3 %all-to-all-done.5.arrived = bf16[16,96,256]{2,1,0:T(8,128)(2,1)S(1)} async-done(((bf16[16,96,256]{2,1,0:T(8,128)(2,1)}), bf16[16,96,256]{2,1,0:T(8,128)(2,1)S(1)}, u32[]{:S(2)}, u32[]{:S(2)}) %all-to-all-start.5) | async-done | bytes 786464 | tf_op jit(solution)/shard_map/all_to_all | solution.py:407
  231.5 12.7 %all_to_all.42.arrived = bf16[16,64,128]{2,1,0:T(8,128)(2,1)S(1)} all-to-all(bf16[16,64,128]{2,1,0:T(8,128)(2,1)S(1)} %get-tuple-element.9), channel_id=1, replica_groups=mesh['zh'=4,'zm'=2,'zp'=2,'yl'=2,'yh'=2,'x'=4,'c'=2] {'yh','x','c'}, dimensions={0} | all-to-all | bytes 524288 | tf_op jit(solution)/shard_map/all_to_all | solution.py:419
  244.3 20.8 %all_to_all.43.states = bf16[16,64,128]{2,1,0:T(8,128)(2,1)S(1)} all-to-all(bf16[16,64,128]{2,1,0:T(8,128)(2,1)S(1)} %shard_map.115), channel_id=1, replica_groups=mesh['zh'=4,'zm'=2,'zp'=2,'yl'=2,'yh'=2,'x'=4,'c'=2] {'zh','zm','yl'}, dimensions={0} | all-to-all | bytes 524288 | tf_op jit(solution)/shard_map/all_to_all | solution.py:424
  272.2 4.7 %shard_map.117 = bf16[80,768]{1,0:T(8,128)(2,1)} custom-call(s32[7]{0:T(128)S(1)} %stack.28.info, s32[2,2,768]{2,1,0:T(2,128)S(1)} %reshape.43.labels_main, s32[2,6,256]{2,1,0:T(8,128)S(1)} %reshape.45.labels_rest, s32[1,768]{1,0:T(1,128)S(1)} %broadcast_in_dim.11.ids, bf16[80,768]{1,0:T(8,128)(2,1)S(1)} %bitcast.39, ...), custom_call_target="tpu_custom_call" | custom-call | flops 100000000 | bytes 1000000 | tf_op jit(solution)/shard_map/pallas_call | solution.py:37
  (72 shorter events, 37.4 us)
Async XLA Ops:
  7.2 139.5 %all-gather.2.cloned.1.call-start = ((), (), s32[]{:S(2)}) async-start(), calls=%async_computation.8 | async-start | bytes 4456448 | tf_op jit(solution)/shard_map/all_gather | solution.py:355
  7.2 9.4 %copy-start.7 = (s32[768]{0:T(1024)S(1)}, s32[768]{0:T(1024)}, u32[]{:S(2)}) copy-start(s32[768]{0:T(1024)} %param.10) | copy-start | bytes 9220
  8.1 9.2 %copy-start.4 = (s32[3072]{0:T(1024)S(1)}, s32[3072]{0:T(1024)}, u32[]{:S(2)}) copy-start(s32[3072]{0:T(1024)} %param.11) | copy-start | bytes 36868
  9.2 6.4 %collective-permute-start.2 = (bf16[128,464]{1,0:T(8,128)(2,1)S(1)}, bf16[128,464]{1,0:T(8,128)(2,1)S(1)}, u32[]{:S(2)}, u32[]{:S(2)}) collective-permute-start(bf16[128,464]{1,0:T(8,128)(2,1)S(1)} %pad_maximum_fusion), channel_id=1, source_target_pairs={{0,16},{16,0},{1,17},{17,1},{2,18},{18,2},{3,19},{19,3},{4,20},{20... | collective-permute-start | bytes 356360 | tf_op jit(solution)/shard_map/ppermute | solution.py:289
  15.7 2.9 %copy-start.2 = (bf16[768,80]{0,1:T(8,128)(2,1)S(1)}, bf16[768,80]{0,1:T(8,128)(2,1)}, u32[]{:S(2)}) copy-start(bf16[768,80]{0,1:T(8,128)(2,1)} %param.9) | copy-start | bytes 368644
  20.9 24.8 %copy-start.3 = (bf16[40,256]{1,0:T(8,128)(2,1)S(1)}, bf16[40,256]{1,0:T(8,128)(2,1)}, u32[]{:S(2)}) copy-start(bf16[40,256]{1,0:T(8,128)(2,1)} %w_in.1) | copy-start | bytes 61444
  20.9 7.1 %collective-permute-start = (bf16[16,64,128]{2,1,0:T(8,128)(2,1)S(1)}, bf16[16,64,128]{2,1,0:T(8,128)(2,1)S(1)}, u32[]{:S(2)}, u32[]{:S(2)}) collective-permute-start(bf16[16,64,128]{2,1,0:T(8,128)(2,1)S(1)} %shard_map.105), channel_id=1, source_target_pairs={{0,16},{16,0},{1,17},{17,1},{2,18},{18,2},{3,19},{19,3},{4,20},{20... | collective-permute-start | bytes 786440 | tf_op jit(solution)/shard_map/ppermute | solution.py:289
  28.8 81.3 %copy-start.6 = (f32[1280]{0:T(1024)S(1)}, f32[1280]{0:T(1024)}, u32[]{:S(2)}) copy-start(f32[1280]{0:T(1024)} %param.12) | copy-start | bytes 15364
  28.8 35.4 %all-to-all-start = ((bf16[16,64,128]{2,1,0:T(8,128)(2,1)}), bf16[16,64,128]{2,1,0:T(8,128)(2,1)S(1)}, u32[]{:S(2)}, u32[]{:S(2)}) async-start(bf16[16,64,128]{2,1,0:T(8,128)(2,1)} %add_convert_fusion.1), calls=%async_computation | async-start | bytes 524288 | tf_op jit(solution)/shard_map/all_to_all | solution.py:365
  64.2 36.1 %all-to-all-start.2 = ((bf16[32,40,128]{2,1,0:T(8,128)(2,1)}), bf16[32,40,128]{2,1,0:T(8,128)(2,1)S(1)}, u32[]{:S(2)}, u32[]{:S(2)}) async-start(bf16[32,40,128]{2,1,0:T(8,128)(2,1)} %shard_map.107), calls=%async_computation.2 | async-start | bytes 655360 | tf_op jit(solution)/shard_map/all_to_all | solution.py:334
  100.3 21.6 %all-to-all-start.1 = ((bf16[32,64,128]{2,1,0:T(8,128)(2,1)}), bf16[32,64,128]{2,1,0:T(8,128)(2,1)S(1)}, u32[]{:S(2)}, u32[]{:S(2)}) async-start(bf16[32,64,128]{2,1,0:T(8,128)(2,1)} %shard_map.106), calls=%async_computation.1 | async-start | bytes 1048576 | tf_op jit(solution)/shard_map/all_to_all | solution.py:369
  121.8 22.9 %copy-start.5 = (f32[4096]{0:T(1024)S(1)}, f32[4096]{0:T(1024)}, u32[]{:S(2)}) copy-start(f32[4096]{0:T(1024)} %param.14) | copy-start | bytes 49156
  141.9 4.8 %collective-permute-start.1 = (bf16[16,192,128]{2,1,0:T(8,128)(2,1)S(1)}, bf16[16,192,128]{2,1,0:T(8,128)(2,1)S(1)}, u32[]{:S(2)}, u32[]{:S(2)}) collective-permute-start(bf16[16,192,128]{2,1,0:T(8,128)(2,1)S(1)} %all_to_all.40.own.embed), channel_id=1, source_target_pairs={{0,1},{1,0},{2,3},{3,2},{4,5},{5,4},{6,7},{7,6},{8,9},{9,8},{10,11... | collective-permute-start | bytes 2359304 | tf_op jit(solution)/shard_map/ppermute | solution.py:289
  174.7 27.8 %collective-permute-start.3 = (bf16[768,256]{1,0:T(8,128)(2,1)S(1)}, bf16[768,256]{1,0:T(8,128)(2,1)S(1)}, u32[]{:S(2)}, u32[]{:S(2)}) collective-permute-start(bf16[768,256]{1,0:T(8,128)(2,1)S(1)} %bitcast.33), channel_id=1, source_target_pairs={{0,32},{32,64},{64,96},{96,128},{128,160},{160,192},{192,224},{224... | collective-permute-start | bytes 1179656 | tf_op jit(solution)/shard_map/ppermute | solution.py:289
  179.2 23.3 %collective-permute-start.4 = (bf16[768,256]{1,0:T(8,128)(2,1)S(1)}, bf16[768,256]{1,0:T(8,128)(2,1)}, u32[]{:S(2)}, u32[]{:S(2)}) collective-permute-start(bf16[768,256]{1,0:T(8,128)(2,1)S(1)} %bitcast.34), channel_id=1, source_target_pairs={{0,480},{32,0},{64,32},{96,64},{128,96},{160,128},{192,160},{224,1... | collective-permute-start | bytes 1179656 | tf_op jit(solution)/shard_map/ppermute | solution.py:289
  182.0 11.3 %collective-permute-start.5 = (bf16[384,256]{1,0:T(8,128)(2,1)}, bf16[384,256]{1,0:T(8,128)(2,1)S(1)}, u32[]{:S(2)}, u32[]{:S(2)}) collective-permute-start(bf16[384,256]{1,0:T(8,128)(2,1)} %bitcast.17), channel_id=1, source_target_pairs={{0,64},{32,96},{64,128},{96,160},{128,192},{160,224},{192,256},{22... | collective-permute-start | bytes 589832 | tf_op jit(solution)/shard_map/ppermute | solution.py:289
  188.3 14.2 %collective-permute-start.6 = (bf16[384,256]{1,0:T(8,128)(2,1)}, bf16[384,256]{1,0:T(8,128)(2,1)}, u32[]{:S(2)}, u32[]{:S(2)}) collective-permute-start(bf16[384,256]{1,0:T(8,128)(2,1)} %bitcast.18), channel_id=1, source_target_pairs={{0,448},{32,480},{64,0},{96,32},{128,64},{160,96},{192,128},{224,1... | collective-permute-start | bytes 589832 | tf_op jit(solution)/shard_map/ppermute | solution.py:289
  202.5 2.5 copy-start.1
  205.9 5.5 %collective-permute-start.7 = (bf16[16,96,256]{2,1,0:T(8,128)(2,1)S(1)}, bf16[16,96,256]{2,1,0:T(8,128)(2,1)S(1)}, u32[]{:S(2)}, u32[]{:S(2)}) collective-permute-start(bf16[16,96,256]{2,1,0:T(8,128)(2,1)S(1)} %shard_map.112), channel_id=1, source_target_pairs={{0,1},{1,0},{2,3},{3,2},{4,5},{5,4},{6,7},{7,6},{8,9},{9,8},{10,11... | collective-permute-start | bytes 2359304 | tf_op jit(solution)/shard_map/ppermute | solution.py:289
  212.6 17.4 %all-to-all-start.5 = ((bf16[16,96,256]{2,1,0:T(8,128)(2,1)}), bf16[16,96,256]{2,1,0:T(8,128)(2,1)S(1)}, u32[]{:S(2)}, u32[]{:S(2)}) async-start(bf16[16,96,256]{2,1,0:T(8,128)(2,1)} %add_convert_fusion), calls=%async_computation.5 | async-start | bytes 1572864 | tf_op jit(solution)/shard_map/all_to_all | solution.py:407
  216.2 2.2 copy-start
  265.1 7.1 %collective-permute-start.8 = (bf16[16,64,128]{2,1,0:T(8,128)(2,1)S(1)}, bf16[16,64,128]{2,1,0:T(8,128)(2,1)S(1)}, u32[]{:S(2)}, u32[]{:S(2)}) collective-permute-start(bf16[16,64,128]{2,1,0:T(8,128)(2,1)S(1)} %all_to_all.43.states), channel_id=1, source_target_pairs={{0,32},{32,0},{1,33},{33,1},{2,34},{34,2},{3,35},{35,3},{4,36},{36... | collective-permute-start | bytes 786440 | tf_op jit(solution)/shard_map/ppermute | solution.py:289
Sparse Core Ops, SparseCore 0:
  16.8 99.5 all-gather.1

commit v4 on v3

--- a/solution.py
+++ b/solution.py
@@ -94,7 +94,7 @@
         out[i] = held
 
 
-def embed_kernel(pooled, gain, w_in, out, keep):
+def embed_kernel(info, pooled, gain, near, far, out, keep):
     heads, count, size = keep.shape
     each = count // 2
     half = each // 2
@@ -113,9 +113,10 @@
         square = square + jnp.sum(rest * rest, axis=1, keepdims=True)
     scale = lax.rsqrt(square / (heads * size) + EPSILON)
     total = jnp.zeros(out.shape[1:], F32)
-    for h in range(heads):
-        normed = keep[h] * scale * gain[h : h + 1, :]
-        total = total + matmul(normed.astype(BF), w_in[h * size : (h + 1) * size, :])
+    for k in range(heads // 2):
+        for source, h in ((near, 2 * k + info[5]), (far, 2 * k + 1 - info[5])):
+            normed = keep[h] * scale * gain[pl.ds(h, 1), :]
+            total = total + matmul(normed.astype(BF), source[k * size : (k + 1) * size, :])
     held = total.astype(BF)
     for i in range(out.shape[0]):
         out[i] = held
@@ -328,11 +329,12 @@
 
     w_in_parts = local_call(
         split_kernel,
-        jax.ShapeDtypeStruct((n_z * n_yl, w_in.shape[0], w_in.shape[1] // n_yl), BF),
+        jax.ShapeDtypeStruct((n_z, w_in.shape[0], w_in.shape[1] // n_yl), BF),
         [w_in],
     )
-    w_in_here = lax.all_to_all(w_in_parts, SEQ, 0, 0, tiled=True)
-    w_in_here = w_in_here.reshape(-1, w_in_parts.shape[2])
+    w_in_near = lax.all_to_all(w_in_parts, SKIP, 0, 0, tiled=True)
+    w_in_near = w_in_near.reshape(-1, w_in_parts.shape[2])
+    w_in_far = shift(w_in_near, "zp", 1)
 
     halves = [
         jnp.concatenate([w_qkv[:, j, k * HEAD_SIZE : (k + 1) * HEAD_SIZE] for j in range(3)], axis=1)
@@ -369,9 +371,10 @@
     pooled = lax.all_to_all(pooled, (*PLANE, "c"), 0, 0, tiled=True)
     embed = local_call(
         embed_kernel,
-        jax.ShapeDtypeStruct((n_plane, rows_z, w_in_here.shape[1]), BF),
-        [pooled, pool_gain.reshape(n_head, cross_size), w_in_here],
+        jax.ShapeDtypeStruct((n_plane, rows_z, w_in_near.shape[1]), BF),
+        [info, pooled, pool_gain.reshape(n_head, cross_size), w_in_near, w_in_far],
         scratch=[pltpu.VMEM((n_head, rows_z, cross_size), F32)],
+        scalars=1,
     )
     own_embed, other_embed = over_plane(embed)
     queries, kv = local_call(

time: 289 us -> 283 us (0.979)
  waiting for transfers between devices: 86.4 us -> 72 us
  starting transfers between devices: 70 us -> 82.6 us
  blocking collectives: 75.5 us -> 71.2 us
    ppermute x9 -> x10, starting transfers between devices: 30.7 us -> 42.9 us  [shift(): return lax.ppermute(x, axis, [(i, (i + by) % n) for i in range(n)])]
    all_to_all x1, waiting for transfers between devices: 11.7 us -> 1.72 us  [layer(): pooled = lax.all_to_all(pooled, (*PLANE, 'c'), 0, 0, tiled=True)]
    all_to_all x1, waiting for transfers between devices: 26.2 us -> 17.1 us  [layer(): w_in_near = lax.all_to_all(w_in_parts, SKIP, 0, 0, tiled=True)]
    all_to_all x1, blocking collectives: 24.8 us -> 19.8 us  [layer(): kv = lax.all_to_all(kv, 'zh', 0, 0, tiled=True).reshape(-1, kv.shape[2])]
    ppermute x9 -> x10, waiting for transfers between devices: 19.5 us -> 24.2 us  [shift(): return lax.ppermute(x, axis, [(i, (i + by) % n) for i in range(n)])]
  transfers between devices with their start and end apart: 14 -> 15, of which waited for: 11 -> 12; matrix products, arithmetic and copies ran while one was open for 2% -> 2% of each run, Pallas kernels for 4% -> 5%
where the time goes in v4:
time: 283 us; the launch traced here: 278 us
  starting transfers between devices  82.6 us (29%)
  waiting for transfers between devices  72 us (25%)
  blocking collectives  71.2 us (25%)
  Pallas kernels  26.1 us (9%)
  between operations  15.1 us (5%)
  local copies, waits for them, and re-layouts  8.27 us (3%)
  other arithmetic  2.97 us (1%)
    ppermute x10, starting transfers between devices, shift(): return lax.ppermute(x, axis, [(i, (i + by) % n) for i in range(n)])  42.9 us
    pallas_call x14, Pallas kernels, local_call(): pl.pallas_call(kernel, out_shape=out, grid=(1,) if last else (), in_specs...  26.1 us
    ppermute x10, waiting for transfers between devices, shift(): return lax.ppermute(x, axis, [(i, (i + by) % n) for i in range(n)])  24.2 us
    all_to_all x1, blocking collectives, layer(): states = lax.all_to_all(states, SKIP, 0, 0, tiled=True)  21 us
    all_to_all x1, blocking collectives, layer(): kv = lax.all_to_all(kv, 'zh', 0, 0, tiled=True).reshape(-1, kv.shape[2])  19.8 us
    all_to_all x1, waiting for transfers between devices, layer(): pooled = lax.all_to_all(pooled, Z, 0, 0, tiled=True)  17.7 us
    all_to_all x1, blocking collectives, over_plane(): near = lax.all_to_all(copies, PLANE, 0, 0, tiled=True)  17.7 us
    all_to_all x1, waiting for transfers between devices, layer(): w_in_near = lax.all_to_all(w_in_parts, SKIP, 0, 0, tiled=True)  17.1 us
  transfers between devices with their start and end apart: 15, of which 12 were waited for; matrix products, arithmetic and copies ran while one was open for 2% of the time, Pallas kernels for 5%

profile of v4, /device:TPU:1, one launch (start us, length us, event | category | flops | bytes accessed | tf_op | source)
XLA Modules:
  0.0 278.2 jit_solution(1478755671488119007)
XLA Ops:
  9.2 4.0 %collective-permute-start.3 = (bf16[128,464]{1,0:T(8,128)(2,1)S(1)}, bf16[128,464]{1,0:T(8,128)(2,1)S(1)}, u32[]{:S(2)}, u32[]{:S(2)}) collective-permute-start(bf16[128,464]{1,0:T(8,128)(2,1)S(1)} %pad_maximum_fusion), channel_id=1, source_target_pairs={{0,16},{16,0},{1,17},{17,1},{2,18},{18,2},{3,19},{19,3},{4,20},{20... | collective-permute-start | bytes 356360 | tf_op jit(solution)/shard_map/ppermute | solution.py:290
  20.9 3.4 %collective-permute-start = (bf16[16,64,128]{2,1,0:T(8,128)(2,1)S(1)}, bf16[16,64,128]{2,1,0:T(8,128)(2,1)S(1)}, u32[]{:S(2)}, u32[]{:S(2)}) collective-permute-start(bf16[16,64,128]{2,1,0:T(8,128)(2,1)S(1)} %shard_map.105), channel_id=1, source_target_pairs={{0,16},{16,0},{1,17},{17,1},{2,18},{18,2},{3,19},{19,3},{4,20},{20... | collective-permute-start | bytes 786440 | tf_op jit(solution)/shard_map/ppermute | solution.py:290
  28.8 16.9 %all-to-all-start = ((bf16[16,64,128]{2,1,0:T(8,128)(2,1)}), bf16[16,64,128]{2,1,0:T(8,128)(2,1)S(1)}, u32[]{:S(2)}, u32[]{:S(2)}) async-start(bf16[16,64,128]{2,1,0:T(8,128)(2,1)} %add_convert_fusion.1), calls=%async_computation | async-start | bytes 524288 | tf_op jit(solution)/shard_map/all_to_all | solution.py:367
  46.4 17.7 %all-to-all-done.arrived = bf16[16,64,128]{2,1,0:T(8,128)(2,1)S(1)} async-done(((bf16[16,64,128]{2,1,0:T(8,128)(2,1)}), bf16[16,64,128]{2,1,0:T(8,128)(2,1)S(1)}, u32[]{:S(2)}, u32[]{:S(2)}) %all-to-all-start) | async-done | bytes 262176 | tf_op jit(solution)/shard_map/all_to_all | solution.py:367
  64.1 8.7 %all-to-all-start.2 = ((bf16[16,40,128]{2,1,0:T(8,128)(2,1)}), bf16[16,40,128]{2,1,0:T(8,128)(2,1)S(1)}, u32[]{:S(2)}, u32[]{:S(2)}) async-start(bf16[16,40,128]{2,1,0:T(8,128)(2,1)} %shard_map.107), calls=%async_computation.2 | async-start | bytes 327680 | tf_op jit(solution)/shard_map/all_to_all | solution.py:335
  73.7 17.1 %all-to-all-done.2 = bf16[16,40,128]{2,1,0:T(8,128)(2,1)S(1)} async-done(((bf16[16,40,128]{2,1,0:T(8,128)(2,1)}), bf16[16,40,128]{2,1,0:T(8,128)(2,1)S(1)}, u32[]{:S(2)}, u32[]{:S(2)}) %all-to-all-start.2) | async-done | bytes 163872 | tf_op jit(solution)/shard_map/all_to_all | solution.py:335
  90.8 10.4 %all-to-all-start.1 = ((bf16[32,64,128]{2,1,0:T(8,128)(2,1)}), bf16[32,64,128]{2,1,0:T(8,128)(2,1)S(1)}, u32[]{:S(2)}, u32[]{:S(2)}) async-start(bf16[32,64,128]{2,1,0:T(8,128)(2,1)} %shard_map.106), calls=%async_computation.1 | async-start | bytes 1048576 | tf_op jit(solution)/shard_map/all_to_all | solution.py:371
  103.3 8.0 %collective-permute-done.1.far = bf16[640,128]{1,0:T(8,128)(2,1)S(1)} collective-permute-done((bf16[640,128]{1,0:T(8,128)(2,1)S(1)}, bf16[640,128]{1,0:T(8,128)(2,1)S(1)}, u32[]{:S(2)}, u32[]{:S(2)}) %collective-permute-start.1) | collective-permute-done | bytes 163872 | tf_op jit(solution)/shard_map/ppermute | solution.py:290
  113.0 3.4 %shard_map.108 = bf16[16,192,128]{2,1,0:T(8,128)(2,1)S(1)} custom-call(s32[7]{0:T(128)S(1)} %stack.28.info, bf16[32,64,128]{2,1,0:T(8,128)(2,1)S(1)} %all-to-all-done.1.pooled, f32[16,80]{1,0:T(8,128)S(1)} %reshape.36.gain, bf16[640,128]{1,0:T(8,128)(2,1)S(1)} %bitcast.40, bf16[640,128]{1,0:T(8,128)(2,1)S(1)} %collective-permute-done.1.far), custom_call_target="tpu_custom_call" | custom-call | flops 100000000 | bytes 1000000 | tf_op jit(solution)/shard_map/pallas_call | solution.py:37
  116.4 17.7 %all_to_all.40.own.embed = bf16[16,192,128]{2,1,0:T(8,128)(2,1)S(1)} all-to-all(bf16[16,192,128]{2,1,0:T(8,128)(2,1)S(1)} %shard_map.108), channel_id=1, replica_groups=mesh['zh'=4,'zm'=2,'zp'=2,'yl'=2,'yh'=2,'x'=4,'c'=2] {'yl','yh','x'}, dimensions={0} | all-to-all | bytes 1572864 | tf_op jit(solution)/shard_map/all_to_all | solution.py:294
  134.1 4.4 %collective-permute-start.2 = (bf16[16,192,128]{2,1,0:T(8,128)(2,1)S(1)}, bf16[16,192,128]{2,1,0:T(8,128)(2,1)S(1)}, u32[]{:S(2)}, u32[]{:S(2)}) collective-permute-start(bf16[16,192,128]{2,1,0:T(8,128)(2,1)S(1)} %all_to_all.40.own.embed), channel_id=1, source_target_pairs={{0,1},{1,0},{2,3},{3,2},{4,5},{5,4},{6,7},{7,6},{8,9},{9,8},{10,11... | collective-permute-start | bytes 2359304 | tf_op jit(solution)/shard_map/ppermute | solution.py:290
  140.4 3.3 %shard_map.109 = (bf16[192,128]{1,0:T(8,128)(2,1)S(1)}, bf16[4,192,256]{2,1,0:T(8,128)(2,1)S(1)}) custom-call(s32[7]{0:T(128)S(1)} %stack.28.info, bf16[16,192,128]{2,1,0:T(8,128)(2,1)S(1)} %all_to_all.40.own.embed, bf16[16,192,128]{2,1,0:T(8,128)(2,1)S(1)} %collective-permute-done.2.other, f32[16,256]{1,0:T(8,128)S(1)} %reshape.38.gain, ...), custom_call_target="tpu_custom_call" | custom-call | flops 100000000 | bytes 1000000 | tf_op jit(solution)/shard_map/pallas_call | solution.py:37
  143.7 19.8 %all_to_all.41 = bf16[4,192,256]{2,1,0:T(8,128)(2,1)S(1)} all-to-all(bf16[4,192,256]{2,1,0:T(8,128)(2,1)S(1)} %get-tuple-element.7), channel_id=1, replica_groups=mesh['zh'=4,'zm'=2,'zp'=2,'yl'=2,'yh'=2,'x'=4,'c'=2] {'zh'}, dimensions={0} | all-to-all | bytes 786432 | tf_op jit(solution)/shard_map/all_to_all | solution.py:397
  163.4 11.7 %collective-permute-start.4 = (bf16[768,256]{1,0:T(8,128)(2,1)S(1)}, bf16[768,256]{1,0:T(8,128)(2,1)S(1)}, u32[]{:S(2)}, u32[]{:S(2)}) collective-permute-start(bf16[768,256]{1,0:T(8,128)(2,1)S(1)} %bitcast.33), channel_id=1, source_target_pairs={{0,32},{32,64},{64,96},{96,128},{128,160},{160,192},{192,224},{224... | collective-permute-start | bytes 1179656 | tf_op jit(solution)/shard_map/ppermute | solution.py:290
  177.9 4.6 %collective-permute-start.6 = (bf16[384,256]{1,0:T(8,128)(2,1)}, bf16[384,256]{1,0:T(8,128)(2,1)S(1)}, u32[]{:S(2)}, u32[]{:S(2)}) collective-permute-start(bf16[384,256]{1,0:T(8,128)(2,1)} %bitcast.17), channel_id=1, source_target_pairs={{0,64},{32,96},{64,128},{96,160},{128,192},{160,224},{192,256},{22... | collective-permute-start | bytes 589832 | tf_op jit(solution)/shard_map/ppermute | solution.py:290
  182.5 2.8 collective-permute-start.7
  189.1 5.0 %collective-permute-done.7.rest_4_ = bf16[384,256]{1,0:T(8,128)(2,1)} collective-permute-done((bf16[384,256]{1,0:T(8,128)(2,1)}, bf16[384,256]{1,0:T(8,128)(2,1)}, u32[]{:S(2)}, u32[]{:S(2)}) %collective-permute-start.7) | collective-permute-done | bytes 196640 | tf_op jit(solution)/shard_map/ppermute | solution.py:290
  194.2 2.5 shard_map.110.attended
  197.6 6.1 %collective-permute-start.8 = (bf16[16,96,256]{2,1,0:T(8,128)(2,1)S(1)}, bf16[16,96,256]{2,1,0:T(8,128)(2,1)S(1)}, u32[]{:S(2)}, u32[]{:S(2)}) collective-permute-start(bf16[16,96,256]{2,1,0:T(8,128)(2,1)S(1)} %shard_map.112), channel_id=1, source_target_pairs={{0,1},{1,0},{2,3},{3,2},{4,5},{5,4},{6,7},{7,6},{8,9},{9,8},{10,11... | collective-permute-start | bytes 2359304 | tf_op jit(solution)/shard_map/ppermute | solution.py:290
  206.8 3.6 %all-to-all-start.5 = ((bf16[16,96,256]{2,1,0:T(8,128)(2,1)}), bf16[16,96,256]{2,1,0:T(8,128)(2,1)S(1)}, u32[]{:S(2)}, u32[]{:S(2)}) async-start(bf16[16,96,256]{2,1,0:T(8,128)(2,1)} %add_convert_fusion), calls=%async_computation.5 | async-start | bytes 1572864 | tf_op jit(solution)/shard_map/all_to_all | solution.py:410
  212.9 11.3 %all-to-all-done.5.arrived = bf16[16,96,256]{2,1,0:T(8,128)(2,1)S(1)} async-done(((bf16[16,96,256]{2,1,0:T(8,128)(2,1)}), bf16[16,96,256]{2,1,0:T(8,128)(2,1)S(1)}, u32[]{:S(2)}, u32[]{:S(2)}) %all-to-all-start.5) | async-done | bytes 786464 | tf_op jit(solution)/shard_map/all_to_all | solution.py:410
  225.8 12.7 %all_to_all.42.arrived = bf16[16,64,128]{2,1,0:T(8,128)(2,1)S(1)} all-to-all(bf16[16,64,128]{2,1,0:T(8,128)(2,1)S(1)} %get-tuple-element.9), channel_id=1, replica_groups=mesh['zh'=4,'zm'=2,'zp'=2,'yl'=2,'yh'=2,'x'=4,'c'=2] {'yh','x','c'}, dimensions={0} | all-to-all | bytes 524288 | tf_op jit(solution)/shard_map/all_to_all | solution.py:422
  238.5 21.0 %all_to_all.43.states = bf16[16,64,128]{2,1,0:T(8,128)(2,1)S(1)} all-to-all(bf16[16,64,128]{2,1,0:T(8,128)(2,1)S(1)} %shard_map.115), channel_id=1, replica_groups=mesh['zh'=4,'zm'=2,'zp'=2,'yl'=2,'yh'=2,'x'=4,'c'=2] {'zh','zm','yl'}, dimensions={0} | all-to-all | bytes 524288 | tf_op jit(solution)/shard_map/all_to_all | solution.py:427
  266.7 4.7 %shard_map.117 = bf16[80,768]{1,0:T(8,128)(2,1)} custom-call(s32[7]{0:T(128)S(1)} %stack.28.info, s32[2,2,768]{2,1,0:T(2,128)S(1)} %reshape.43.labels_main, s32[2,6,256]{2,1,0:T(8,128)S(1)} %reshape.45.labels_rest, s32[1,768]{1,0:T(1,128)S(1)} %broadcast_in_dim.11.ids, bf16[80,768]{1,0:T(8,128)(2,1)S(1)} %bitcast.38, ...), custom_call_target="tpu_custom_call" | custom-call | flops 100000000 | bytes 1000000 | tf_op jit(solution)/shard_map/pallas_call | solution.py:37
  (74 shorter events, 42.3 us)
Async XLA Ops:
  7.2 133.2 %all-gather.2.cloned.1.call-start = ((), (), s32[]{:S(2)}) async-start(), calls=%async_computation.8 | async-start | bytes 4456448 | tf_op jit(solution)/shard_map/all_gather | solution.py:357
  7.2 9.4 %copy-start.7 = (s32[768]{0:T(1024)S(1)}, s32[768]{0:T(1024)}, u32[]{:S(2)}) copy-start(s32[768]{0:T(1024)} %param.10) | copy-start | bytes 9220
  8.1 9.2 %copy-start.4 = (s32[3072]{0:T(1024)S(1)}, s32[3072]{0:T(1024)}, u32[]{:S(2)}) copy-start(s32[3072]{0:T(1024)} %param.11) | copy-start | bytes 36868
  9.2 6.4 %collective-permute-start.3 = (bf16[128,464]{1,0:T(8,128)(2,1)S(1)}, bf16[128,464]{1,0:T(8,128)(2,1)S(1)}, u32[]{:S(2)}, u32[]{:S(2)}) collective-permute-start(bf16[128,464]{1,0:T(8,128)(2,1)S(1)} %pad_maximum_fusion), channel_id=1, source_target_pairs={{0,16},{16,0},{1,17},{17,1},{2,18},{18,2},{3,19},{19,3},{4,20},{20... | collective-permute-start | bytes 356360 | tf_op jit(solution)/shard_map/ppermute | solution.py:290
  15.7 2.9 %copy-start.2 = (bf16[768,80]{0,1:T(8,128)(2,1)S(1)}, bf16[768,80]{0,1:T(8,128)(2,1)}, u32[]{:S(2)}) copy-start(bf16[768,80]{0,1:T(8,128)(2,1)} %param.9) | copy-start | bytes 368644
  20.9 24.8 %copy-start.3 = (bf16[40,256]{1,0:T(8,128)(2,1)S(1)}, bf16[40,256]{1,0:T(8,128)(2,1)}, u32[]{:S(2)}) copy-start(bf16[40,256]{1,0:T(8,128)(2,1)} %w_in.1) | copy-start | bytes 61444
  20.9 7.1 %collective-permute-start = (bf16[16,64,128]{2,1,0:T(8,128)(2,1)S(1)}, bf16[16,64,128]{2,1,0:T(8,128)(2,1)S(1)}, u32[]{:S(2)}, u32[]{:S(2)}) collective-permute-start(bf16[16,64,128]{2,1,0:T(8,128)(2,1)S(1)} %shard_map.105), channel_id=1, source_target_pairs={{0,16},{16,0},{1,17},{17,1},{2,18},{18,2},{3,19},{19,3},{4,20},{20... | collective-permute-start | bytes 786440 | tf_op jit(solution)/shard_map/ppermute | solution.py:290
  28.8 74.4 %copy-start.6 = (f32[1280]{0:T(1024)S(1)}, f32[1280]{0:T(1024)}, u32[]{:S(2)}) copy-start(f32[1280]{0:T(1024)} %param.12) | copy-start | bytes 15364
  28.8 35.3 %all-to-all-start = ((bf16[16,64,128]{2,1,0:T(8,128)(2,1)}), bf16[16,64,128]{2,1,0:T(8,128)(2,1)S(1)}, u32[]{:S(2)}, u32[]{:S(2)}) async-start(bf16[16,64,128]{2,1,0:T(8,128)(2,1)} %add_convert_fusion.1), calls=%async_computation | async-start | bytes 524288 | tf_op jit(solution)/shard_map/all_to_all | solution.py:367
  64.1 26.7 %all-to-all-start.2 = ((bf16[16,40,128]{2,1,0:T(8,128)(2,1)}), bf16[16,40,128]{2,1,0:T(8,128)(2,1)S(1)}, u32[]{:S(2)}, u32[]{:S(2)}) async-start(bf16[16,40,128]{2,1,0:T(8,128)(2,1)} %shard_map.107), calls=%async_computation.2 | async-start | bytes 327680 | tf_op jit(solution)/shard_map/all_to_all | solution.py:335
  90.8 22.2 %all-to-all-start.1 = ((bf16[32,64,128]{2,1,0:T(8,128)(2,1)}), bf16[32,64,128]{2,1,0:T(8,128)(2,1)S(1)}, u32[]{:S(2)}, u32[]{:S(2)}) async-start(bf16[32,64,128]{2,1,0:T(8,128)(2,1)} %shard_map.106), calls=%async_computation.1 | async-start | bytes 1048576 | tf_op jit(solution)/shard_map/all_to_all | solution.py:371
  101.3 10.0 %collective-permute-start.1 = (bf16[640,128]{1,0:T(8,128)(2,1)S(1)}, bf16[640,128]{1,0:T(8,128)(2,1)S(1)}, u32[]{:S(2)}, u32[]{:S(2)}) collective-permute-start(bf16[640,128]{1,0:T(8,128)(2,1)S(1)} %bitcast.39), channel_id=1, source_target_pairs={{0,32},{32,0},{1,33},{33,1},{2,34},{34,2},{3,35},{35,3},{4,36},{36... | collective-permute-start | bytes 491528 | tf_op jit(solution)/shard_map/ppermute | solution.py:290
  103.3 35.2 %copy-start.5 = (f32[4096]{0:T(1024)S(1)}, f32[4096]{0:T(1024)}, u32[]{:S(2)}) copy-start(f32[4096]{0:T(1024)} %param.14) | copy-start | bytes 49156
  134.1 6.3 %collective-permute-start.2 = (bf16[16,192,128]{2,1,0:T(8,128)(2,1)S(1)}, bf16[16,192,128]{2,1,0:T(8,128)(2,1)S(1)}, u32[]{:S(2)}, u32[]{:S(2)}) collective-permute-start(bf16[16,192,128]{2,1,0:T(8,128)(2,1)S(1)} %all_to_all.40.own.embed), channel_id=1, source_target_pairs={{0,1},{1,0},{2,3},{3,2},{4,5},{5,4},{6,7},{7,6},{8,9},{9,8},{10,11... | collective-permute-start | bytes 2359304 | tf_op jit(solution)/shard_map/ppermute | solution.py:290
  163.4 30.7 %collective-permute-start.4 = (bf16[768,256]{1,0:T(8,128)(2,1)S(1)}, bf16[768,256]{1,0:T(8,128)(2,1)S(1)}, u32[]{:S(2)}, u32[]{:S(2)}) collective-permute-start(bf16[768,256]{1,0:T(8,128)(2,1)S(1)} %bitcast.33), channel_id=1, source_target_pairs={{0,32},{32,64},{64,96},{96,128},{128,160},{160,192},{192,224},{224... | collective-permute-start | bytes 1179656 | tf_op jit(solution)/shard_map/ppermute | solution.py:290
  175.1 19.1 %collective-permute-start.5 = (bf16[768,256]{1,0:T(8,128)(2,1)S(1)}, bf16[768,256]{1,0:T(8,128)(2,1)}, u32[]{:S(2)}, u32[]{:S(2)}) collective-permute-start(bf16[768,256]{1,0:T(8,128)(2,1)S(1)} %bitcast.34), channel_id=1, source_target_pairs={{0,480},{32,0},{64,32},{96,64},{128,96},{160,128},{192,160},{224,1... | collective-permute-start | bytes 1179656 | tf_op jit(solution)/shard_map/ppermute | solution.py:290
  177.9 11.3 %collective-permute-start.6 = (bf16[384,256]{1,0:T(8,128)(2,1)}, bf16[384,256]{1,0:T(8,128)(2,1)S(1)}, u32[]{:S(2)}, u32[]{:S(2)}) collective-permute-start(bf16[384,256]{1,0:T(8,128)(2,1)} %bitcast.17), channel_id=1, source_target_pairs={{0,64},{32,96},{64,128},{96,160},{128,192},{160,224},{192,256},{22... | collective-permute-start | bytes 589832 | tf_op jit(solution)/shard_map/ppermute | solution.py:290
  182.5 11.7 %collective-permute-start.7 = (bf16[384,256]{1,0:T(8,128)(2,1)}, bf16[384,256]{1,0:T(8,128)(2,1)}, u32[]{:S(2)}, u32[]{:S(2)}) collective-permute-start(bf16[384,256]{1,0:T(8,128)(2,1)} %bitcast.18), channel_id=1, source_target_pairs={{0,448},{32,480},{64,0},{96,32},{128,64},{160,96},{192,128},{224,1... | collective-permute-start | bytes 589832 | tf_op jit(solution)/shard_map/ppermute | solution.py:290
  194.2 2.5 copy-start.1
  197.6 8.0 %collective-permute-start.8 = (bf16[16,96,256]{2,1,0:T(8,128)(2,1)S(1)}, bf16[16,96,256]{2,1,0:T(8,128)(2,1)S(1)}, u32[]{:S(2)}, u32[]{:S(2)}) collective-permute-start(bf16[16,96,256]{2,1,0:T(8,128)(2,1)S(1)} %shard_map.112), channel_id=1, source_target_pairs={{0,1},{1,0},{2,3},{3,2},{4,5},{5,4},{6,7},{7,6},{8,9},{9,8},{10,11... | collective-permute-start | bytes 2359304 | tf_op jit(solution)/shard_map/ppermute | solution.py:290
  206.8 17.4 %all-to-all-start.5 = ((bf16[16,96,256]{2,1,0:T(8,128)(2,1)}), bf16[16,96,256]{2,1,0:T(8,128)(2,1)S(1)}, u32[]{:S(2)}, u32[]{:S(2)}) async-start(bf16[16,96,256]{2,1,0:T(8,128)(2,1)} %add_convert_fusion), calls=%async_computation.5 | async-start | bytes 1572864 | tf_op jit(solution)/shard_map/all_to_all | solution.py:410
  210.4 2.2 copy-start
  259.6 7.1 %collective-permute-start.9 = (bf16[16,64,128]{2,1,0:T(8,128)(2,1)S(1)}, bf16[16,64,128]{2,1,0:T(8,128)(2,1)S(1)}, u32[]{:S(2)}, u32[]{:S(2)}) collective-permute-start(bf16[16,64,128]{2,1,0:T(8,128)(2,1)S(1)} %all_to_all.43.states), channel_id=1, source_target_pairs={{0,32},{32,0},{1,33},{33,1},{2,34},{34,2},{3,35},{35,3},{4,36},{36... | collective-permute-start | bytes 786440 | tf_op jit(solution)/shard_map/ppermute | solution.py:290
Sparse Core Ops, SparseCore 0:
  16.8 94.2 all-gather.1

commit v5 on v3

--- a/solution.py
+++ b/solution.py
@@ -31,7 +31,7 @@
 SMEM = pl.BlockSpec(memory_space=pltpu.SMEM)
 
 
-def local_call(kernel, out, inputs, scratch=(), scalars=0, last=(), flops=10**8, moved=10**6):
+def local_call(kernel, out, inputs, scratch=(), scalars=0, last=(), room=48, flops=10**8, moved=10**6):
     specs = [SMEM] * scalars + [VMEM] * (len(inputs) - scalars - len(last)) + list(last)
     many = isinstance(out, (list, tuple))
     return pl.pallas_call(
@@ -41,7 +41,7 @@
         in_specs=specs,
         out_specs=[VMEM] * len(out) if many else VMEM,
         scratch_shapes=list(scratch),
-        compiler_params=pltpu.CompilerParams(vmem_limit_bytes=48 << 20),
+        compiler_params=pltpu.CompilerParams(vmem_limit_bytes=room << 20),
         cost_estimate=pl.CostEstimate(flops=flops, bytes_accessed=moved, transcendentals=0),
     )(*inputs)
 
@@ -60,8 +60,11 @@
         out[i] = w_in[:, (i % 2) * width : (i % 2 + 1) * width]
 
 
-def take_kernel(weights, out):
-    out[...] = weights[...]
+def take_kernel(weights, out, arrived):
+    count = weights.shape[1]
+    copy = pltpu.make_async_copy(weights.at[:, count - LANES : count], out, arrived)
+    copy.start()
+    copy.wait()
 
 
 def pool_kernel(flip, info, slots, ids, rows, out):
@@ -154,11 +157,15 @@
     own = pl.multiple_of(info[4] * query.shape[0], query.shape[0])
     mine = slots[pl.ds(own, query.shape[0]), :]
     peak = jnp.full((query.shape[0], 1), FLOOR_SCORE, F32)
-    turns = ((0, 0), (3, 0), (1, 0), (2, 0), (2, labels.shape[1] // 2))
+    turns = ((0, 0), (3, 0), (1, 0), (2, 0), (2, 2))
     start = 0
-    for piece, (turn, at) in zip(pieces, turns):
+    for piece, (turn, first) in zip(pieces, turns):
         size = piece.shape[0]
-        here = labels[pl.ds((info[3] + turn) % 4, 1), at : at + size]
+        column = (info[3] + turn) % 4
+        here = [
+            labels[pl.ds(4 * (first + i) + column, 1), :] for i in range(size // labels.shape[1])
+        ]
+        here = jnp.concatenate(here, axis=1)
         part = matmul_t(query, piece[:, 0:HEAD_SIZE]) * (1.0 / math.sqrt(HEAD_SIZE))
         part = jnp.where(here <= mine, part, FLOOR_SCORE)
         scores[:, start : start + size] = part
@@ -388,9 +395,11 @@
         take_kernel,
         jax.ShapeDtypeStruct((weights.shape[0], LANES), BF),
         [weights],
-        last=[pl.BlockSpec((weights.shape[0], LANES), lambda i: (0, wide // LANES))],
-    )
-    labels = slot_patch.reshape(n_z // n_zl, n_zl, rows_z).transpose(1, 0, 2).reshape(n_zl, -1)
+        scratch=[pltpu.SemaphoreType.DMA],
+        last=[pl.BlockSpec(memory_space=pl.ANY)],
+        room=60,
+    )
+    labels = slot_patch.reshape(n_z, rows_z)
     kv = lax.all_to_all(kv, "zh", 0, 0, tiled=True).reshape(-1, kv.shape[2])
     attended = local_call(
         attend_kernel,

time: 289 us -> 290 us (level)
  transfers between devices with their start and end apart: 14 -> 14, of which waited for: 11 -> 11; matrix products, arithmetic and copies ran while one was open for 2% -> 1% of each run, Pallas kernels for 4% -> 5%
where the time goes in v5:
time: 290 us; the launch traced here: 286 us
  waiting for transfers between devices  88.1 us (30%)
  blocking collectives  76.2 us (26%)
  starting transfers between devices  69.8 us (24%)
  Pallas kernels  27.7 us (10%)
  between operations  15.1 us (5%)
  local copies, waits for them, and re-layouts  5.88 us (2%)
  other arithmetic  2.95 us (1%)
    ppermute x9, starting transfers between devices, shift(): return lax.ppermute(x, axis, [(i, (i + by) % n) for i in range(n)])  30.5 us
    pallas_call x14, Pallas kernels, local_call(): pl.pallas_call(kernel, out_shape=out, grid=(1,) if last else (), in_specs...  27.7 us
    all_to_all x1, waiting for transfers between devices, layer(): w_in_here = lax.all_to_all(w_in_parts, SEQ, 0, 0, tiled=True)  26.2 us
    all_to_all x1, blocking collectives, layer(): kv = lax.all_to_all(kv, 'zh', 0, 0, tiled=True).reshape(-1, kv.shape[2])  24.8 us
    all_to_all x1, blocking collectives, layer(): states = lax.all_to_all(states, SKIP, 0, 0, tiled=True)  21.3 us
    ppermute x9, waiting for transfers between devices, shift(): return lax.ppermute(x, axis, [(i, (i + by) % n) for i in range(n)])  21.1 us
    all_to_all x1, waiting for transfers between devices, layer(): pooled = lax.all_to_all(pooled, Z, 0, 0, tiled=True)  17.8 us
    all_to_all x1, blocking collectives, over_plane(): near = lax.all_to_all(copies, PLANE, 0, 0, tiled=True)  17.4 us
  transfers between devices with their start and end apart: 14, of which 11 were waited for; matrix products, arithmetic and copies ran while one was open for 1% of the time, Pallas kernels for 5%

profile of v5, /device:TPU:1, one launch (start us, length us, event | category | flops | bytes accessed | tf_op | source)
XLA Modules:
  0.0 285.8 jit_solution(6049878879675943832)
XLA Ops:
  9.2 4.0 %collective-permute-start.2 = (bf16[128,464]{1,0:T(8,128)(2,1)S(1)}, bf16[128,464]{1,0:T(8,128)(2,1)S(1)}, u32[]{:S(2)}, u32[]{:S(2)}) collective-permute-start(bf16[128,464]{1,0:T(8,128)(2,1)S(1)} %pad_maximum_fusion), channel_id=1, source_target_pairs={{0,16},{16,0},{1,17},{17,1},{2,18},{18,2},{3,19},{19,3},{4,20},{20... | collective-permute-start | bytes 356360 | tf_op jit(solution)/shard_map/ppermute | solution.py:296
  20.9 3.4 %collective-permute-start = (bf16[16,64,128]{2,1,0:T(8,128)(2,1)S(1)}, bf16[16,64,128]{2,1,0:T(8,128)(2,1)S(1)}, u32[]{:S(2)}, u32[]{:S(2)}) collective-permute-start(bf16[16,64,128]{2,1,0:T(8,128)(2,1)S(1)} %shard_map.105), channel_id=1, source_target_pairs={{0,16},{16,0},{1,17},{17,1},{2,18},{18,2},{3,19},{19,3},{4,20},{20... | collective-permute-start | bytes 786440 | tf_op jit(solution)/shard_map/ppermute | solution.py:296
  28.8 16.9 %all-to-all-start = ((bf16[16,64,128]{2,1,0:T(8,128)(2,1)}), bf16[16,64,128]{2,1,0:T(8,128)(2,1)S(1)}, u32[]{:S(2)}, u32[]{:S(2)}) async-start(bf16[16,64,128]{2,1,0:T(8,128)(2,1)} %add_convert_fusion.1), calls=%async_computation | async-start | bytes 524288 | tf_op jit(solution)/shard_map/all_to_all | solution.py:372
  46.4 17.8 %all-to-all-done.arrived = bf16[16,64,128]{2,1,0:T(8,128)(2,1)S(1)} async-done(((bf16[16,64,128]{2,1,0:T(8,128)(2,1)}), bf16[16,64,128]{2,1,0:T(8,128)(2,1)S(1)}, u32[]{:S(2)}, u32[]{:S(2)}) %all-to-all-start) | async-done | bytes 262176 | tf_op jit(solution)/shard_map/all_to_all | solution.py:372
  64.2 9.0 %all-to-all-start.2 = ((bf16[32,40,128]{2,1,0:T(8,128)(2,1)}), bf16[32,40,128]{2,1,0:T(8,128)(2,1)S(1)}, u32[]{:S(2)}, u32[]{:S(2)}) async-start(bf16[32,40,128]{2,1,0:T(8,128)(2,1)} %shard_map.107), calls=%async_computation.2 | async-start | bytes 655360 | tf_op jit(solution)/shard_map/all_to_all | solution.py:341
  74.1 26.2 %all-to-all-done.2 = bf16[32,40,128]{2,1,0:T(8,128)(2,1)S(1)} async-done(((bf16[32,40,128]{2,1,0:T(8,128)(2,1)}), bf16[32,40,128]{2,1,0:T(8,128)(2,1)S(1)}, u32[]{:S(2)}, u32[]{:S(2)}) %all-to-all-start.2) | async-done | bytes 327712 | tf_op jit(solution)/shard_map/all_to_all | solution.py:341
  100.3 9.8 %all-to-all-start.1 = ((bf16[32,64,128]{2,1,0:T(8,128)(2,1)}), bf16[32,64,128]{2,1,0:T(8,128)(2,1)S(1)}, u32[]{:S(2)}, u32[]{:S(2)}) async-start(bf16[32,64,128]{2,1,0:T(8,128)(2,1)} %shard_map.106), calls=%async_computation.1 | async-start | bytes 1048576 | tf_op jit(solution)/shard_map/all_to_all | solution.py:376
  110.2 11.7 %all-to-all-done.1.pooled = bf16[32,64,128]{2,1,0:T(8,128)(2,1)S(1)} async-done(((bf16[32,64,128]{2,1,0:T(8,128)(2,1)}), bf16[32,64,128]{2,1,0:T(8,128)(2,1)S(1)}, u32[]{:S(2)}, u32[]{:S(2)}) %all-to-all-start.1) | async-done | bytes 524320 | tf_op jit(solution)/shard_map/all_to_all | solution.py:376
  121.8 2.7 shard_map.108
  124.6 17.4 %all_to_all.40.own.embed = bf16[16,192,128]{2,1,0:T(8,128)(2,1)S(1)} all-to-all(bf16[16,192,128]{2,1,0:T(8,128)(2,1)S(1)} %shard_map.108), channel_id=1, replica_groups=mesh['zh'=4,'zm'=2,'zp'=2,'yl'=2,'yh'=2,'x'=4,'c'=2] {'yl','yh','x'}, dimensions={0} | all-to-all | bytes 1572864 | tf_op jit(solution)/shard_map/all_to_all | solution.py:300
  142.0 2.8 collective-permute-start.1
  146.8 3.5 %shard_map.109 = (bf16[192,128]{1,0:T(8,128)(2,1)S(1)}, bf16[4,192,256]{2,1,0:T(8,128)(2,1)S(1)}) custom-call(s32[7]{0:T(128)S(1)} %stack.28.info, bf16[16,192,128]{2,1,0:T(8,128)(2,1)S(1)} %all_to_all.40.own.embed, bf16[16,192,128]{2,1,0:T(8,128)(2,1)} %collective-permute-done.1.other, f32[16,256]{1,0:T(8,128)S(1)} %reshape.35.gain, ...), custom_call_target="tpu_custom_call" | custom-call | flops 100000000 | bytes 1000000 | tf_op jit(solution)/shard_map/pallas_call | solution.py:37
  150.3 24.8 %all_to_all.41 = bf16[4,192,256]{2,1,0:T(8,128)(2,1)S(1)} all-to-all(bf16[4,192,256]{2,1,0:T(8,128)(2,1)S(1)} %get-tuple-element.7), channel_id=1, replica_groups=mesh['zh'=4,'zm'=2,'zp'=2,'yl'=2,'yh'=2,'x'=4,'c'=2] {'zh'}, dimensions={0} | all-to-all | bytes 786432 | tf_op jit(solution)/shard_map/all_to_all | solution.py:403
  175.2 4.3 %collective-permute-start.3 = (bf16[768,256]{1,0:T(8,128)(2,1)S(1)}, bf16[768,256]{1,0:T(8,128)(2,1)S(1)}, u32[]{:S(2)}, u32[]{:S(2)}) collective-permute-start(bf16[768,256]{1,0:T(8,128)(2,1)S(1)} %bitcast.32), channel_id=1, source_target_pairs={{0,32},{32,64},{64,96},{96,128},{128,160},{160,192},{192,224},{224... | collective-permute-start | bytes 1179656 | tf_op jit(solution)/shard_map/ppermute | solution.py:296
  182.4 6.2 %collective-permute-start.5 = (bf16[384,256]{1,0:T(8,128)(2,1)}, bf16[384,256]{1,0:T(8,128)(2,1)S(1)}, u32[]{:S(2)}, u32[]{:S(2)}) collective-permute-start(bf16[384,256]{1,0:T(8,128)(2,1)} %bitcast.16), channel_id=1, source_target_pairs={{0,64},{32,96},{64,128},{96,160},{128,192},{160,224},{192,256},{22... | collective-permute-start | bytes 589832 | tf_op jit(solution)/shard_map/ppermute | solution.py:296
  190.6 4.5 %collective-permute-done.5.rest_3_ = bf16[384,256]{1,0:T(8,128)(2,1)S(1)} collective-permute-done((bf16[384,256]{1,0:T(8,128)(2,1)}, bf16[384,256]{1,0:T(8,128)(2,1)S(1)}, u32[]{:S(2)}, u32[]{:S(2)}) %collective-permute-start.5) | collective-permute-done | bytes 196640 | tf_op jit(solution)/shard_map/ppermute | solution.py:296
  195.1 7.7 %collective-permute-done.6.rest_4_ = bf16[384,256]{1,0:T(8,128)(2,1)} collective-permute-done((bf16[384,256]{1,0:T(8,128)(2,1)}, bf16[384,256]{1,0:T(8,128)(2,1)}, u32[]{:S(2)}, u32[]{:S(2)}) %collective-permute-start.6) | collective-permute-done | bytes 196640 | tf_op jit(solution)/shard_map/ppermute | solution.py:296
  202.8 2.5 shard_map.110.attended
  206.2 3.6 %collective-permute-start.7 = (bf16[16,96,256]{2,1,0:T(8,128)(2,1)S(1)}, bf16[16,96,256]{2,1,0:T(8,128)(2,1)S(1)}, u32[]{:S(2)}, u32[]{:S(2)}) collective-permute-start(bf16[16,96,256]{2,1,0:T(8,128)(2,1)S(1)} %shard_map.112), channel_id=1, source_target_pairs={{0,1},{1,0},{2,3},{3,2},{4,5},{5,4},{6,7},{7,6},{8,9},{9,8},{10,11... | collective-permute-start | bytes 2359304 | tf_op jit(solution)/shard_map/ppermute | solution.py:296
  212.9 3.6 %all-to-all-start.5 = ((bf16[16,96,256]{2,1,0:T(8,128)(2,1)}), bf16[16,96,256]{2,1,0:T(8,128)(2,1)S(1)}, u32[]{:S(2)}, u32[]{:S(2)}) async-start(bf16[16,96,256]{2,1,0:T(8,128)(2,1)} %add_convert_fusion), calls=%async_computation.5 | async-start | bytes 1572864 | tf_op jit(solution)/shard_map/all_to_all | solution.py:416
  218.8 11.5 %all-to-all-done.5.arrived = bf16[16,96,256]{2,1,0:T(8,128)(2,1)S(1)} async-done(((bf16[16,96,256]{2,1,0:T(8,128)(2,1)}), bf16[16,96,256]{2,1,0:T(8,128)(2,1)S(1)}, u32[]{:S(2)}, u32[]{:S(2)}) %all-to-all-start.5) | async-done | bytes 786464 | tf_op jit(solution)/shard_map/all_to_all | solution.py:416
  233.1 12.7 %all_to_all.42.arrived = bf16[16,64,128]{2,1,0:T(8,128)(2,1)S(1)} all-to-all(bf16[16,64,128]{2,1,0:T(8,128)(2,1)S(1)} %get-tuple-element.9), channel_id=1, replica_groups=mesh['zh'=4,'zm'=2,'zp'=2,'yl'=2,'yh'=2,'x'=4,'c'=2] {'yh','x','c'}, dimensions={0} | all-to-all | bytes 524288 | tf_op jit(solution)/shard_map/all_to_all | solution.py:428
  245.8 21.3 %all_to_all.43.states = bf16[16,64,128]{2,1,0:T(8,128)(2,1)S(1)} all-to-all(bf16[16,64,128]{2,1,0:T(8,128)(2,1)S(1)} %shard_map.115), channel_id=1, replica_groups=mesh['zh'=4,'zm'=2,'zp'=2,'yl'=2,'yh'=2,'x'=4,'c'=2] {'zh','zm','yl'}, dimensions={0} | all-to-all | bytes 524288 | tf_op jit(solution)/shard_map/all_to_all | solution.py:433
  274.2 4.7 %shard_map.117 = bf16[80,768]{1,0:T(8,128)(2,1)} custom-call(s32[7]{0:T(128)S(1)} %stack.28.info, s32[2,2,768]{2,1,0:T(2,128)S(1)} %reshape.39.labels_main, s32[2,6,256]{2,1,0:T(8,128)S(1)} %reshape.41.labels_rest, s32[1,768]{1,0:T(1,128)S(1)} %broadcast_in_dim.11.ids, bf16[80,768]{1,0:T(8,128)(2,1)S(1)} %bitcast.38, ...), custom_call_target="tpu_custom_call" | custom-call | flops 100000000 | bytes 1000000 | tf_op jit(solution)/shard_map/pallas_call | solution.py:37
  (70 shorter events, 38.2 us)
Async XLA Ops:
  7.2 139.7 %all-gather.2.cloned.1.call-start = ((), (), s32[]{:S(2)}) async-start(), calls=%async_computation.8 | async-start | bytes 4456448 | tf_op jit(solution)/shard_map/all_gather | solution.py:362
  7.2 9.4 %copy-start.7 = (s32[768]{0:T(1024)S(1)}, s32[768]{0:T(1024)}, u32[]{:S(2)}) copy-start(s32[768]{0:T(1024)} %param.10) | copy-start | bytes 9220
  8.1 9.2 %copy-start.4 = (s32[3072]{0:T(1024)S(1)}, s32[3072]{0:T(1024)}, u32[]{:S(2)}) copy-start(s32[3072]{0:T(1024)} %param.11) | copy-start | bytes 36868
  9.2 6.4 %collective-permute-start.2 = (bf16[128,464]{1,0:T(8,128)(2,1)S(1)}, bf16[128,464]{1,0:T(8,128)(2,1)S(1)}, u32[]{:S(2)}, u32[]{:S(2)}) collective-permute-start(bf16[128,464]{1,0:T(8,128)(2,1)S(1)} %pad_maximum_fusion), channel_id=1, source_target_pairs={{0,16},{16,0},{1,17},{17,1},{2,18},{18,2},{3,19},{19,3},{4,20},{20... | collective-permute-start | bytes 356360 | tf_op jit(solution)/shard_map/ppermute | solution.py:296
  15.7 2.9 copy-start.2
  20.9 24.8 %copy-start.3 = (bf16[40,256]{1,0:T(8,128)(2,1)S(1)}, bf16[40,256]{1,0:T(8,128)(2,1)}, u32[]{:S(2)}) copy-start(bf16[40,256]{1,0:T(8,128)(2,1)} %w_in.1) | copy-start | bytes 61444
  20.9 7.1 %collective-permute-start = (bf16[16,64,128]{2,1,0:T(8,128)(2,1)S(1)}, bf16[16,64,128]{2,1,0:T(8,128)(2,1)S(1)}, u32[]{:S(2)}, u32[]{:S(2)}) collective-permute-start(bf16[16,64,128]{2,1,0:T(8,128)(2,1)S(1)} %shard_map.105), channel_id=1, source_target_pairs={{0,16},{16,0},{1,17},{17,1},{2,18},{18,2},{3,19},{19,3},{4,20},{20... | collective-permute-start | bytes 786440 | tf_op jit(solution)/shard_map/ppermute | solution.py:296
  28.8 81.3 %copy-start.6 = (f32[1280]{0:T(1024)S(1)}, f32[1280]{0:T(1024)}, u32[]{:S(2)}) copy-start(f32[1280]{0:T(1024)} %param.12) | copy-start | bytes 15364
  28.8 35.4 %all-to-all-start = ((bf16[16,64,128]{2,1,0:T(8,128)(2,1)}), bf16[16,64,128]{2,1,0:T(8,128)(2,1)S(1)}, u32[]{:S(2)}, u32[]{:S(2)}) async-start(bf16[16,64,128]{2,1,0:T(8,128)(2,1)} %add_convert_fusion.1), calls=%async_computation | async-start | bytes 524288 | tf_op jit(solution)/shard_map/all_to_all | solution.py:372
  64.2 36.1 %all-to-all-start.2 = ((bf16[32,40,128]{2,1,0:T(8,128)(2,1)}), bf16[32,40,128]{2,1,0:T(8,128)(2,1)S(1)}, u32[]{:S(2)}, u32[]{:S(2)}) async-start(bf16[32,40,128]{2,1,0:T(8,128)(2,1)} %shard_map.107), calls=%async_computation.2 | async-start | bytes 655360 | tf_op jit(solution)/shard_map/all_to_all | solution.py:341
  100.3 21.6 %all-to-all-start.1 = ((bf16[32,64,128]{2,1,0:T(8,128)(2,1)}), bf16[32,64,128]{2,1,0:T(8,128)(2,1)S(1)}, u32[]{:S(2)}, u32[]{:S(2)}) async-start(bf16[32,64,128]{2,1,0:T(8,128)(2,1)} %shard_map.106), calls=%async_computation.1 | async-start | bytes 1048576 | tf_op jit(solution)/shard_map/all_to_all | solution.py:376
  121.8 23.0 %copy-start.5 = (f32[4096]{0:T(1024)S(1)}, f32[4096]{0:T(1024)}, u32[]{:S(2)}) copy-start(f32[4096]{0:T(1024)} %param.14) | copy-start | bytes 49156
  142.0 4.9 %collective-permute-start.1 = (bf16[16,192,128]{2,1,0:T(8,128)(2,1)S(1)}, bf16[16,192,128]{2,1,0:T(8,128)(2,1)}, u32[]{:S(2)}, u32[]{:S(2)}) collective-permute-start(bf16[16,192,128]{2,1,0:T(8,128)(2,1)S(1)} %all_to_all.40.own.embed), channel_id=1, source_target_pairs={{0,1},{1,0},{2,3},{3,2},{4,5},{5,4},{6,7},{7,6},{8,9},{9,8},{10,11... | collective-permute-start | bytes 2359304 | tf_op jit(solution)/shard_map/ppermute | solution.py:296
  175.2 27.7 %collective-permute-start.3 = (bf16[768,256]{1,0:T(8,128)(2,1)S(1)}, bf16[768,256]{1,0:T(8,128)(2,1)S(1)}, u32[]{:S(2)}, u32[]{:S(2)}) collective-permute-start(bf16[768,256]{1,0:T(8,128)(2,1)S(1)} %bitcast.32), channel_id=1, source_target_pairs={{0,32},{32,64},{64,96},{96,128},{128,160},{160,192},{192,224},{224... | collective-permute-start | bytes 1179656 | tf_op jit(solution)/shard_map/ppermute | solution.py:296
  179.5 23.4 %collective-permute-start.4 = (bf16[768,256]{1,0:T(8,128)(2,1)S(1)}, bf16[768,256]{1,0:T(8,128)(2,1)}, u32[]{:S(2)}, u32[]{:S(2)}) collective-permute-start(bf16[768,256]{1,0:T(8,128)(2,1)S(1)} %bitcast.33), channel_id=1, source_target_pairs={{0,480},{32,0},{64,32},{96,64},{128,96},{160,128},{192,160},{224,1... | collective-permute-start | bytes 1179656 | tf_op jit(solution)/shard_map/ppermute | solution.py:296
  182.4 12.7 %collective-permute-start.5 = (bf16[384,256]{1,0:T(8,128)(2,1)}, bf16[384,256]{1,0:T(8,128)(2,1)S(1)}, u32[]{:S(2)}, u32[]{:S(2)}) collective-permute-start(bf16[384,256]{1,0:T(8,128)(2,1)} %bitcast.16), channel_id=1, source_target_pairs={{0,64},{32,96},{64,128},{96,160},{128,192},{160,224},{192,256},{22... | collective-permute-start | bytes 589832 | tf_op jit(solution)/shard_map/ppermute | solution.py:296
  188.6 14.2 %collective-permute-start.6 = (bf16[384,256]{1,0:T(8,128)(2,1)}, bf16[384,256]{1,0:T(8,128)(2,1)}, u32[]{:S(2)}, u32[]{:S(2)}) collective-permute-start(bf16[384,256]{1,0:T(8,128)(2,1)} %bitcast.17), channel_id=1, source_target_pairs={{0,448},{32,480},{64,0},{96,32},{128,64},{160,96},{192,128},{224,1... | collective-permute-start | bytes 589832 | tf_op jit(solution)/shard_map/ppermute | solution.py:296
  202.8 2.5 copy-start
  206.2 5.5 %collective-permute-start.7 = (bf16[16,96,256]{2,1,0:T(8,128)(2,1)S(1)}, bf16[16,96,256]{2,1,0:T(8,128)(2,1)S(1)}, u32[]{:S(2)}, u32[]{:S(2)}) collective-permute-start(bf16[16,96,256]{2,1,0:T(8,128)(2,1)S(1)} %shard_map.112), channel_id=1, source_target_pairs={{0,1},{1,0},{2,3},{3,2},{4,5},{5,4},{6,7},{7,6},{8,9},{9,8},{10,11... | collective-permute-start | bytes 2359304 | tf_op jit(solution)/shard_map/ppermute | solution.py:296
  212.9 17.4 %all-to-all-start.5 = ((bf16[16,96,256]{2,1,0:T(8,128)(2,1)}), bf16[16,96,256]{2,1,0:T(8,128)(2,1)S(1)}, u32[]{:S(2)}, u32[]{:S(2)}) async-start(bf16[16,96,256]{2,1,0:T(8,128)(2,1)} %add_convert_fusion), calls=%async_computation.5 | async-start | bytes 1572864 | tf_op jit(solution)/shard_map/all_to_all | solution.py:416
  230.2 1.2 copy-start.1
  267.1 7.1 %collective-permute-start.8 = (bf16[16,64,128]{2,1,0:T(8,128)(2,1)S(1)}, bf16[16,64,128]{2,1,0:T(8,128)(2,1)S(1)}, u32[]{:S(2)}, u32[]{:S(2)}) collective-permute-start(bf16[16,64,128]{2,1,0:T(8,128)(2,1)S(1)} %all_to_all.43.states), channel_id=1, source_target_pairs={{0,32},{32,0},{1,33},{33,1},{2,34},{34,2},{3,35},{35,3},{4,36},{36... | collective-permute-start | bytes 786440 | tf_op jit(solution)/shard_map/ppermute | solution.py:296
Sparse Core Ops, SparseCore 0:
  16.8 99.5 all-gather.1

commit v6 on v3

--- a/solution.py
+++ b/solution.py
@@ -239,8 +239,9 @@
     return pick
 
 
-def near_kernel(info, labels_main, labels_rest, states, out, main, rest):
+def near_kernel(info, spans, labels_main, labels_rest, states, out, main, rest):
     group = info[5]
+    out[...] = jnp.zeros(out.shape, F32)
 
     def put(at, low, tail):
         blank = jnp.zeros((LANES, LANES - MAIN - LONGEST), F32)
@@ -249,39 +250,42 @@
     pick = pick_rows(
         info[6], labels_main.at[group], labels_rest.at[group], states, main, rest, put
     )
-    lax.fori_loop(0, out.shape[0] // LANES, pick, 0, unroll=True)
+    lax.fori_loop(0, (spans[spans.shape[0] - 1] + LANES - 1) >> 7, pick, 0)
 
 
 def cross_kernel(
-    info, labels_main, labels_rest, ids, rows, states, near, out, picked, main, rest
+    info, spans, labels_main, labels_rest, ids, rows, states, near, out, picked, main, rest
 ):
     size = rows.shape[0]
     group = 1 - info[5]
     base = info[6]
+    picked[...] = near[...]
 
     def put(at, low, tail):
         blank = jnp.zeros((LANES, LANES - MAIN - LONGEST), F32)
         here = jnp.concatenate([low, tail, blank], axis=1)
-        picked[pl.ds(at, LANES), :] = near[pl.ds(at, LANES), :] + here
+        picked[pl.ds(at, LANES), :] = picked[pl.ds(at, LANES), :] + here
 
     pick = pick_rows(base, labels_main.at[group], labels_rest.at[group], states, main, rest, put)
-    lax.fori_loop(0, near.shape[0] // LANES, pick, 0, unroll=True)
-    keys = picked[...].astype(BF)[:, 0:size]
-    turned = picked[...].T.astype(BF)
-    wanted = base + lax.broadcasted_iota(jnp.int32, (near.shape[0], LANES), 0)
-    allowed = wanted >= 0
+    lax.fori_loop(0, (spans[spans.shape[0] - 1] + LANES - 1) >> 7, pick, 0)
+    reach = LANES + 2 * WINDOW
 
     for i in range(rows.shape[1] // LANES):
         at = slice(i * LANES, (i + 1) * LANES)
         mine = rows[:, at]
+        start = pl.multiple_of((spans[i] >> 3) << 3, 8)
+        keys = picked[pl.ds(start, reach), :].astype(BF)[:, 0:size]
+        wanted = base + start + lax.broadcasted_iota(jnp.int32, (reach, LANES), 0)
         far = ids[:, at] - wanted
-        close = (far >= 0) & (far < WINDOW) & allowed
+        close = (far >= 0) & (far < WINDOW) & (wanted >= 0)
         scores = matmul(keys, mine) * (1.0 / math.sqrt(size))
         scores = jnp.where(close, scores, FLOOR_SCORE)
         weights = jnp.exp(scores - jnp.max(scores, axis=0, keepdims=True))
         total = jnp.sum(weights, axis=0, keepdims=True)
-        reached = matmul(turned, weights.astype(BF))[0:size] / total
-        out[:, at] = (mine.astype(F32) + reached).astype(BF)
+        reached = lax.dot_general(
+            keys, weights.astype(BF), (((0,), (0,)), ((), ())), preferred_element_type=F32
+        )
+        out[:, at] = (mine.astype(F32) + reached / total).astype(BF)
 
 
 def shift(x, axis, by):
@@ -428,6 +432,7 @@
     labels_main = by_source.reshape(2, n_skip, 2, -1).transpose(0, 2, 1, 3).reshape(2, 2, -1)
     labels_rest = by_source.reshape(2, n_skip, -1, LONGEST).transpose(0, 2, 1, 3)
     labels_rest = labels_rest.reshape(2, rows_each // LONGEST, -1)
+    spans = jnp.concatenate([patch_ids[::LANES], patch_ids[-1:] + WINDOW]) - patch_ids[0]
     capacity = bytes_here + LANES
     room = [
         pltpu.VMEM((n_skip * rows_each // 2, LANES), BF),
@@ -436,16 +441,16 @@
     near = local_call(
         near_kernel,
         jax.ShapeDtypeStruct((capacity, LANES), F32),
-        [info, labels_main, labels_rest, states],
+        [info, spans, labels_main, labels_rest, states],
         scratch=room,
-        scalars=1,
+        scalars=2,
     )
     byte_out = local_call(
         cross_kernel,
         jax.ShapeDtypeStruct((cross_size, bytes_here), BF),
-        [info, labels_main, labels_rest, patch_ids[None, :], rows, others, near],
+        [info, spans, labels_main, labels_rest, patch_ids[None, :], rows, others, near],
         scratch=[pltpu.VMEM((capacity, LANES), F32), *room],
-        scalars=1,
+        scalars=2,
     ).T
     return (stream, byte_out)
 

time: 289 us -> 287 us (level)
  no operation moved by 1% of the time
where the time goes in v6:
time: 287 us; the launch traced here: 283 us
  waiting for transfers between devices  86.5 us (30%)
  blocking collectives  75.3 us (26%)
  starting transfers between devices  70.5 us (25%)
  Pallas kernels  22.8 us (8%)
  between operations  15.6 us (5%)
  local copies, waits for them, and re-layouts  8.37 us (3%)
  other arithmetic  3.64 us (1%)
    ppermute x9, starting transfers between devices, shift(): return lax.ppermute(x, axis, [(i, (i + by) % n) for i in range(n)])  31.3 us
    all_to_all x1, waiting for transfers between devices, layer(): w_in_here = lax.all_to_all(w_in_parts, SEQ, 0, 0, tiled=True)  26 us
    all_to_all x1, blocking collectives, layer(): kv = lax.all_to_all(kv, 'zh', 0, 0, tiled=True).reshape(-1, kv.shape[2])  23.9 us
    pallas_call x14, Pallas kernels, local_call(): pl.pallas_call(kernel, out_shape=out, grid=(1,) if last else (), in_specs...  22.8 us
    all_to_all x1, blocking collectives, layer(): states = lax.all_to_all(states, SKIP, 0, 0, tiled=True)  21.3 us
    ppermute x9, waiting for transfers between devices, shift(): return lax.ppermute(x, axis, [(i, (i + by) % n) for i in range(n)])  19.5 us
    all_to_all x1, waiting for transfers between devices, layer(): pooled = lax.all_to_all(pooled, Z, 0, 0, tiled=True)  18 us
    all_to_all x1, blocking collectives, over_plane(): near = lax.all_to_all(copies, PLANE, 0, 0, tiled=True)  17.3 us
  transfers between devices with their start and end apart: 14, of which 11 were waited for; matrix products, arithmetic and copies ran while one was open for 2% of the time, Pallas kernels for 4%

profile of v6, /device:TPU:1, one launch (start us, length us, event | category | flops | bytes accessed | tf_op | source)
XLA Modules:
  0.0 282.6 jit_solution(8892359448056624918)
XLA Ops:
  9.2 4.0 %collective-permute-start.2 = (bf16[128,464]{1,0:T(8,128)(2,1)S(1)}, bf16[128,464]{1,0:T(8,128)(2,1)S(1)}, u32[]{:S(2)}, u32[]{:S(2)}) collective-permute-start(bf16[128,464]{1,0:T(8,128)(2,1)S(1)} %pad_maximum_fusion), channel_id=1, source_target_pairs={{0,16},{16,0},{1,17},{17,1},{2,18},{18,2},{3,19},{19,3},{4,20},{20... | collective-permute-start | bytes 356360 | tf_op jit(solution)/shard_map/ppermute | solution.py:293
  20.8 3.4 %collective-permute-start = (bf16[16,64,128]{2,1,0:T(8,128)(2,1)S(1)}, bf16[16,64,128]{2,1,0:T(8,128)(2,1)S(1)}, u32[]{:S(2)}, u32[]{:S(2)}) collective-permute-start(bf16[16,64,128]{2,1,0:T(8,128)(2,1)S(1)} %shard_map.105), channel_id=1, source_target_pairs={{0,16},{16,0},{1,17},{17,1},{2,18},{18,2},{3,19},{19,3},{4,20},{20... | collective-permute-start | bytes 786440 | tf_op jit(solution)/shard_map/ppermute | solution.py:293
  28.7 16.9 %all-to-all-start = ((bf16[16,64,128]{2,1,0:T(8,128)(2,1)}), bf16[16,64,128]{2,1,0:T(8,128)(2,1)S(1)}, u32[]{:S(2)}, u32[]{:S(2)}) async-start(bf16[16,64,128]{2,1,0:T(8,128)(2,1)} %add_convert_fusion.1), calls=%async_computation | async-start | bytes 524288 | tf_op jit(solution)/shard_map/all_to_all | solution.py:369
  46.4 18.0 %all-to-all-done.arrived = bf16[16,64,128]{2,1,0:T(8,128)(2,1)S(1)} async-done(((bf16[16,64,128]{2,1,0:T(8,128)(2,1)}), bf16[16,64,128]{2,1,0:T(8,128)(2,1)S(1)}, u32[]{:S(2)}, u32[]{:S(2)}) %all-to-all-start) | async-done | bytes 262176 | tf_op jit(solution)/shard_map/all_to_all | solution.py:369
  64.4 8.9 %all-to-all-start.2 = ((bf16[32,40,128]{2,1,0:T(8,128)(2,1)}), bf16[32,40,128]{2,1,0:T(8,128)(2,1)S(1)}, u32[]{:S(2)}, u32[]{:S(2)}) async-start(bf16[32,40,128]{2,1,0:T(8,128)(2,1)} %shard_map.107), calls=%async_computation.2 | async-start | bytes 655360 | tf_op jit(solution)/shard_map/all_to_all | solution.py:338
  74.2 26.0 %all-to-all-done.2 = bf16[32,40,128]{2,1,0:T(8,128)(2,1)S(1)} async-done(((bf16[32,40,128]{2,1,0:T(8,128)(2,1)}), bf16[32,40,128]{2,1,0:T(8,128)(2,1)S(1)}, u32[]{:S(2)}, u32[]{:S(2)}) %all-to-all-start.2) | async-done | bytes 327712 | tf_op jit(solution)/shard_map/all_to_all | solution.py:338
  100.1 9.8 %all-to-all-start.1 = ((bf16[32,64,128]{2,1,0:T(8,128)(2,1)}), bf16[32,64,128]{2,1,0:T(8,128)(2,1)S(1)}, u32[]{:S(2)}, u32[]{:S(2)}) async-start(bf16[32,64,128]{2,1,0:T(8,128)(2,1)} %shard_map.106), calls=%async_computation.1 | async-start | bytes 1048576 | tf_op jit(solution)/shard_map/all_to_all | solution.py:373
  110.0 11.7 %all-to-all-done.1.pooled = bf16[32,64,128]{2,1,0:T(8,128)(2,1)S(1)} async-done(((bf16[32,64,128]{2,1,0:T(8,128)(2,1)}), bf16[32,64,128]{2,1,0:T(8,128)(2,1)S(1)}, u32[]{:S(2)}, u32[]{:S(2)}) %all-to-all-start.1) | async-done | bytes 524320 | tf_op jit(solution)/shard_map/all_to_all | solution.py:373
  121.7 2.8 shard_map.108
  124.4 17.3 %all_to_all.40.own.embed = bf16[16,192,128]{2,1,0:T(8,128)(2,1)S(1)} all-to-all(bf16[16,192,128]{2,1,0:T(8,128)(2,1)S(1)} %shard_map.108), channel_id=1, replica_groups=mesh['zh'=4,'zm'=2,'zp'=2,'yl'=2,'yh'=2,'x'=4,'c'=2] {'yl','yh','x'}, dimensions={0} | all-to-all | bytes 1572864 | tf_op jit(solution)/shard_map/all_to_all | solution.py:297
  141.8 2.8 %collective-permute-start.1 = (bf16[16,192,128]{2,1,0:T(8,128)(2,1)S(1)}, bf16[16,192,128]{2,1,0:T(8,128)(2,1)S(1)}, u32[]{:S(2)}, u32[]{:S(2)}) collective-permute-start(bf16[16,192,128]{2,1,0:T(8,128)(2,1)S(1)} %all_to_all.40.own.embed), channel_id=1, source_target_pairs={{0,1},{1,0},{2,3},{3,2},{4,5},{5,4},{6,7},{7,6},{8,9},{9,8},{10,11... | collective-permute-start | bytes 2359304 | tf_op jit(solution)/shard_map/ppermute | solution.py:293
  146.5 3.3 %shard_map.109 = (bf16[192,128]{1,0:T(8,128)(2,1)S(1)}, bf16[4,192,256]{2,1,0:T(8,128)(2,1)S(1)}) custom-call(s32[7]{0:T(128)S(1)} %stack.31.info, bf16[16,192,128]{2,1,0:T(8,128)(2,1)S(1)} %all_to_all.40.own.embed, bf16[16,192,128]{2,1,0:T(8,128)(2,1)S(1)} %collective-permute-done.1.other, f32[16,256]{1,0:T(8,128)S(1)} %reshape.35.gain, ...), custom_call_target="tpu_custom_call" | custom-call | flops 100000000 | bytes 1000000 | tf_op jit(solution)/shard_map/pallas_call | solution.py:37
  149.8 23.9 %all_to_all.41 = bf16[4,192,256]{2,1,0:T(8,128)(2,1)S(1)} all-to-all(bf16[4,192,256]{2,1,0:T(8,128)(2,1)S(1)} %get-tuple-element.7), channel_id=1, replica_groups=mesh['zh'=4,'zm'=2,'zp'=2,'yl'=2,'yh'=2,'x'=4,'c'=2] {'zh'}, dimensions={0} | all-to-all | bytes 786432 | tf_op jit(solution)/shard_map/all_to_all | solution.py:398
  173.8 5.8 %collective-permute-start.3 = (bf16[768,256]{1,0:T(8,128)(2,1)S(1)}, bf16[768,256]{1,0:T(8,128)(2,1)S(1)}, u32[]{:S(2)}, u32[]{:S(2)}) collective-permute-start(bf16[768,256]{1,0:T(8,128)(2,1)S(1)} %bitcast.35), channel_id=1, source_target_pairs={{0,32},{32,64},{64,96},{96,128},{128,160},{160,192},{192,224},{224... | collective-permute-start | bytes 1179656 | tf_op jit(solution)/shard_map/ppermute | solution.py:293
  182.3 5.9 %collective-permute-start.5 = (bf16[384,256]{1,0:T(8,128)(2,1)}, bf16[384,256]{1,0:T(8,128)(2,1)S(1)}, u32[]{:S(2)}, u32[]{:S(2)}) collective-permute-start(bf16[384,256]{1,0:T(8,128)(2,1)} %bitcast.19), channel_id=1, source_target_pairs={{0,64},{32,96},{64,128},{96,160},{128,192},{160,224},{192,256},{22... | collective-permute-start | bytes 589832 | tf_op jit(solution)/shard_map/ppermute | solution.py:293
  191.7 2.8 collective-permute-done.5.rest_3_
  194.5 8.0 %collective-permute-done.6.rest_4_ = bf16[384,256]{1,0:T(8,128)(2,1)} collective-permute-done((bf16[384,256]{1,0:T(8,128)(2,1)}, bf16[384,256]{1,0:T(8,128)(2,1)}, u32[]{:S(2)}, u32[]{:S(2)}) %collective-permute-start.6) | collective-permute-done | bytes 196640 | tf_op jit(solution)/shard_map/ppermute | solution.py:293
  202.4 2.5 shard_map.110.attended
  205.8 3.6 %collective-permute-start.7 = (bf16[16,96,256]{2,1,0:T(8,128)(2,1)S(1)}, bf16[16,96,256]{2,1,0:T(8,128)(2,1)S(1)}, u32[]{:S(2)}, u32[]{:S(2)}) collective-permute-start(bf16[16,96,256]{2,1,0:T(8,128)(2,1)S(1)} %shard_map.112), channel_id=1, source_target_pairs={{0,1},{1,0},{2,3},{3,2},{4,5},{5,4},{6,7},{7,6},{8,9},{9,8},{10,11... | collective-permute-start | bytes 2359304 | tf_op jit(solution)/shard_map/ppermute | solution.py:293
  212.5 3.6 %all-to-all-start.5 = ((bf16[16,96,256]{2,1,0:T(8,128)(2,1)}), bf16[16,96,256]{2,1,0:T(8,128)(2,1)S(1)}, u32[]{:S(2)}, u32[]{:S(2)}) async-start(bf16[16,96,256]{2,1,0:T(8,128)(2,1)} %add_convert_fusion), calls=%async_computation.5 | async-start | bytes 1572864 | tf_op jit(solution)/shard_map/all_to_all | solution.py:411
  218.6 11.3 %all-to-all-done.5.arrived = bf16[16,96,256]{2,1,0:T(8,128)(2,1)S(1)} async-done(((bf16[16,96,256]{2,1,0:T(8,128)(2,1)}), bf16[16,96,256]{2,1,0:T(8,128)(2,1)S(1)}, u32[]{:S(2)}, u32[]{:S(2)}) %all-to-all-start.5) | async-done | bytes 786464 | tf_op jit(solution)/shard_map/all_to_all | solution.py:411
  231.5 12.7 %all_to_all.42.arrived = bf16[16,64,128]{2,1,0:T(8,128)(2,1)S(1)} all-to-all(bf16[16,64,128]{2,1,0:T(8,128)(2,1)S(1)} %get-tuple-element.9), channel_id=1, replica_groups=mesh['zh'=4,'zm'=2,'zp'=2,'yl'=2,'yh'=2,'x'=4,'c'=2] {'yh','x','c'}, dimensions={0} | all-to-all | bytes 524288 | tf_op jit(solution)/shard_map/all_to_all | solution.py:423
  244.2 21.3 %all_to_all.43.states = bf16[16,64,128]{2,1,0:T(8,128)(2,1)S(1)} all-to-all(bf16[16,64,128]{2,1,0:T(8,128)(2,1)S(1)} %shard_map.115), channel_id=1, replica_groups=mesh['zh'=4,'zm'=2,'zp'=2,'yl'=2,'yh'=2,'x'=4,'c'=2] {'zh','zm','yl'}, dimensions={0} | all-to-all | bytes 524288 | tf_op jit(solution)/shard_map/all_to_all | solution.py:428
  272.7 3.1 %shard_map.117 = bf16[80,768]{1,0:T(8,128)(2,1)} custom-call(s32[7]{0:T(128)S(1)} %stack.31.info, s32[7]{0:T(128)S(1)} %add_subtract_fusion.spans, s32[2,2,768]{2,1,0:T(2,128)S(1)} %reshape.40.labels_main, s32[2,6,256]{2,1,0:T(8,128)S(1)} %reshape.42.labels_rest, s32[1,768]{1,0:T(1,128)S(1)} %broadcast_in_dim.11.ids, bf16[80,768]{1,0:T(8,128)(2,1)S(1)} %bitcast.41, ...), custom_call_target="tpu_custom_call" | custom-call | flops 100000000 | bytes 1000000 | tf_op jit(solution)/shard_map/pallas_call | solution.py:37
  (74 shorter events, 37.7 us)
Async XLA Ops:
  7.2 139.4 %all-gather.2.cloned.1.call-start = ((), (), s32[]{:S(2)}) async-start(), calls=%async_computation.8 | async-start | bytes 4456448 | tf_op jit(solution)/shard_map/all_gather | solution.py:359
  8.1 8.6 %copy-start.4 = (s32[3072]{0:T(1024)S(1)}, s32[3072]{0:T(1024)}, u32[]{:S(2)}) copy-start(s32[3072]{0:T(1024)} %param.11) | copy-start | bytes 36868
  9.2 6.4 %collective-permute-start.2 = (bf16[128,464]{1,0:T(8,128)(2,1)S(1)}, bf16[128,464]{1,0:T(8,128)(2,1)S(1)}, u32[]{:S(2)}, u32[]{:S(2)}) collective-permute-start(bf16[128,464]{1,0:T(8,128)(2,1)S(1)} %pad_maximum_fusion), channel_id=1, source_target_pairs={{0,16},{16,0},{1,17},{17,1},{2,18},{18,2},{3,19},{19,3},{4,20},{20... | collective-permute-start | bytes 356360 | tf_op jit(solution)/shard_map/ppermute | solution.py:293
  15.7 1.5 copy-start.7
  15.7 2.8 copy-start.2
  20.8 24.8 %copy-start.3 = (bf16[40,256]{1,0:T(8,128)(2,1)S(1)}, bf16[40,256]{1,0:T(8,128)(2,1)}, u32[]{:S(2)}) copy-start(bf16[40,256]{1,0:T(8,128)(2,1)} %w_in.1) | copy-start | bytes 61444
  20.8 7.1 %collective-permute-start = (bf16[16,64,128]{2,1,0:T(8,128)(2,1)S(1)}, bf16[16,64,128]{2,1,0:T(8,128)(2,1)S(1)}, u32[]{:S(2)}, u32[]{:S(2)}) collective-permute-start(bf16[16,64,128]{2,1,0:T(8,128)(2,1)S(1)} %shard_map.105), channel_id=1, source_target_pairs={{0,16},{16,0},{1,17},{17,1},{2,18},{18,2},{3,19},{19,3},{4,20},{20... | collective-permute-start | bytes 786440 | tf_op jit(solution)/shard_map/ppermute | solution.py:293
  28.7 81.2 %copy-start.6 = (f32[1280]{0:T(1024)S(1)}, f32[1280]{0:T(1024)}, u32[]{:S(2)}) copy-start(f32[1280]{0:T(1024)} %param.12) | copy-start | bytes 15364
  28.7 35.7 %all-to-all-start = ((bf16[16,64,128]{2,1,0:T(8,128)(2,1)}), bf16[16,64,128]{2,1,0:T(8,128)(2,1)S(1)}, u32[]{:S(2)}, u32[]{:S(2)}) async-start(bf16[16,64,128]{2,1,0:T(8,128)(2,1)} %add_convert_fusion.1), calls=%async_computation | async-start | bytes 524288 | tf_op jit(solution)/shard_map/all_to_all | solution.py:369
  64.4 35.7 %all-to-all-start.2 = ((bf16[32,40,128]{2,1,0:T(8,128)(2,1)}), bf16[32,40,128]{2,1,0:T(8,128)(2,1)S(1)}, u32[]{:S(2)}, u32[]{:S(2)}) async-start(bf16[32,40,128]{2,1,0:T(8,128)(2,1)} %shard_map.107), calls=%async_computation.2 | async-start | bytes 655360 | tf_op jit(solution)/shard_map/all_to_all | solution.py:338
  100.1 21.5 %all-to-all-start.1 = ((bf16[32,64,128]{2,1,0:T(8,128)(2,1)}), bf16[32,64,128]{2,1,0:T(8,128)(2,1)S(1)}, u32[]{:S(2)}, u32[]{:S(2)}) async-start(bf16[32,64,128]{2,1,0:T(8,128)(2,1)} %shard_map.106), calls=%async_computation.1 | async-start | bytes 1048576 | tf_op jit(solution)/shard_map/all_to_all | solution.py:373
  121.7 23.0 %copy-start.5 = (f32[4096]{0:T(1024)S(1)}, f32[4096]{0:T(1024)}, u32[]{:S(2)}) copy-start(f32[4096]{0:T(1024)} %param.14) | copy-start | bytes 49156
  141.8 4.7 %collective-permute-start.1 = (bf16[16,192,128]{2,1,0:T(8,128)(2,1)S(1)}, bf16[16,192,128]{2,1,0:T(8,128)(2,1)S(1)}, u32[]{:S(2)}, u32[]{:S(2)}) collective-permute-start(bf16[16,192,128]{2,1,0:T(8,128)(2,1)S(1)} %all_to_all.40.own.embed), channel_id=1, source_target_pairs={{0,1},{1,0},{2,3},{3,2},{4,5},{5,4},{6,7},{7,6},{8,9},{9,8},{10,11... | collective-permute-start | bytes 2359304 | tf_op jit(solution)/shard_map/ppermute | solution.py:293
  173.8 28.7 %collective-permute-start.3 = (bf16[768,256]{1,0:T(8,128)(2,1)S(1)}, bf16[768,256]{1,0:T(8,128)(2,1)S(1)}, u32[]{:S(2)}, u32[]{:S(2)}) collective-permute-start(bf16[768,256]{1,0:T(8,128)(2,1)S(1)} %bitcast.35), channel_id=1, source_target_pairs={{0,32},{32,64},{64,96},{96,128},{128,160},{160,192},{192,224},{224... | collective-permute-start | bytes 1179656 | tf_op jit(solution)/shard_map/ppermute | solution.py:293
  179.6 22.9 %collective-permute-start.4 = (bf16[768,256]{1,0:T(8,128)(2,1)S(1)}, bf16[768,256]{1,0:T(8,128)(2,1)}, u32[]{:S(2)}, u32[]{:S(2)}) collective-permute-start(bf16[768,256]{1,0:T(8,128)(2,1)S(1)} %bitcast.36), channel_id=1, source_target_pairs={{0,480},{32,0},{64,32},{96,64},{128,96},{160,128},{192,160},{224,1... | collective-permute-start | bytes 1179656 | tf_op jit(solution)/shard_map/ppermute | solution.py:293
  182.3 12.2 %collective-permute-start.5 = (bf16[384,256]{1,0:T(8,128)(2,1)}, bf16[384,256]{1,0:T(8,128)(2,1)S(1)}, u32[]{:S(2)}, u32[]{:S(2)}) collective-permute-start(bf16[384,256]{1,0:T(8,128)(2,1)} %bitcast.19), channel_id=1, source_target_pairs={{0,64},{32,96},{64,128},{96,160},{128,192},{160,224},{192,256},{22... | collective-permute-start | bytes 589832 | tf_op jit(solution)/shard_map/ppermute | solution.py:293
  188.2 14.2 %collective-permute-start.6 = (bf16[384,256]{1,0:T(8,128)(2,1)}, bf16[384,256]{1,0:T(8,128)(2,1)}, u32[]{:S(2)}, u32[]{:S(2)}) collective-permute-start(bf16[384,256]{1,0:T(8,128)(2,1)} %bitcast.20), channel_id=1, source_target_pairs={{0,448},{32,480},{64,0},{96,32},{128,64},{160,96},{192,128},{224,1... | collective-permute-start | bytes 589832 | tf_op jit(solution)/shard_map/ppermute | solution.py:293
  202.4 2.5 copy-start.1
  205.8 5.5 %collective-permute-start.7 = (bf16[16,96,256]{2,1,0:T(8,128)(2,1)S(1)}, bf16[16,96,256]{2,1,0:T(8,128)(2,1)S(1)}, u32[]{:S(2)}, u32[]{:S(2)}) collective-permute-start(bf16[16,96,256]{2,1,0:T(8,128)(2,1)S(1)} %shard_map.112), channel_id=1, source_target_pairs={{0,1},{1,0},{2,3},{3,2},{4,5},{5,4},{6,7},{7,6},{8,9},{9,8},{10,11... | collective-permute-start | bytes 2359304 | tf_op jit(solution)/shard_map/ppermute | solution.py:293
  212.5 17.4 %all-to-all-start.5 = ((bf16[16,96,256]{2,1,0:T(8,128)(2,1)}), bf16[16,96,256]{2,1,0:T(8,128)(2,1)S(1)}, u32[]{:S(2)}, u32[]{:S(2)}) async-start(bf16[16,96,256]{2,1,0:T(8,128)(2,1)} %add_convert_fusion), calls=%async_computation.5 | async-start | bytes 1572864 | tf_op jit(solution)/shard_map/all_to_all | solution.py:411
  216.1 2.2 copy-start
  265.6 7.1 %collective-permute-start.8 = (bf16[16,64,128]{2,1,0:T(8,128)(2,1)S(1)}, bf16[16,64,128]{2,1,0:T(8,128)(2,1)S(1)}, u32[]{:S(2)}, u32[]{:S(2)}) collective-permute-start(bf16[16,64,128]{2,1,0:T(8,128)(2,1)S(1)} %all_to_all.43.states), channel_id=1, source_target_pairs={{0,32},{32,0},{1,33},{33,1},{2,34},{34,2},{3,35},{35,3},{4,36},{36... | collective-permute-start | bytes 786440 | tf_op jit(solution)/shard_map/ppermute | solution.py:293
Sparse Core Ops, SparseCore 0:
  16.8 99.0 all-gather.1
